TPU v7x, 32 devices: a whole 2x2x4 slice. The times are simulated.
32 devices in a mesh: batch: 8 (over y, x, core), pos: 4 (over z).
Axes of the slice: x: 2, y: 2, z: 4, core: 2. Of those that a mesh axis runs over, the one named last changes fastest.
Arguments:
- tokens: bfloat16 [64, 512, 512], P('batch', 'pos'), may hold values from -6 to 6
- cotangent: bfloat16 [64, 512, 512], P('batch', 'pos'), may hold values from -6 to 6
- segment_ids: int32 [64, 512], P('batch'), may hold values from 0 to 5, never falling along the last dimension, each value on 1 to 256 neighbouring positions
- pad_mask: int32 [64, 512], P('batch'), may hold values 0 or 1
- skip_flags: int32 [64], P('batch'), may hold values from 0 to 1, as said below
- in_master: float32 [1572864], P(('batch', 'pos')), may hold values from -0.25 to 0.25
- spatial_master: float32 [262144], P(('batch', 'pos')), may hold values from -0.5 to 0.5
- out_master: float32 [786432], P(('batch', 'pos')), may hold values from -0.15625 to 0.15625
- vector_master: float32 [8192], P(('batch', 'pos')), may hold values from -0.5 to 1.5, as said below
- in_first: float32 [1572864], P(('batch', 'pos')), may hold values from -48 to 48
- spatial_first: float32 [262144], P(('batch', 'pos')), may hold values from -40 to 40
- out_first: float32 [786432], P(('batch', 'pos')), may hold values from -128 to 128
- vector_first: float32 [8192], P(('batch', 'pos')), may hold values from -40.22652 to 40.22652
- in_second: float32 [1572864], P(('batch', 'pos')), may hold values from 5.24288 to 20.97152
- spatial_second: float32 [262144], P(('batch', 'pos')), may hold values from 3.93216 to 15.72864
- out_second: float32 [786432], P(('batch', 'pos')), may hold values from 32.768 to 131.072
- vector_second: float32 [8192], P(('batch', 'pos')), may hold values from 3.5684352 to 131.072, as said below
Outputs:
- mixed: bfloat16 [64, 512, 512], P('batch', 'pos')
- input_grad: float32 [64, 512, 512], P('batch', 'pos')
- in_master_new: float32 [1572864], P(('batch', 'pos'))
- in_first_new: float32 [1572864], P(('batch', 'pos'))
- in_second_new: float32 [1572864], P(('batch', 'pos'))
- spatial_master_new: float32 [262144], P(('batch', 'pos'))
- spatial_first_new: float32 [262144], P(('batch', 'pos'))
- spatial_second_new: float32 [262144], P(('batch', 'pos'))
- out_master_new: float32 [786432], P(('batch', 'pos'))
- out_first_new: float32 [786432], P(('batch', 'pos'))
- out_second_new: float32 [786432], P(('batch', 'pos'))
- vector_master_new: float32 [8192], P(('batch', 'pos'))
- vector_first_new: float32 [8192], P(('batch', 'pos'))
- vector_second_new: float32 [8192], P(('batch', 'pos'))
Inputs may be any that keep to these rules, and one draw needn't show every extreme that they name: `vector_master`: gains lie in 0.6 to 1.4, the spatial bias in 0.5 to 1.5, the other biases in -0.5 to 0.5. `vector_second`: all entries are positive. `skip_flags`: values are 0 or 1; at least one row skips.
All inputs are finite; a program needn't handle non-finite values. No bound on the sum of `pad_mask` on one device may be relied on, other than what follows from the above.
Results may differ from a plain program's by a relative error of at most 0.011.
Values may be sent and summed in bfloat16 or wider, within the bound.
No kernel may reach another device: no remote copies, remote signals or barrier semaphores. Data moves between devices by JAX's collectives and lax.ppermute only.
A program may use at most 192 MiB of HBM per device.

v0:
```python
import jax
import jax.numpy as jnp
from jax import lax
from jax.sharding import PartitionSpec as P

D = 512
HID = 3072
SEQ = 512
GATE = 1536


norm_eps = 1e-05
beta_one = 0.9
beta_two = 0.999
adam_eps = 1e-08
step_count = 10.0
decay_matrix = 0.1
rate_in = 0.12
rate_spatial = 0.2
rate_out = 0.07
rate_vector = 1.0


def split_vector(vector):
    lengths = [D, D, HID, GATE, GATE, SEQ, D]
    pieces = []
    cursor = 0
    for length in lengths:
        pieces.append(vector[cursor : cursor + length])
        cursor = cursor + length
    return pieces


def norm_parts(values):
    average = jnp.mean(values, -1, keepdims=True)
    centred = values - average
    spread = jnp.mean(centred * centred, -1, keepdims=True)
    inverse = lax.rsqrt(spread + norm_eps)
    return (centred * inverse, inverse)


def norm_back(grad_hat, normed, inverse):
    first_mean = jnp.mean(grad_hat, -1, keepdims=True)
    cross_mean = jnp.mean(grad_hat * normed, -1, keepdims=True)
    return (grad_hat - first_mean - normed * cross_mean) * inverse


def gelu_exact(values):
    return jax.nn.gelu(values, approximate=False)


def adamw(master, first, second, gradient, rate, decay):
    first_new = beta_one * first + (1.0 - beta_one) * gradient
    second_new = beta_two * second + (1.0 - beta_two) * gradient * gradient
    first_hat = first_new / (1.0 - beta_one**step_count)
    second_hat = second_new / (1.0 - beta_two**step_count)
    master_new = master - rate * (first_hat / (jnp.sqrt(second_hat) + adam_eps) + decay * master)
    return (master_new, first_new, second_new)


def local(
    tokens,
    cotangent,
    segment_ids,
    pad_mask,
    skip_flags,
    in_master,
    spatial_master,
    out_master,
    vector_master,
    in_first,
    spatial_first,
    out_first,
    vector_first,
    in_second,
    spatial_second,
    out_second,
    vector_second,
):
    row_count = tokens.shape[0]
    local_len = tokens.shape[1]
    offset = lax.axis_index("pos") * local_len
    low_type = jnp.bfloat16
    in_flat, spatial_flat, out_flat, vector_flat = (
        lax.all_gather(in_master.astype(low_type), ("batch", "pos"), axis=0, tiled=True),
        lax.all_gather(spatial_master.astype(low_type), ("batch", "pos"), axis=0, tiled=True),
        lax.all_gather(out_master.astype(low_type), ("batch", "pos"), axis=0, tiled=True),
        lax.all_gather(vector_master.astype(low_type), ("batch", "pos"), axis=0, tiled=True),
    )
    weight_in = in_flat.reshape(D, HID)
    weight_spatial = spatial_flat.reshape(SEQ, SEQ)
    weight_out = out_flat.reshape(GATE, D)
    gain_in, bias_in, bias_hidden, gain_gate, bias_gate, bias_spatial, bias_out = split_vector(
        vector_flat.astype(jnp.float32)
    )
    seg_local = lax.dynamic_slice_in_dim(segment_ids, offset, local_len, 1)
    pad_local = lax.dynamic_slice_in_dim(pad_mask, offset, local_len, 1)
    keeping = pad_local.astype(jnp.float32) * (1.0 - skip_flags.astype(jnp.float32))[:, None]
    keep_flat = keeping.reshape(-1, 1)
    same_rows = (seg_local[:, :, None] == segment_ids[:, None, :]) & (pad_mask[:, None, :] == 1)
    spatial_rows = lax.dynamic_slice_in_dim(weight_spatial, offset, local_len, 0)
    mixing = jnp.where(same_rows, spatial_rows[None], jnp.zeros((), low_type))
    inputs = tokens.astype(jnp.float32).reshape(-1, D)
    normed_in, inverse_in = norm_parts(inputs)
    scaled_in = (normed_in * gain_in + bias_in).astype(low_type)
    hidden_pre = jnp.dot(scaled_in, weight_in, preferred_element_type=jnp.float32) + bias_hidden
    hidden, gelu_back = jax.vjp(gelu_exact, hidden_pre)
    left_half = hidden[:, :GATE]
    normed_gate, inverse_gate = norm_parts(hidden[:, GATE:])
    gate_low = (
        (normed_gate * gain_gate + bias_gate).astype(low_type).reshape(row_count, local_len, GATE)
    )
    gate_whole = lax.all_gather(gate_low, "pos", axis=1, tiled=True)
    bias_local = lax.dynamic_slice_in_dim(bias_spatial, offset, local_len)
    spatial = (
        jnp.einsum("rij,rjc->ric", mixing, gate_whole, preferred_element_type=jnp.float32)
        + bias_local[None, :, None]
    )
    spatial = spatial.reshape(-1, GATE)
    gated = (left_half * spatial).astype(low_type)
    branch = jnp.dot(gated, weight_out, preferred_element_type=jnp.float32) + bias_out
    mixed = (inputs + branch * keep_flat).astype(low_type).reshape(tokens.shape)
    back_flat = cotangent.astype(jnp.float32).reshape(-1, D)
    grad_branch = back_flat * keep_flat
    grad_bias_out = jnp.sum(grad_branch, 0)
    branch_low = grad_branch.astype(low_type)
    grad_weight_out = jnp.einsum("tg,td->gd", gated, branch_low, preferred_element_type=jnp.float32)
    grad_gated = jnp.einsum("td,gd->tg", branch_low, weight_out, preferred_element_type=jnp.float32)
    grad_spatial = grad_gated * left_half
    grad_left = grad_gated * spatial
    spatial_sum = jnp.sum(grad_spatial.reshape(row_count, local_len, GATE), (0, 2))
    grad_bias_spatial = lax.dynamic_update_slice_in_dim(
        jnp.zeros((SEQ,), jnp.float32), spatial_sum, offset, 0
    )
    spatial_low = grad_spatial.astype(low_type).reshape(row_count, local_len, GATE)
    partial_gate = jnp.einsum(
        "rij,ric->rjc", mixing, spatial_low, preferred_element_type=jnp.float32
    )
    grad_gate = lax.psum_scatter(partial_gate, "pos", scatter_dimension=1, tiled=True)
    products = jnp.einsum(
        "ric,rjc->rij", spatial_low, gate_whole, preferred_element_type=jnp.float32
    )
    row_block = jnp.sum(jnp.where(same_rows, products, 0.0), 0)
    grad_weight_spatial = lax.dynamic_update_slice_in_dim(
        jnp.zeros((SEQ, SEQ), jnp.float32), row_block, offset, 0
    )
    grad_gate = grad_gate.reshape(-1, GATE)
    grad_gain_gate = jnp.sum(grad_gate * normed_gate, 0)
    grad_bias_gate = jnp.sum(grad_gate, 0)
    grad_right = norm_back(grad_gate * gain_gate, normed_gate, inverse_gate)
    grad_hidden = jnp.concatenate([grad_left, grad_right], 1)
    grad_pre = gelu_back(grad_hidden)[0]
    grad_bias_hidden = jnp.sum(grad_pre, 0)
    pre_low = grad_pre.astype(low_type)
    grad_weight_in = jnp.einsum("td,th->dh", scaled_in, pre_low, preferred_element_type=jnp.float32)
    grad_scaled = jnp.einsum("th,dh->td", pre_low, weight_in, preferred_element_type=jnp.float32)
    grad_gain_in = jnp.sum(grad_scaled * normed_in, 0)
    grad_bias_in = jnp.sum(grad_scaled, 0)
    input_grad = (back_flat + norm_back(grad_scaled * gain_in, normed_in, inverse_in)).reshape(
        tokens.shape
    )
    grad_vector = jnp.concatenate(
        [
            grad_gain_in,
            grad_bias_in,
            grad_bias_hidden,
            grad_gain_gate,
            grad_bias_gate,
            grad_bias_spatial,
            grad_bias_out,
        ]
    )
    terms = (
        grad_weight_in.reshape(-1),
        grad_weight_spatial.reshape(-1),
        grad_weight_out.reshape(-1),
        grad_vector,
    )
    summed_all = lax.psum((terms[0], terms[1], terms[2], terms[3]), ("batch", "pos"))
    position = lax.axis_index(("batch", "pos"))
    owned = (in_master, spatial_master, out_master, vector_master)
    shards = tuple(
        (
            lax.dynamic_slice_in_dim(
                summed_part, position * master_part.shape[0], master_part.shape[0]
            )
            for summed_part, master_part in zip(summed_all, owned)
        )
    )
    in_new = adamw(in_master, in_first, in_second, shards[0], rate_in, decay_matrix)
    spatial_new = adamw(
        spatial_master, spatial_first, spatial_second, shards[1], rate_spatial, decay_matrix
    )
    out_new = adamw(out_master, out_first, out_second, shards[2], rate_out, decay_matrix)
    vector_new = adamw(vector_master, vector_first, vector_second, shards[3], rate_vector, 0.0)
    return (
        mixed,
        input_grad,
        in_new[0],
        in_new[1],
        in_new[2],
        spatial_new[0],
        spatial_new[1],
        spatial_new[2],
        out_new[0],
        out_new[1],
        out_new[2],
        vector_new[0],
        vector_new[1],
        vector_new[2],
    )


def solution(mesh):
    placed = (
        P("batch", "pos", None),
        P("batch", "pos", None),
        P("batch", None),
        P("batch", None),
        P("batch"),
        P(("batch", "pos")),
        P(("batch", "pos")),
        P(("batch", "pos")),
        P(("batch", "pos")),
        P(("batch", "pos")),
        P(("batch", "pos")),
        P(("batch", "pos")),
        P(("batch", "pos")),
        P(("batch", "pos")),
        P(("batch", "pos")),
        P(("batch", "pos")),
        P(("batch", "pos")),
    )
    return jax.shard_map(
        local,
        mesh=mesh,
        in_specs=placed,
        out_specs=(
            P("batch", "pos", None),
            P("batch", "pos", None),
            P(("batch", "pos")),
            P(("batch", "pos")),
            P(("batch", "pos")),
            P(("batch", "pos")),
            P(("batch", "pos")),
            P(("batch", "pos")),
            P(("batch", "pos")),
            P(("batch", "pos")),
            P(("batch", "pos")),
            P(("batch", "pos")),
            P(("batch", "pos")),
            P(("batch", "pos")),
        ),
        check_vma=False,
    )
```

profile of v0, /device:TPU:0, one launch (start us, length us, event | category | flops | bytes accessed | tf_op | source)
XLA Modules:
  0.0 1157.1 jit_solution(18101610685811018205)
XLA Ops:
  7.2 1.6 convert_element_type.67
  8.9 1.6 convert_element_type.63
  12.0 69.9 %all-gather = bf16[32,1,256]{2,1,0:T(2,128)(2,1)S(1)} all-gather(bf16[1,1,256]{2,1,0:T(2,128)(2,1)S(1)} %reshape.203), channel_id=1, replica_groups=mesh['batch'=8,'pos'=4] {'batch','pos'}, dimensions={0}, use_global_device_ids=true | all-gather | bytes 16896 | tf_op jit(solution)/shard_map/all_gather | solution.py:88
  82.0 69.2 %all_gather.17 = bf16[262144]{0:T(1024)(128)(2,1)S(1)} all-gather(bf16[8192]{0:T(1024)(128)(2,1)S(1)} %convert_element_type.64), channel_id=1, replica_groups=mesh['batch'=8,'pos'=4] {'batch','pos'}, dimensions={0}, use_global_device_ids=true | all-gather | bytes 540672 | tf_op jit(solution)/shard_map/all_gather | solution.py:86
  154.3 1.7 fusion.23
  159.3 2.1 fusion.18
  162.8 2.7 reshape.194
  165.6 6.2 reshape.190
  171.8 33.6 %multiply_multiply_fusion.5 = (f32[1024,3072]{1,0:T(8,128)S(1)}, f32[1024,3072]{1,0:T(8,128)}, f32[1024,3072]{1,0:T(8,128)}) fusion(f32[3072]{0:T(1024)S(1)} %bitcast.107, bf16[1024,512]{1,0:T(8,128)(2,1)} %bitcast.106, bf16[512,3072]{1,0:T(8,128)(2,1)} %reshape.190), kind=kOutput, calls=%fused_computation.17 | convolution fusion | flops 3425697792 | bytes 41955328 | tf_op jit(solution)/shard_map/dot_general | solution.py:106
  205.8 4.8 fusion.17
  211.8 1.6 copy-done.4
  213.4 10.1 fusion.40
  223.9 412.2 %reduce-scatter.2.cloned.1.call-done = f32[8,128,1536]{2,1,0:T(8,128)} async-done(((f32[8,512,1536]{2,1,0:T(8,128)}), f32[8,128,1536]{2,1,0:T(8,128)}) %reduce-scatter.2.cloned.1.call-update) | async-done | bytes 6291472 | tf_op jit(solution)/shard_map/reduce_scatter | solution.py:139
  636.1 3.6 fusion.61
  639.8 10.1 fusion.6
  651.8 5.7 subtract_multiply_fusion
  658.4 219.4 %all-gather.7.cloned.1.call-done = bf16[8,512,1536]{2,1,0:T(8,128)(2,1)} async-done(((bf16[8,128,1536]{2,1,0:T(8,128)(2,1)}), bf16[8,512,1536]{2,1,0:T(8,128)(2,1)}) %all-gather.7.cloned.1.call-update) | async-done | bytes 12582928 | tf_op jit(solution)/shard_map/all_gather | solution.py:113
  877.9 9.1 convolution_add_fusion
  887.0 12.1 %bitcast_multiply_fusion.2 = (f32[1024,1536]{1,0:T(8,128)}, bf16[1024,1536]{1,0:T(8,128)(2,1)}) fusion(f32[1024,1536]{1,0:T(8,128)} %get-tuple-element.64, f32[8,128,1536]{2,1,0:T(8,128)} %convolution_add_fusion, f32[1024,3072]{1,0:T(8,128)} %copy-done), kind=kLoop, calls=%fused_computation.21 | loop fusion | flops 4718592 | bytes 28311552 | tf_op jit(solution)/shard_map/mul | solution.py:130
  899.1 9.9 select_reduce_fusion
  910.4 13.6 %fusion.63 = (f32[3072]{0:T(1024)S(1)}, bf16[1024,3072]{1,0:T(8,128)(2,1)S(1)}) fusion(f32[1024,3072]{1,0:T(8,128)} %get-tuple-element.43, f32[1024,1536]{1,0:T(8,128)} %get-tuple-element.44, f32[1024,1536]{1,0:T(8,128)S(1)} %copy-done.1, f32[1024,3072]{1,0:T(8,128)} %get-tuple-element.63, f32[3072]{0:T(1024)S(1)} %bitcast.108), kind=kLoop, calls=%fused_computation.130 | loop fusion | flops 53474304 | bytes 44064768 | tf_op jit(solution)/shard_map/reduce_sum | solution.py:153
  924.1 4.1 fusion.38
  928.1 3.6 fusion.13
  931.8 4.0 copy.35
  935.9 2.5 fusion.20
  938.4 1.9 convolution_bitcast_fusion
  940.2 2.5 copy.37
  943.4 40.4 %psum.31 = f32[8192]{0:T(1024)S(1)} all-reduce(f32[8192]{0:T(1024)S(1)} %constant_dynamic-update-slice_fusion), channel_id=1, replica_groups=mesh['batch'=8,'pos'=4] {'batch','pos'}, use_global_device_ids=true, to_apply=%region_21.22 | all-reduce | flops 8192 | bytes 65536 | tf_op jit(solution)/shard_map/psum | solution.py:179
  984.6 5.3 fusion.27
  989.9 155.3 %all-reduce.3.cloned.1.call-done = (f32[1572864]{0:T(1024)}, f32[262144]{0:T(1024)}, f32[786432]{0:T(1024)}) async-done(((f32[1572864]{0:T(1024)}, f32[262144]{0:T(1024)}, f32[786432]{0:T(1024)}), (f32[1572864]{0:T(1024)}, f32[262144]{0:T(1024)}, f32[786432]{0:T(1024)})) %all-reduce.3.cloned.1.call-update) | async-done | bytes 10485776 | tf_op jit(solution)/shard_map/psum | solution.py:179
  1145.2 1.8 multiply_subtract_fusion
  1148.5 1.6 multiply_subtract_fusion.1
  (126 shorter events, 18.2 us)
Async XLA Ops:
  7.2 154.2 %copy-start.2 = (bf16[8,128,512]{2,1,0:T(8,128)(2,1)S(1)}, bf16[8,128,512]{2,1,0:T(8,128)(2,1)}, u32[]{:S(2)}) copy-start(bf16[8,128,512]{2,1,0:T(8,128)(2,1)} %param.17) | copy-start | bytes 3145732
  7.2 155.6 %all-gather.9.cloned.1.call-start = ((), (), s32[]{:S(2)}) async-start(), calls=%async_computation.3 | async-start | bytes 1622016 | tf_op jit(solution)/shard_map/all_gather | solution.py:87
  8.9 156.7 %all-gather.5.cloned.1.call-start = ((), (), s32[]{:S(2)}) async-start(), calls=%async_computation.1 | async-start | bytes 3244032 | tf_op jit(solution)/shard_map/all_gather | solution.py:85
  10.5 625.6 %reduce-scatter.2.cloned.1.call-start = ((), (), s32[]{:S(2)}) async-start(), calls=%async_computation.4 | async-start | bytes 31457280 | tf_op jit(solution)/shard_map/reduce_scatter | solution.py:139
  158.5 13.3 %copy-start.19 = (f32[2,1,256]{2,1,0:T(1,128)}, f32[2,1,256]{2,1,0:T(1,128)S(1)}, u32[]{:S(2)}) copy-start(f32[2,1,256]{2,1,0:T(1,128)S(1)} %get-tuple-element.57) | copy-start | bytes 6148
  158.5 13.3 %copy-start.24 = (f32[2,1,256]{2,1,0:T(1,128)}, f32[2,1,256]{2,1,0:T(1,128)S(1)}, u32[]{:S(2)}) copy-start(f32[2,1,256]{2,1,0:T(1,128)S(1)} %get-tuple-element.58) | copy-start | bytes 6148
  165.6 40.2 %copy-start.5 = (bf16[1536,512]{1,0:T(8,128)(2,1)}, bf16[1536,512]{1,0:T(8,128)(2,1)S(1)}, u32[]{:S(2)}) copy-start(bf16[1536,512]{1,0:T(8,128)(2,1)S(1)} %reshape.194) | copy-start | bytes 4718596
  223.6 654.3 %all-gather.7.cloned.1.call-start = ((), (), s32[]{:S(2)}) async-start(), calls=%async_computation.2 | async-start | bytes 15728640 | tf_op jit(solution)/shard_map/all_gather | solution.py:113
  636.1 13.8 %slice-start = ((s8[12582912]{0:T(1024)(128)(4,1)}), s8[4194304]{0:T(1024)(128)(4,1)S(1)}, s32[]{:S(2)}) async-start(s8[12582912]{0:T(1024)(128)(4,1)} %bitcast.93), calls=%async_computation.6 | async-start | bytes 8388608
  636.1 13.8 %slice-start.3 = ((s8[6291456]{0:T(1024)(128)(4,1)}), s8[4194304]{0:T(1024)(128)(4,1)S(1)}, s32[]{:S(2)}) async-start(s8[6291456]{0:T(1024)(128)(4,1)} %bitcast.95), calls=%async_computation.9 | async-start | bytes 8388608
  639.8 11.4 slice-start.2
  639.8 12.0 %slice-start.4 = ((s8[6291456]{0:T(1024)(128)(4,1)}), s8[2097152]{0:T(1024)(128)(4,1)S(1)}, s32[]{:S(2)}) async-start(s8[6291456]{0:T(1024)(128)(4,1)} %bitcast.95), calls=%async_computation.10 | async-start | bytes 4194304
  657.5 487.7 %all-reduce.3.cloned.1.call-start = ((), (), s32[]{:S(2)}) async-start(), calls=%async_computation.5 | async-start | bytes 20971520 | tf_op jit(solution)/shard_map/psum | solution.py:179
  910.4 13.6 %copy-start.3 = (bf16[8,128,512]{2,1,0:T(8,128)(2,1)S(1)}, bf16[8,128,512]{2,1,0:T(8,128)(2,1)}, u32[]{:S(2)}) copy-start(bf16[8,128,512]{2,1,0:T(8,128)(2,1)} %param.17) | copy-start | bytes 3145732
  910.4 13.7 %copy-start.8 = (bf16[512,3072]{1,0:T(8,128)(2,1)S(1)}, bf16[512,3072]{1,0:T(8,128)(2,1)}, u32[]{:S(2)}) copy-start(bf16[512,3072]{1,0:T(8,128)(2,1)} %reshape.190) | copy-start | bytes 9437188
  910.4 13.7 %copy-start.20 = (f32[2,1,256]{2,1,0:T(1,128)S(1)}, f32[2,1,256]{2,1,0:T(1,128)}, u32[]{:S(2)}) copy-start(f32[2,1,256]{2,1,0:T(1,128)} %copy-done.19) | copy-start | bytes 6148
  910.4 13.7 %copy-start.21 = (f32[1024]{0:T(1024)S(1)}, f32[1024]{0:T(1024)}, u32[]{:S(2)}) copy-start(f32[1024]{0:T(1024)} %get-tuple-element.59) | copy-start | bytes 12292
  910.4 13.7 %copy-start.22 = (f32[1024]{0:T(1024)S(1)}, f32[1024]{0:T(1024)}, u32[]{:S(2)}) copy-start(f32[1024]{0:T(1024)} %get-tuple-element.61) | copy-start | bytes 12292
  910.4 13.7 %copy-start.25 = (f32[2,1,256]{2,1,0:T(1,128)S(1)}, f32[2,1,256]{2,1,0:T(1,128)}, u32[]{:S(2)}) copy-start(f32[2,1,256]{2,1,0:T(1,128)} %copy-done.24) | copy-start | bytes 6148
  942.7 41.1 %copy-start.27 = (f32[256]{0:T(256)S(1)}, f32[256]{0:T(256)}, u32[]{:S(2)}) copy-start(f32[256]{0:T(256)} %param.25) | copy-start | bytes 3076
  942.7 41.1 %copy-start.28 = (f32[256]{0:T(256)S(1)}, f32[256]{0:T(256)}, u32[]{:S(2)}) copy-start(f32[256]{0:T(256)} %param.29) | copy-start | bytes 3076
  942.7 41.1 %copy-start.29 = (f32[256]{0:T(256)S(1)}, f32[256]{0:T(256)}, u32[]{:S(2)}) copy-start(f32[256]{0:T(256)} %param.33) | copy-start | bytes 3076
  942.7 41.8 %copy-start.26 = (f32[2,1,256]{2,1,0:T(1,128)S(1)}, f32[2,1,256]{2,1,0:T(1,128)}, u32[]{:S(2)}) copy-start(f32[2,1,256]{2,1,0:T(1,128)} %get-tuple-element.55) | copy-start | bytes 6148
  984.5 160.7 %copy-start.10 = (f32[49152]{0:T(1024)S(1)}, f32[49152]{0:T(1024)}, u32[]{:S(2)}) copy-start(f32[49152]{0:T(1024)} %param.22) | copy-start | bytes 589828
  984.5 160.7 %copy-start.12 = (f32[49152]{0:T(1024)S(1)}, f32[49152]{0:T(1024)}, u32[]{:S(2)}) copy-start(f32[49152]{0:T(1024)} %param.26) | copy-start | bytes 589828
  984.5 160.7 %copy-start.13 = (f32[49152]{0:T(1024)S(1)}, f32[49152]{0:T(1024)}, u32[]{:S(2)}) copy-start(f32[49152]{0:T(1024)} %param.30) | copy-start | bytes 589828
  984.5 162.5 %copy-start.14 = (f32[8192]{0:T(1024)S(1)}, f32[8192]{0:T(1024)}, u32[]{:S(2)}) copy-start(f32[8192]{0:T(1024)} %param.23) | copy-start | bytes 98308
  984.5 162.5 %copy-start.17 = (f32[8192]{0:T(1024)S(1)}, f32[8192]{0:T(1024)}, u32[]{:S(2)}) copy-start(f32[8192]{0:T(1024)} %param.27) | copy-start | bytes 98308
  984.6 162.5 %copy-start.18 = (f32[8192]{0:T(1024)S(1)}, f32[8192]{0:T(1024)}, u32[]{:S(2)}) copy-start(f32[8192]{0:T(1024)} %param.31) | copy-start | bytes 98308
  984.6 163.9 %copy-start.11 = (f32[24576]{0:T(1024)S(1)}, f32[24576]{0:T(1024)}, u32[]{:S(2)}) copy-start(f32[24576]{0:T(1024)} %param.24) | copy-start | bytes 294916
  984.6 163.9 %copy-start.15 = (f32[24576]{0:T(1024)S(1)}, f32[24576]{0:T(1024)}, u32[]{:S(2)}) copy-start(f32[24576]{0:T(1024)} %param.28) | copy-start | bytes 294916
  984.6 163.9 %copy-start.16 = (f32[24576]{0:T(1024)S(1)}, f32[24576]{0:T(1024)}, u32[]{:S(2)}) copy-start(f32[24576]{0:T(1024)} %param.32) | copy-start | bytes 294916
  (8 other events, 44.4 us)
Sparse Core Ops, SparseCore 0:
  11.4 57.6 all-gather.8
  72.6 59.3 all-gather.4
  223.7 412.3 reduce-scatter.1
  657.6 220.1 all-gather.6
  942.9 202.3 all-reduce.2
where the time goes:
time: 1170 us; the launch traced here: 1160 us
  waiting for transfers between devices  787 us (67%)
  blocking collectives  180 us (15%)
  matrix products  82.5 us (7%)
  other arithmetic  69 us (6%)
  local copies, waits for them, and re-layouts  23.9 us (2%)
  between operations  14.7 us (1%)
    reduce_scatter x1, waiting for transfers between devices, local(): lax.psum_scatter(partial_gate, 'pos', scatter_dimension=1, tiled=True)  412 us
    all_gather x1, waiting for transfers between devices, local(): gate_whole = lax.all_gather(gate_low, 'pos', axis=1, tiled=True)  219 us
    psum x1, waiting for transfers between devices, local(): lax.psum((terms[0], terms[1], terms[2], terms[3]), ('batch', 'pos'))  155 us
    all_gather x1, blocking collectives, local(): lax.all_gather(vector_master.astype(low_type), ('batch', 'pos'), axis=0,...  69.9 us
    all_gather x1, blocking collectives, local(): lax.all_gather(spatial_master.astype(low_type), ('batch', 'pos'), axis=0,...  69.2 us
    psum x1, blocking collectives, local(): lax.psum((terms[0], terms[1], terms[2], terms[3]), ('batch', 'pos'))  40.4 us
    dot_general x1, matrix products, local(): jnp.dot(scaled_in, weight_in, preferred_element_type=jnp.float32)  33.6 us
  transfers between devices with their start and end apart: 5, of which 3 were waited for; matrix products, arithmetic and copies ran while one was open for 2% of the time, Pallas kernels for 0%

commit v1 on v0

v1 whole, which is shorter than its diff:
```python
import jax
import jax.numpy as jnp
from jax import lax
from jax.sharding import PartitionSpec as P

D = 512
HID = 3072
SEQ = 512
GATE = 1536
LANE = 128

norm_eps = 1e-05
beta_one = 0.9
beta_two = 0.999
adam_eps = 1e-08
step_count = 10.0
decay_matrix = 0.1
rate_in = 0.12
rate_spatial = 0.2
rate_out = 0.07
rate_vector = 1.0

low_type = jnp.bfloat16
wide = jnp.float32


def split_vector(vector):
    lengths = [D, D, HID, GATE, GATE, SEQ, D]
    pieces = []
    cursor = 0
    for length in lengths:
        pieces.append(vector[cursor : cursor + length])
        cursor = cursor + length
    return pieces


def norm_parts(values):
    average = jnp.mean(values, -1, keepdims=True)
    centred = values - average
    spread = jnp.mean(centred * centred, -1, keepdims=True)
    inverse = lax.rsqrt(spread + norm_eps)
    return (centred * inverse, inverse)


def norm_back(grad_hat, normed, inverse):
    first_mean = jnp.mean(grad_hat, -1, keepdims=True)
    cross_mean = jnp.mean(grad_hat * normed, -1, keepdims=True)
    return (grad_hat - first_mean - normed * cross_mean) * inverse


def gelu_exact(values):
    return jax.nn.gelu(values, approximate=False)


def adamw(master, first, second, gradient, rate, decay):
    first_new = beta_one * first + (1.0 - beta_one) * gradient
    second_new = beta_two * second + (1.0 - beta_two) * gradient * gradient
    first_hat = first_new / (1.0 - beta_one**step_count)
    second_hat = second_new / (1.0 - beta_two**step_count)
    master_new = master - rate * (first_hat / (jnp.sqrt(second_hat) + adam_eps) + decay * master)
    return (master_new, first_new, second_new)


def swap(value, axis, size, mask):
    return lax.ppermute(value, axis, [(i, i ^ mask) for i in range(size)])


def bit_count(size):
    bits = size.bit_length() - 1
    assert size == 1 << bits
    return bits


def batch_rounds(bits):
    if bits == 3:
        return [(1, 2), (0,)]
    return [(b,) for b in range(1, bits)] + [(0,)]


def gather_blocks(block, sizes, place):
    batch_size, pos_size = sizes
    b, z = place
    rows, cols = block.shape
    bits = bit_count(batch_size)
    zbits = bit_count(pos_size)
    total = bits + zbits
    held = block.reshape((1,) * total + (rows, cols))

    def exchange(held, axis_name, size, index, group, shift):
        pieces = [held]
        for g in range(1, 1 << len(group)):
            mask = sum((1 << group[i]) for i in range(len(group)) if (g >> i) & 1)
            pieces.append(swap(held, axis_name, size, mask))
        for bit in group:
            axis = total - 1 - (bit + shift)
            mine = (index >> bit) & 1
            merged = []
            for a, c in zip(pieces[0::2], pieces[1::2]):
                merged.append(
                    jnp.where(
                        mine == 0,
                        jnp.concatenate([a, c], axis),
                        jnp.concatenate([c, a], axis),
                    )
                )
            pieces = merged
        return pieces[0]

    for bit in reversed(range(zbits)):
        held = exchange(held, "pos", pos_size, z, (bit,), 0)
    for group in batch_rounds(bits):
        held = exchange(held, "batch", batch_size, b, group, zbits)
    return held.reshape(batch_size * pos_size * rows, cols)


def reduce_blocks(grad, sizes, place):
    batch_size, pos_size = sizes
    b, z = place
    bits = bit_count(batch_size)
    zbits = bit_count(pos_size)
    total = bits + zbits
    cols = grad.shape[1]
    rows = grad.shape[0] // (batch_size * pos_size)
    held = grad.reshape((2,) * total + (rows, cols))

    def halve(held, axis_name, size, index, group, shift):
        parts = {0: held}
        for i, bit in enumerate(group):
            axis = total - 1 - (bit + shift)
            mine = (index >> bit) & 1
            spread = {}
            for g, part in parts.items():
                spread[g] = lax.dynamic_slice_in_dim(part, mine, 1, axis)
                spread[g | (1 << i)] = lax.dynamic_slice_in_dim(part, 1 - mine, 1, axis)
            parts = spread
        summed = parts[0].astype(wide)
        for g, part in parts.items():
            if g:
                mask = sum((1 << group[i]) for i in range(len(group)) if (g >> i) & 1)
                summed = summed + swap(part, axis_name, size, mask).astype(wide)
        return summed.astype(grad.dtype)

    for group in reversed(batch_rounds(bits)):
        held = halve(held, "batch", batch_size, b, group, zbits)
    for bit in range(zbits):
        held = halve(held, "pos", pos_size, z, (bit,), 0)
    return held.reshape(rows, cols)


def local_fn(sizes):
    batch_size, pos_size = sizes

    def local(
        tokens,
        cotangent,
        segment_ids,
        pad_mask,
        skip_flags,
        in_master,
        spatial_master,
        out_master,
        vector_master,
        in_first,
        spatial_first,
        out_first,
        vector_first,
        in_second,
        spatial_second,
        out_second,
        vector_second,
    ):
        b = lax.axis_index("batch")
        z = lax.axis_index("pos")
        place = (b, z)
        devices = batch_size * pos_size
        rows = tokens.shape[0]
        length = tokens.shape[1]
        mine = rows // pos_size

        def relative(value, axis):
            return jnp.concatenate(
                [
                    lax.dynamic_slice_in_dim(
                        value, (z ^ k) * (value.shape[axis] // pos_size), value.shape[axis] // pos_size, axis
                    )
                    for k in range(pos_size)
                ],
                axis,
            )

        def to_rows(value):
            parts = []
            for k in range(pos_size):
                part = lax.dynamic_slice_in_dim(value, (z ^ k) * mine, mine, 0)
                parts.append(part if k == 0 else swap(part, "pos", pos_size, k))
            return jnp.concatenate(parts, 1)

        def to_places(value):
            parts = []
            for k in range(pos_size):
                part = lax.slice_in_dim(value, k * length, (k + 1) * length, axis=1)
                parts.append(part if k == 0 else swap(part, "pos", pos_size, k))
            return relative(jnp.concatenate(parts, 0), 0)

        in_rows = D // devices if D % devices == 0 else 1
        in_block = in_master.astype(low_type).reshape(in_rows, -1)
        vector_block = vector_master.astype(low_type).reshape(in_rows, -1)
        vector_cols = vector_block.shape[1]
        vector_block = jnp.pad(vector_block, ((0, 0), (0, LANE - vector_cols)))
        in_block = jnp.concatenate([in_block, vector_block], 1)
        spatial_block = spatial_master.astype(low_type).reshape(-1, D)
        out_block = out_master.astype(low_type).reshape(-1, D)
        rest_block = jnp.concatenate([spatial_block, out_block], 0)
        spatial_rows = spatial_block.shape[0]
        in_width = in_master.shape[0] // in_rows

        in_all = gather_blocks(in_block, sizes, place)
        inputs_low = to_rows(tokens)
        rest_all = gather_blocks(rest_block, sizes, place).reshape(devices, -1, D)
        back_low = to_rows(cotangent)

        weight_in = in_all[:, :in_width].reshape(D, HID)
        vector_flat = in_all[:, in_width : in_width + vector_cols].reshape(-1)
        weight_spatial = rest_all[:, :spatial_rows].reshape(SEQ, SEQ)
        weight_out = rest_all[:, spatial_rows:].reshape(GATE, D)
        gain_in, bias_in, bias_hidden, gain_gate, bias_gate, bias_spatial, bias_out = split_vector(
            vector_flat.astype(wide)
        )

        own_rows = lambda value: lax.dynamic_slice_in_dim(value, z * mine, mine, 0)
        segments = relative(own_rows(segment_ids), 1)
        padding = relative(own_rows(pad_mask), 1)
        keeping = padding.astype(wide) * (1.0 - own_rows(skip_flags).astype(wide))[:, None]
        keep_flat = keeping.reshape(-1, 1)
        same_rows = (segments[:, :, None] == segments[:, None, :]) & (padding[:, None, :] == 1)
        mixing_rows = relative(relative(weight_spatial, 0), 1)
        bias_rows = relative(bias_spatial, 0)
        mixing = jnp.where(same_rows, mixing_rows[None], jnp.zeros((), low_type))

        inputs = inputs_low.astype(wide).reshape(-1, D)
        normed_in, inverse_in = norm_parts(inputs)
        scaled_in = (normed_in * gain_in + bias_in).astype(low_type)
        hidden_pre = jnp.dot(scaled_in, weight_in, preferred_element_type=wide) + bias_hidden
        hidden, gelu_back = jax.vjp(gelu_exact, hidden_pre)
        left_half = hidden[:, :GATE]
        normed_gate, inverse_gate = norm_parts(hidden[:, GATE:])
        gate_low = (normed_gate * gain_gate + bias_gate).astype(low_type).reshape(mine, SEQ, GATE)
        spatial = (
            jnp.einsum("rij,rjc->ric", mixing, gate_low, preferred_element_type=wide)
            + bias_rows[None, :, None]
        ).reshape(-1, GATE)
        gated = (left_half * spatial).astype(low_type)
        branch = jnp.dot(gated, weight_out, preferred_element_type=wide) + bias_out
        mixed_rows = (inputs + branch * keep_flat).astype(low_type).reshape(mine, SEQ, D)
        mixed = to_places(mixed_rows)

        grad_branch = back_low.astype(wide).reshape(-1, D) * keep_flat
        grad_bias_out = jnp.sum(grad_branch, 0)
        branch_low = grad_branch.astype(low_type)
        grad_weight_out = jnp.einsum("tg,td->gd", gated, branch_low, preferred_element_type=wide)
        grad_gated = jnp.einsum("td,gd->tg", branch_low, weight_out, preferred_element_type=wide)
        grad_spatial = grad_gated * left_half
        grad_left = grad_gated * spatial
        grad_bias_spatial = jnp.sum(grad_spatial.reshape(mine, SEQ, GATE), (0, 2))
        spatial_low = grad_spatial.astype(low_type).reshape(mine, SEQ, GATE)
        grad_gate = jnp.einsum("rij,ric->rjc", mixing, spatial_low, preferred_element_type=wide)
        products = jnp.einsum("ric,rjc->rij", spatial_low, gate_low, preferred_element_type=wide)
        grad_weight_spatial = jnp.sum(jnp.where(same_rows, products, 0.0), 0)
        grad_gate = grad_gate.reshape(-1, GATE)
        grad_gain_gate = jnp.sum(grad_gate * normed_gate, 0)
        grad_bias_gate = jnp.sum(grad_gate, 0)

        grad_rest = jnp.concatenate(
            [
                relative(relative(grad_weight_spatial, 0), 1)
                .astype(low_type)
                .reshape(devices, spatial_rows, D),
                grad_weight_out.astype(low_type).reshape(devices, -1, D),
            ],
            1,
        )
        rest_sum = reduce_blocks(grad_rest.reshape(-1, D), sizes, place)

        grad_right = norm_back(grad_gate * gain_gate, normed_gate, inverse_gate)
        grad_hidden = jnp.concatenate([grad_left, grad_right], 1)
        grad_pre = gelu_back(grad_hidden)[0]
        grad_bias_hidden = jnp.sum(grad_pre, 0)
        pre_low = grad_pre.astype(low_type)
        grad_weight_in = jnp.einsum("td,th->dh", scaled_in, pre_low, preferred_element_type=wide)
        grad_scaled = jnp.einsum("th,dh->td", pre_low, weight_in, preferred_element_type=wide)
        grad_gain_in = jnp.sum(grad_scaled * normed_in, 0)
        grad_bias_in = jnp.sum(grad_scaled, 0)
        branch_grad = norm_back(grad_scaled * gain_in, normed_in, inverse_in)
        branch_grad = branch_grad.astype(low_type).reshape(mine, SEQ, D)
        input_grad = cotangent.astype(wide) + to_places(branch_grad).astype(wide)

        grad_vector = jnp.concatenate(
            [
                grad_gain_in,
                grad_bias_in,
                grad_bias_hidden,
                grad_gain_gate,
                grad_bias_gate,
                relative(grad_bias_spatial, 0),
                grad_bias_out,
            ]
        )
        vector_part = grad_vector.astype(low_type).reshape(in_rows * devices, -1)
        vector_part = jnp.pad(vector_part, ((0, 0), (0, LANE - vector_cols)))
        in_part = grad_weight_in.astype(low_type).reshape(in_rows * devices, -1)
        in_sum = reduce_blocks(jnp.concatenate([in_part, vector_part], 1), sizes, place)

        shards = (
            in_sum[:, :in_width].reshape(-1).astype(wide),
            rest_sum[:spatial_rows].reshape(-1).astype(wide),
            rest_sum[spatial_rows:].reshape(-1).astype(wide),
            in_sum[:, in_width : in_width + vector_cols].reshape(-1).astype(wide),
        )
        in_new = adamw(in_master, in_first, in_second, shards[0], rate_in, decay_matrix)
        spatial_new = adamw(
            spatial_master, spatial_first, spatial_second, shards[1], rate_spatial, decay_matrix
        )
        out_new = adamw(out_master, out_first, out_second, shards[2], rate_out, decay_matrix)
        vector_new = adamw(vector_master, vector_first, vector_second, shards[3], rate_vector, 0.0)
        return (
            mixed,
            input_grad,
            in_new[0],
            in_new[1],
            in_new[2],
            spatial_new[0],
            spatial_new[1],
            spatial_new[2],
            out_new[0],
            out_new[1],
            out_new[2],
            vector_new[0],
            vector_new[1],
            vector_new[2],
        )

    return local


def solution(mesh):
    sizes = (mesh.shape["batch"], mesh.shape["pos"])
    flat = P(("batch", "pos"))
    acts = P("batch", "pos", None)
    placed = (acts, acts, P("batch", None), P("batch", None), P("batch")) + (flat,) * 12
    return jax.shard_map(
        local_fn(sizes),
        mesh=mesh,
        in_specs=placed,
        out_specs=(acts, acts) + (flat,) * 12,
        check_vma=False,
    )
```

time: 1170 us -> 321 us (0.27)
  waiting for transfers between devices: 787 us -> 98.8 us
  blocking collectives: 180 us -> 0 us
  starting transfers between devices: 0.38 us -> 53.8 us
  between operations: 14.7 us -> 1.97 us
    reduce_scatter x1 -> x0, waiting for transfers between devices: 412 us -> none  [local(): lax.psum_scatter(partial_gate, 'pos', scatter_dimension=1, tiled=True)]
    all_gather x3 -> x0, waiting for transfers between devices: 219 us -> none  [the longest x1 219 us: local(): gate_whole = lax.all_gather(gate_low, 'pos', axis=1, tiled=True)]
    psum x1 -> x0, waiting for transfers between devices: 155 us -> none  [local(): lax.psum((terms[0], terms[1], terms[2], terms[3]), ('batch', 'pos'))]
    all_gather x2 -> x0, blocking collectives: 139 us -> none  [the longest x1 69.9 us: local(): lax.all_gather(vector_master.astype(low_type), ('batch', 'pos'), axis=0,...]
    ppermute x0 -> x36, waiting for transfers between devices: none -> 98.8 us  [swap(): return lax.ppermute(value, axis, [(i, i ^ mask) for i in range(size)])]
    ppermute x0 -> x36, starting transfers between devices: none -> 53.8 us  [swap(): return lax.ppermute(value, axis, [(i, i ^ mask) for i in range(size)])]
    psum x1 -> x0, blocking collectives: 40.4 us -> none  [local(): lax.psum((terms[0], terms[1], terms[2], terms[3]), ('batch', 'pos'))]
  transfers between devices with their start and end apart: 5 -> 36, of which waited for: 3 -> 14; matrix products, arithmetic and copies ran while one was open for 2% -> 10% of each run, Pallas kernels for 0% -> 0%
where the time goes in v1:
time: 321 us; the launch traced here: 316 us
  waiting for transfers between devices  98.8 us (31%)
  matrix products  73.2 us (23%)
  other arithmetic  67.3 us (21%)
  starting transfers between devices  53.8 us (17%)
  local copies, waits for them, and re-layouts  20.8 us (6%)
    ppermute x36, waiting for transfers between devices, swap(): return lax.ppermute(value, axis, [(i, i ^ mask) for i in range(size)])  98.8 us
    ppermute x36, starting transfers between devices, swap(): return lax.ppermute(value, axis, [(i, i ^ mask) for i in range(size)])  53.8 us
    dot_general x1, matrix products, local(): jnp.dot(scaled_in, weight_in, preferred_element_type=wide) + bias_hidden  33.2 us
    reduce_sum x1, other arithmetic, local(): grad_bias_hidden = jnp.sum(grad_pre, 0)  14.1 us
    mul x1, other arithmetic, local(): grad_left = grad_gated * spatial  11.9 us
    unnamed x107, local copies, waits for them, and re-layouts  11.3 us
    mul x1, other arithmetic, norm_back(): return (grad_hat - first_mean - normed * cross_mean) * inverse  8.73 us
    dot_general x1, matrix products, local(): jnp.einsum('td,gd->tg', branch_low, weight_out, preferred_element_type=wide)  7.65 us
  transfers between devices with their start and end apart: 36, of which 14 were waited for; matrix products, arithmetic and copies ran while one was open for 10% of the time, Pallas kernels for 0%

profile of v1, /device:TPU:0, one launch (start us, length us, event | category | flops | bytes accessed | tf_op | source)
XLA Modules:
  0.0 315.9 jit_solution(5626351855210109248)
XLA Ops:
  2.5 4.1 %collective-permute-start.9 = (bf16[1,1,1,1,1,64,512]{6,5,4,3,2,1,0:T(8,128)(2,1)S(1)}, bf16[1,1,1,1,1,64,512]{6,5,4,3,2,1,0:T(8,128)(2,1)S(1)}, u32[]{:S(2)}, u32[]{:S(2)}) collective-permute-start(bf16[1,1,1,1,1,64,512]{6,5,4,3,2,1,0:T(8,128)(2,1)S(1)} %bitcast.170), channel_id=1, source_target_pairs={{0,2},{1,3},{2,0},{3,1},{4,6},{5,7},{6,4},{7,5},{8,10},{9,11},{10,... | collective-permute-start | bytes 196616 | tf_op jit(solution)/shard_map/ppermute | solution.py:65
  12.5 2.6 collective-permute-start.1
  21.1 13.7 %collective-permute-done.10 = bf16[1,1,1,2,1,64,512]{6,5,3,4,2,1,0:T(8,128)(2,1)S(1)} collective-permute-done((bf16[1,1,1,2,1,64,512]{6,5,3,4,2,1,0:T(8,128)(2,1)S(1)}, bf16[1,1,1,2,1,64,512]{6,5,3,4,2,1,0:T(8,128)(2,1)S(1)}, u32[]{:S(2)}, u32[]{:S(2)}) %collective-permute-start.10) | collective-permute-done | bytes 131104 | tf_op jit(solution)/shard_map/ppermute | solution.py:65
  43.5 11.0 %collective-permute-done.12 = bf16[1,1,1,2,2,64,512]{6,5,4,3,2,1,0:T(8,128)(2,1)S(1)} collective-permute-done((bf16[1,1,1,2,2,64,512]{6,5,4,3,2,1,0:T(8,128)(2,1)S(1)}, bf16[1,1,1,2,2,64,512]{6,5,4,3,2,1,0:T(8,128)(2,1)S(1)}, u32[]{:S(2)}, u32[]{:S(2)}) %collective-permute-start.12) | collective-permute-done | bytes 262176 | tf_op jit(solution)/shard_map/ppermute | solution.py:65
  55.9 3.1 collective-permute-start.20
  59.3 2.5 collective-permute-done.6
  63.7 8.0 %collective-permute-done.5 = bf16[1,1,1,2,2,16,3200]{6,5,4,3,2,1,0:T(8,128)(2,1)S(1)} collective-permute-done((bf16[1,1,1,2,2,16,3200]{6,5,4,3,2,1,0:T(8,128)(2,1)S(1)}, bf16[1,1,1,2,2,16,3200]{6,5,4,3,2,1,0:T(8,128)(2,1)S(1)}, u32[]{:S(2)}, u32[]{:S(2)}) %collective-permute-start.5) | collective-permute-done | bytes 409632 | tf_op jit(solution)/shard_map/ppermute | solution.py:65
  81.8 33.2 %multiply_multiply_fusion.5 = (f32[1024,3072]{1,0:T(8,128)S(1)}, f32[1024,3072]{1,0:T(8,128)}, f32[1024,3072]{1,0:T(8,128)}) fusion(f32[3072]{0:T(1024)S(1)} %slice.105, bf16[1024,512]{1,0:T(8,128)(2,1)S(1)} %fusion.28, bf16[512,3200]{1,0:T(8,128)(2,1)} %bitcast.149), kind=kOutput, calls=%fused_computation.17 | convolution fusion | flops 3425697792 | bytes 41955328 | tf_op jit(solution)/shard_map/dot_general | solution.py:243
  115.0 4.6 %copy-done = f32[1024,3072]{1,0:T(8,128)} copy-done((f32[1024,3072]{1,0:T(8,128)}, f32[1024,3072]{1,0:T(8,128)S(1)}, u32[]{:S(2)}) %copy-start) | copy-done | bytes 12582936
  120.1 7.7 %fusion.18 = (bf16[1024,1536]{1,0:T(8,128)(2,1)}, f32[1024]{0:T(1024)S(1)}, f32[1024,1536]{1,0:T(8,128)S(1)}) fusion(f32[1024,3072]{1,0:T(8,128)} %copy-done, f32[1024]{0:T(1024)S(1)} %broadcast_multiply_fusion.3, bf16[1024,512]{1,0:T(8,128)(2,1)S(1)} %bitcast.146, bf16[1536,512]{1,0:T(8,128)(2,1)} %bitcast.144), kind=kOutput, calls=%fused_computation.48 | convolution fusion | flops 1618476032 | bytes 24649728 | tf_op jit(solution)/shard_map/td,gd->tg/dot_general | solution.py:261
  128.3 6.6 %fusion.73 = (bf16[1536]{0:T(1024)(128)(2,1)}, f32[2,512]{1,0:T(2,128)}, f32[2,512,1536]{2,1,0:T(8,128)S(1)}) fusion(f32[1536]{0:T(1024)S(1)} %slice.110, bf16[2,512,1536]{2,1,0:T(8,128)(2,1)} %bitcast.151, s32[2,512]{1,0:T(2,128)} %pad_add_fusion, pred[2,512]{1,0:T(4,128)(4,1)} %broadcast_compare_fusion, bf16[512,512]{1,0:T(8,128)(2,1)} %pad_maximum_fusion.9), kind=kOutput, calls=%fused_computation.230 | convolution fusion | flops 1616901632 | bytes 9979904 | tf_op jit(solution)/shard_map/rij,ric->rjc/dot_general | solution.py:266
  135.0 4.5 %fusion.7 = (bf16[1536]{0:T(1024)(128)(2,1)}, f32[1024]{0:T(1024)}, f32[1024]{0:T(1024)}) fusion(f32[2,512,1536]{2,1,0:T(8,128)S(1)} %get-tuple-element.131, f32[1024]{0:T(1024)} %add_rsqrt_fusion, f32[1024]{0:T(1024)S(1)} %broadcast_multiply_fusion.3, f32[1024,3072]{1,0:T(8,128)S(1)} %bitcast.139, f32[1536]{0:T(1024)S(1)} %slice.110, ...), kind=kLoop, calls=%fused_computation.22 | loop fusion | flops 14152192 | bytes 25191424 | tf_op jit(solution)/shard_map/reduce_sum | solution.py:270
  141.0 8.7 %subtract_multiply_fusion = (f32[1024,1536]{1,0:T(8,128)}, bf16[1024,1536]{1,0:T(8,128)(2,1)S(1)}) fusion(f32[2,512,1536]{2,1,0:T(8,128)} %copy-done.2, f32[1024]{0:T(1024)S(1)} %broadcast_multiply_fusion.2, f32[1024]{0:T(1024)S(1)} %bitcast.187, f32[1536]{0:T(1024)S(1)} %slice.110, f32[1024]{0:T(1024)} %add_rsqrt_fusion, ...), kind=kLoop, calls=%fused_computation.26 | loop fusion | flops 15728640 | bytes 22048768 | tf_op jit(solution)/shard_map/mul | solution.py:48
  149.8 2.8 select_reduce_fusion
  152.8 6.4 %convolution_add_fusion = f32[2,512,1536]{2,1,0:T(8,128)} fusion(bf16[2,512,1536]{2,1,0:T(8,128)(2,1)} %bitcast.154, f32[512]{0:T(512)S(1)} %pad_maximum_fusion.14, s32[2,512]{1,0:T(2,128)S(1)} %copy-done.37, pred[2,512]{1,0:T(4,128)(4,1)S(1)} %copy-done.38, bf16[512,512]{1,0:T(8,128)(2,1)S(1)} %copy-done.17), kind=kOutput, calls=%fused_computation.36 | convolution fusion | flops 1613758464 | bytes 9968640 | tf_op jit(solution)/shard_map/rij,rjc->ric/dot_general | solution.py:249
  159.2 11.9 %bitcast_multiply_fusion.2 = (f32[1024,1536]{1,0:T(8,128)}, bf16[1024,1536]{1,0:T(8,128)(2,1)}) fusion(f32[1024,1536]{1,0:T(8,128)} %copy-done.1, f32[2,512,1536]{2,1,0:T(8,128)} %convolution_add_fusion, f32[1024,3072]{1,0:T(8,128)} %copy-done), kind=kLoop, calls=%fused_computation.23 | loop fusion | flops 4718592 | bytes 28311552 | tf_op jit(solution)/shard_map/mul | solution.py:263
  171.2 14.1 %fusion.78 = (bf16[3072]{0:T(1024)(128)(2,1)S(1)}, bf16[1024,3072]{1,0:T(8,128)(2,1)S(1)}) fusion(f32[1024,3072]{1,0:T(8,128)} %get-tuple-element.38, f32[1024,1536]{1,0:T(8,128)} %get-tuple-element.41, f32[1024,1536]{1,0:T(8,128)} %get-tuple-element.45, f32[1024,3072]{1,0:T(8,128)} %get-tuple-element.129, f32[3072]{0:T(1024)S(1)} %slice.105), kind=kLoop, calls=%fused_computation.231 | loop fusion | flops 53474304 | bytes 44058624 | tf_op jit(solution)/shard_map/reduce_sum | solution.py:287
  185.3 5.2 %convolution_convert_fusion = bf16[512,3072]{1,0:T(8,128)(2,1)} fusion(bf16[1024,512]{1,0:T(8,128)(2,1)S(1)} %fusion.28, bf16[1024,3072]{1,0:T(8,128)(2,1)S(1)} %get-tuple-element.36), kind=kOutput, calls=%fused_computation.35 | convolution fusion | flops 3222798336 | bytes 10485760 | tf_op jit(solution)/shard_map/td,th->dh/dot_general | solution.py:289
  190.6 5.1 %fusion.33 = (bf16[512]{0:T(512)(128)(2,1)S(1)}, f32[1024]{0:T(1024)S(1)}, f32[1024]{0:T(1024)S(1)}, bf16[512]{0:T(512)(128)(2,1)S(1)}, f32[1024,512]{1,0:T(8,128)}) fusion(bf16[2,512,512]{2,1,0:T(8,128)(2,1)S(1)} %get-tuple-element.40, f32[1024]{0:T(1024)S(1)} %bitcast.180, f32[1024]{0:T(1024)S(1)} %bitcast.183, f32[512]{0:T(512)S(1)} %copy-done.29, ...), kind=kOutput, calls=%fused_computation.70 | convolution fusion | flops 3226465280 | bytes 12603392 | tf_op jit(solution)/shard_map/th,dh->td/dot_general | solution.py:290
  207.6 4.3 %fusion.34 = bf16[1024,512]{1,0:T(8,128)(2,1)S(1)} fusion(bf16[2,512,512]{2,1,0:T(8,128)(2,1)S(1)} %get-tuple-element.40, bf16[1024,1536]{1,0:T(8,128)(2,1)} %get-tuple-element.46, bf16[1536,512]{1,0:T(8,128)(2,1)} %bitcast.145, f32[1024]{0:T(1024)S(1)} %bitcast.186, f32[512]{0:T(512)S(1)} %slice.117), kind=kOutput, calls=%fused_computation.71 | convolution fusion | flops 1613234176 | bytes 6821888 | tf_op jit(solution)/shard_map/dot_general | solution.py:253
  212.0 2.5 collective-permute-start.15
  214.5 6.2 %collective-permute-start.16 = (bf16[2,128,512]{2,1,0:T(8,128)(2,1)S(1)}, bf16[2,128,512]{2,1,0:T(8,128)(2,1)S(1)}, u32[]{:S(2)}, u32[]{:S(2)}) collective-permute-start(bf16[2,128,512]{2,1,0:T(8,128)(2,1)S(1)} %get-tuple-element.73), channel_id=1, source_target_pairs={{0,2},{1,3},{2,0},{3,1},{4,6},{5,7},{6,4},{7,5},{8,10},{9,11},{10,... | collective-permute-start | bytes 786440 | tf_op jit(solution)/shard_map/ppermute | solution.py:65
  223.1 15.9 %collective-permute-done.16 = bf16[2,128,512]{2,1,0:T(8,128)(2,1)S(1)} collective-permute-done((bf16[2,128,512]{2,1,0:T(8,128)(2,1)S(1)}, bf16[2,128,512]{2,1,0:T(8,128)(2,1)S(1)}, u32[]{:S(2)}, u32[]{:S(2)}) %collective-permute-start.16) | collective-permute-done | bytes 262176 | tf_op jit(solution)/shard_map/ppermute | solution.py:65
  239.1 2.7 collective-permute-start.23
  245.5 16.1 %collective-permute-done.22 = bf16[2,128,512]{2,1,0:T(8,128)(2,1)S(1)} collective-permute-done((bf16[2,128,512]{2,1,0:T(8,128)(2,1)S(1)}, bf16[2,128,512]{2,1,0:T(8,128)(2,1)S(1)}, u32[]{:S(2)}, u32[]{:S(2)}) %collective-permute-start.22) | collective-permute-done | bytes 262176 | tf_op jit(solution)/shard_map/ppermute | solution.py:65
  264.4 5.4 %collective-permute-done.33 = bf16[1,1,1,2,2,64,512]{6,5,4,3,2,1,0:T(8,128)(2,1)S(1)} collective-permute-done((bf16[1,1,1,2,2,64,512]{6,5,4,3,2,1,0:T(8,128)(2,1)S(1)}, bf16[1,1,1,2,2,64,512]{6,5,4,3,2,1,0:T(8,128)(2,1)S(1)}, u32[]{:S(2)}, u32[]{:S(2)}) %collective-permute-start.33) | collective-permute-done | bytes 262176 | tf_op jit(solution)/shard_map/ppermute | solution.py:65
  270.0 2.9 collective-permute-start.34
  278.8 2.6 collective-permute-done.35
  287.8 8.1 %collective-permute-done.25 = bf16[1,1,1,2,2,16,3200]{6,5,4,3,2,1,0:T(8,128)(2,1)S(1)} collective-permute-done((bf16[1,1,1,2,2,16,3200]{6,5,4,3,2,1,0:T(8,128)(2,1)S(1)}, bf16[1,1,1,2,2,16,3200]{6,5,4,3,2,1,0:T(8,128)(2,1)S(1)}, u32[]{:S(2)}, u32[]{:S(2)}) %collective-permute-start.25) | collective-permute-done | bytes 409632 | tf_op jit(solution)/shard_map/ppermute | solution.py:65
  296.0 4.4 %collective-permute-done.27 = bf16[1,1,1,2,2,16,3200]{6,5,4,3,2,1,0:T(8,128)(2,1)S(1)} collective-permute-done((bf16[1,1,1,2,2,16,3200]{6,5,4,3,2,1,0:T(8,128)(2,1)S(1)}, bf16[1,1,1,2,2,16,3200]{6,5,4,3,2,1,0:T(8,128)(2,1)S(1)}, u32[]{:S(2)}, u32[]{:S(2)}) %collective-permute-start.27) | collective-permute-done | bytes 409632 | tf_op jit(solution)/shard_map/ppermute | solution.py:65
  302.4 4.7 %collective-permute-done.28 = bf16[1,1,1,2,1,16,3200]{6,5,4,3,2,1,0:T(8,128)(2,1)S(1)} collective-permute-done((bf16[1,1,1,2,1,16,3200]{6,5,4,3,2,1,0:T(8,128)(2,1)S(1)}, bf16[1,1,1,2,1,16,3200]{6,5,4,3,2,1,0:T(8,128)(2,1)S(1)}, u32[]{:S(2)}, u32[]{:S(2)}) %collective-permute-start.28) | collective-permute-done | bytes 204832 | tf_op jit(solution)/shard_map/ppermute | solution.py:65
  309.3 4.6 %collective-permute-done.29 = bf16[1,1,1,1,1,16,3200]{6,5,4,3,2,1,0:T(8,128)(2,1)S(1)} collective-permute-done((bf16[1,1,1,1,1,16,3200]{6,5,4,3,2,1,0:T(8,128)(2,1)S(1)}, bf16[1,1,1,1,1,16,3200]{6,5,4,3,2,1,0:T(8,128)(2,1)S(1)}, u32[]{:S(2)}, u32[]{:S(2)}) %collective-permute-start.29) | collective-permute-done | bytes 102432 | tf_op jit(solution)/shard_map/ppermute | solution.py:65
  (274 shorter events, 77.7 us)
Async XLA Ops:
  2.5 16.3 %collective-permute-start.9 = (bf16[1,1,1,1,1,64,512]{6,5,4,3,2,1,0:T(8,128)(2,1)S(1)}, bf16[1,1,1,1,1,64,512]{6,5,4,3,2,1,0:T(8,128)(2,1)S(1)}, u32[]{:S(2)}, u32[]{:S(2)}) collective-permute-start(bf16[1,1,1,1,1,64,512]{6,5,4,3,2,1,0:T(8,128)(2,1)S(1)} %bitcast.170), channel_id=1, source_target_pairs={{0,2},{1,3},{2,0},{3,1},{4,6},{5,7},{6,4},{7,5},{8,10},{9,11},{10,... | collective-permute-start | bytes 196616 | tf_op jit(solution)/shard_map/ppermute | solution.py:65
  8.4 11.4 %collective-permute-start.3 = (bf16[1,1,1,1,1,16,3200]{6,5,4,3,2,1,0:T(8,128)(2,1)S(1)}, bf16[1,1,1,1,1,16,3200]{6,5,4,3,2,1,0:T(8,128)(2,1)S(1)}, u32[]{:S(2)}, u32[]{:S(2)}) collective-permute-start(bf16[1,1,1,1,1,16,3200]{6,5,4,3,2,1,0:T(8,128)(2,1)S(1)} %get-tuple-element.109), channel_id=1, source_target_pairs={{0,2},{1,3},{2,0},{3,1},{4,6},{5,7},{6,4},{7,5},{8,10},{9,11},{10,... | collective-permute-start | bytes 307208 | tf_op jit(solution)/shard_map/ppermute | solution.py:65
  10.6 26.3 %collective-permute-start = (bf16[2,128,512]{2,1,0:T(8,128)(2,1)}, bf16[2,128,512]{2,1,0:T(8,128)(2,1)}, u32[]{:S(2)}, u32[]{:S(2)}) collective-permute-start(bf16[2,128,512]{2,1,0:T(8,128)(2,1)} %get-tuple-element.76), channel_id=1, source_target_pairs={{0,1},{1,0},{2,3},{3,2},{4,5},{5,4},{6,7},{7,6},{8,9},{9,8},{10,11... | collective-permute-start | bytes 786440 | tf_op jit(solution)/shard_map/ppermute | solution.py:65
  12.5 25.9 %collective-permute-start.1 = (bf16[2,128,512]{2,1,0:T(8,128)(2,1)}, bf16[2,128,512]{2,1,0:T(8,128)(2,1)}, u32[]{:S(2)}, u32[]{:S(2)}) collective-permute-start(bf16[2,128,512]{2,1,0:T(8,128)(2,1)} %get-tuple-element.78), channel_id=1, source_target_pairs={{0,2},{1,3},{2,0},{3,1},{4,6},{5,7},{6,4},{7,5},{8,10},{9,11},{10,... | collective-permute-start | bytes 786440 | tf_op jit(solution)/shard_map/ppermute | solution.py:65
  15.0 23.6 %collective-permute-start.2 = (bf16[2,128,512]{2,1,0:T(8,128)(2,1)S(1)}, bf16[2,128,512]{2,1,0:T(8,128)(2,1)}, u32[]{:S(2)}, u32[]{:S(2)}) collective-permute-start(bf16[2,128,512]{2,1,0:T(8,128)(2,1)S(1)} %get-tuple-element.77), channel_id=1, source_target_pairs={{0,3},{1,2},{2,1},{3,0},{4,7},{5,6},{6,5},{7,4},{8,11},{9,10},{10,... | collective-permute-start | bytes 786440 | tf_op jit(solution)/shard_map/ppermute | solution.py:65
  18.9 16.0 %collective-permute-start.10 = (bf16[1,1,1,2,1,64,512]{6,5,3,4,2,1,0:T(8,128)(2,1)S(1)}, bf16[1,1,1,2,1,64,512]{6,5,3,4,2,1,0:T(8,128)(2,1)S(1)}, u32[]{:S(2)}, u32[]{:S(2)}) collective-permute-start(bf16[1,1,1,2,1,64,512]{6,5,3,4,2,1,0:T(8,128)(2,1)S(1)} %fusion.58), channel_id=1, source_target_pairs={{0,1},{1,0},{2,3},{3,2},{4,5},{5,4},{6,7},{7,6},{8,9},{9,8},{10,11... | collective-permute-start | bytes 393224 | tf_op jit(solution)/shard_map/ppermute | solution.py:65
  19.9 20.1 %collective-permute-start.4 = (bf16[1,1,1,2,1,16,3200]{6,5,3,4,2,1,0:T(8,128)(2,1)S(1)}, bf16[1,1,1,2,1,16,3200]{6,5,3,4,2,1,0:T(8,128)(2,1)S(1)}, u32[]{:S(2)}, u32[]{:S(2)}) collective-permute-start(bf16[1,1,1,2,1,16,3200]{6,5,3,4,2,1,0:T(8,128)(2,1)S(1)} %fusion.55), channel_id=1, source_target_pairs={{0,1},{1,0},{2,3},{3,2},{4,5},{5,4},{6,7},{7,6},{8,9},{9,8},{10,11... | collective-permute-start | bytes 614408 | tf_op jit(solution)/shard_map/ppermute | solution.py:65
  35.0 19.5 %collective-permute-start.12 = (bf16[1,1,1,2,2,64,512]{6,5,4,3,2,1,0:T(8,128)(2,1)S(1)}, bf16[1,1,1,2,2,64,512]{6,5,4,3,2,1,0:T(8,128)(2,1)S(1)}, u32[]{:S(2)}, u32[]{:S(2)}) collective-permute-start(bf16[1,1,1,2,2,64,512]{6,5,4,3,2,1,0:T(8,128)(2,1)S(1)} %copy_select_fusion.1), channel_id=1, source_target_pairs={{0,16},{4,20},{8,24},{12,28},{16,0},{20,4},{24,8},{28,12},{1,17},{... | collective-permute-start | bytes 786440 | tf_op jit(solution)/shard_map/ppermute | solution.py:65
  36.9 18.9 %collective-permute-start.13 = (bf16[1,1,1,2,2,64,512]{6,5,4,3,2,1,0:T(8,128)(2,1)S(1)}, bf16[1,1,1,2,2,64,512]{6,5,4,3,2,1,0:T(8,128)(2,1)S(1)}, u32[]{:S(2)}, u32[]{:S(2)}) collective-permute-start(bf16[1,1,1,2,2,64,512]{6,5,4,3,2,1,0:T(8,128)(2,1)S(1)} %copy_select_fusion.1), channel_id=1, source_target_pairs={{0,24},{4,28},{8,16},{12,20},{16,8},{20,12},{24,0},{28,4},{1,25},{... | collective-permute-start | bytes 786440 | tf_op jit(solution)/shard_map/ppermute | solution.py:65
  38.4 17.5 %collective-permute-start.11 = (bf16[1,1,1,2,2,64,512]{6,5,4,3,2,1,0:T(8,128)(2,1)S(1)}, bf16[1,1,1,2,2,64,512]{6,5,4,3,2,1,0:T(8,128)(2,1)S(1)}, u32[]{:S(2)}, u32[]{:S(2)}) collective-permute-start(bf16[1,1,1,2,2,64,512]{6,5,4,3,2,1,0:T(8,128)(2,1)S(1)} %copy_select_fusion.1), channel_id=1, source_target_pairs={{0,8},{4,12},{8,0},{12,4},{16,24},{20,28},{24,16},{28,20},{1,9},{5... | collective-permute-start | bytes 786440 | tf_op jit(solution)/shard_map/ppermute | solution.py:65
  40.1 21.6 %collective-permute-start.6 = (bf16[1,1,1,2,2,16,3200]{6,5,4,3,2,1,0:T(8,128)(2,1)S(1)}, bf16[1,1,1,2,2,16,3200]{6,5,4,3,2,1,0:T(8,128)(2,1)S(1)}, u32[]{:S(2)}, u32[]{:S(2)}) collective-permute-start(bf16[1,1,1,2,2,16,3200]{6,5,4,3,2,1,0:T(8,128)(2,1)S(1)} %copy_select_fusion), channel_id=1, source_target_pairs={{0,16},{4,20},{8,24},{12,28},{16,0},{20,4},{24,8},{28,12},{1,17},{... | collective-permute-start | bytes 1228808 | tf_op jit(solution)/shard_map/ppermute | solution.py:65
  42.0 21.6 %collective-permute-start.7 = (bf16[1,1,1,2,2,16,3200]{6,5,4,3,2,1,0:T(8,128)(2,1)S(1)}, bf16[1,1,1,2,2,16,3200]{6,5,4,3,2,1,0:T(8,128)(2,1)S(1)}, u32[]{:S(2)}, u32[]{:S(2)}) collective-permute-start(bf16[1,1,1,2,2,16,3200]{6,5,4,3,2,1,0:T(8,128)(2,1)S(1)} %copy_select_fusion), channel_id=1, source_target_pairs={{0,24},{4,28},{8,16},{12,20},{16,8},{20,12},{24,0},{28,4},{1,25},{... | collective-permute-start | bytes 1228808 | tf_op jit(solution)/shard_map/ppermute | solution.py:65
  54.4 18.3 %collective-permute-start.18 = (bf16[2,128,512]{2,1,0:T(8,128)(2,1)S(1)}, bf16[2,128,512]{2,1,0:T(8,128)(2,1)S(1)}, u32[]{:S(2)}, u32[]{:S(2)}) collective-permute-start(bf16[2,128,512]{2,1,0:T(8,128)(2,1)S(1)} %get-tuple-element.64), channel_id=1, source_target_pairs={{0,1},{1,0},{2,3},{3,2},{4,5},{5,4},{6,7},{7,6},{8,9},{9,8},{10,11... | collective-permute-start | bytes 786440 | tf_op jit(solution)/shard_map/ppermute | solution.py:65
  55.8 17.0 %collective-permute-start.19 = (bf16[2,128,512]{2,1,0:T(8,128)(2,1)S(1)}, bf16[2,128,512]{2,1,0:T(8,128)(2,1)S(1)}, u32[]{:S(2)}, u32[]{:S(2)}) collective-permute-start(bf16[2,128,512]{2,1,0:T(8,128)(2,1)S(1)} %get-tuple-element.66), channel_id=1, source_target_pairs={{0,2},{1,3},{2,0},{3,1},{4,6},{5,7},{6,4},{7,5},{8,10},{9,11},{10,... | collective-permute-start | bytes 786440 | tf_op jit(solution)/shard_map/ppermute | solution.py:65
  55.9 16.9 %collective-permute-start.20 = (bf16[2,128,512]{2,1,0:T(8,128)(2,1)S(1)}, bf16[2,128,512]{2,1,0:T(8,128)(2,1)S(1)}, u32[]{:S(2)}, u32[]{:S(2)}) collective-permute-start(bf16[2,128,512]{2,1,0:T(8,128)(2,1)S(1)} %get-tuple-element.65), channel_id=1, source_target_pairs={{0,3},{1,2},{2,1},{3,0},{4,7},{5,6},{6,5},{7,4},{8,11},{9,10},{10,... | collective-permute-start | bytes 786440 | tf_op jit(solution)/shard_map/ppermute | solution.py:65
  61.8 9.9 %collective-permute-start.5 = (bf16[1,1,1,2,2,16,3200]{6,5,4,3,2,1,0:T(8,128)(2,1)S(1)}, bf16[1,1,1,2,2,16,3200]{6,5,4,3,2,1,0:T(8,128)(2,1)S(1)}, u32[]{:S(2)}, u32[]{:S(2)}) collective-permute-start(bf16[1,1,1,2,2,16,3200]{6,5,4,3,2,1,0:T(8,128)(2,1)S(1)} %copy_select_fusion), channel_id=1, source_target_pairs={{0,8},{4,12},{8,0},{12,4},{16,24},{20,28},{24,16},{28,20},{1,9},{5... | collective-permute-start | bytes 1228808 | tf_op jit(solution)/shard_map/ppermute | solution.py:65
  63.5 11.4 %collective-permute-start.14 = (bf16[2,2,1,2,2,64,512]{6,5,4,3,2,1,0:T(8,128)(2,1)S(1)}, bf16[2,2,1,2,2,64,512]{6,5,4,3,2,1,0:T(8,128)(2,1)S(1)}, u32[]{:S(2)}, u32[]{:S(2)}) collective-permute-start(bf16[2,2,1,2,2,64,512]{6,5,4,3,2,1,0:T(8,128)(2,1)S(1)} %maximum_select_fusion.3), channel_id=1, source_target_pairs={{0,4},{4,0},{8,12},{12,8},{16,20},{20,16},{24,28},{28,24},{1,5},{5... | collective-permute-start | bytes 3145736 | tf_op jit(solution)/shard_map/ppermute | solution.py:65
  199.5 42.4 %collective-permute-start.30 = (bf16[2,2,1,2,2,64,512]{6,5,4,3,2,1,0:T(8,128)(2,1)S(1)}, bf16[2,2,1,2,2,64,512]{6,5,4,3,2,1,0:T(8,128)(2,1)S(1)}, u32[]{:S(2)}, u32[]{:S(2)}) collective-permute-start(bf16[2,2,1,2,2,64,512]{6,5,4,3,2,1,0:T(8,128)(2,1)S(1)} %constant_dynamic-slice_fusion.5), channel_id=1, source_target_pairs={{0,4},{4,0},{8,12},{12,8},{16,20},{20,16},{24,28},{28,24},{1,5},{5... | collective-permute-start | bytes 3145736 | tf_op jit(solution)/shard_map/ppermute | solution.py:65
  207.5 73.9 %collective-permute-start.24 = (bf16[2,2,1,2,2,16,3200]{6,5,4,3,2,1,0:T(8,128)(2,1)}, bf16[2,2,1,2,2,16,3200]{6,5,4,3,2,1,0:T(8,128)(2,1)}, u32[]{:S(2)}, u32[]{:S(2)}) collective-permute-start(bf16[2,2,1,2,2,16,3200]{6,5,4,3,2,1,0:T(8,128)(2,1)} %constant_dynamic-slice_fusion.15), channel_id=1, source_target_pairs={{0,4},{4,0},{8,12},{12,8},{16,20},{20,16},{24,28},{28,24},{1,5},{5... | collective-permute-start | bytes 4915208 | tf_op jit(solution)/shard_map/ppermute | solution.py:65
  212.0 10.0 %collective-permute-start.15 = (bf16[2,128,512]{2,1,0:T(8,128)(2,1)S(1)}, bf16[2,128,512]{2,1,0:T(8,128)(2,1)S(1)}, u32[]{:S(2)}, u32[]{:S(2)}) collective-permute-start(bf16[2,128,512]{2,1,0:T(8,128)(2,1)S(1)} %get-tuple-element.74), channel_id=1, source_target_pairs={{0,1},{1,0},{2,3},{3,2},{4,5},{5,4},{6,7},{7,6},{8,9},{9,8},{10,11... | collective-permute-start | bytes 786440 | tf_op jit(solution)/shard_map/ppermute | solution.py:65
  214.5 24.6 %collective-permute-start.16 = (bf16[2,128,512]{2,1,0:T(8,128)(2,1)S(1)}, bf16[2,128,512]{2,1,0:T(8,128)(2,1)S(1)}, u32[]{:S(2)}, u32[]{:S(2)}) collective-permute-start(bf16[2,128,512]{2,1,0:T(8,128)(2,1)S(1)} %get-tuple-element.73), channel_id=1, source_target_pairs={{0,2},{1,3},{2,0},{3,1},{4,6},{5,7},{6,4},{7,5},{8,10},{9,11},{10,... | collective-permute-start | bytes 786440 | tf_op jit(solution)/shard_map/ppermute | solution.py:65
  220.7 18.4 %collective-permute-start.17 = (bf16[2,128,512]{2,1,0:T(8,128)(2,1)S(1)}, bf16[2,128,512]{2,1,0:T(8,128)(2,1)S(1)}, u32[]{:S(2)}, u32[]{:S(2)}) collective-permute-start(bf16[2,128,512]{2,1,0:T(8,128)(2,1)S(1)} %get-tuple-element.72), channel_id=1, source_target_pairs={{0,3},{1,2},{2,1},{3,0},{4,7},{5,6},{6,5},{7,4},{8,11},{9,10},{10,... | collective-permute-start | bytes 786440 | tf_op jit(solution)/shard_map/ppermute | solution.py:65
  222.0 21.9 %collective-permute-start.21 = (bf16[2,128,512]{2,1,0:T(8,128)(2,1)S(1)}, bf16[2,128,512]{2,1,0:T(8,128)(2,1)S(1)}, u32[]{:S(2)}, u32[]{:S(2)}) collective-permute-start(bf16[2,128,512]{2,1,0:T(8,128)(2,1)S(1)} %get-tuple-element.62), channel_id=1, source_target_pairs={{0,1},{1,0},{2,3},{3,2},{4,5},{5,4},{6,7},{7,6},{8,9},{9,8},{10,11... | collective-permute-start | bytes 786440 | tf_op jit(solution)/shard_map/ppermute | solution.py:65
  239.1 22.5 %collective-permute-start.22 = (bf16[2,128,512]{2,1,0:T(8,128)(2,1)S(1)}, bf16[2,128,512]{2,1,0:T(8,128)(2,1)S(1)}, u32[]{:S(2)}, u32[]{:S(2)}) collective-permute-start(bf16[2,128,512]{2,1,0:T(8,128)(2,1)S(1)} %get-tuple-element.61), channel_id=1, source_target_pairs={{0,2},{1,3},{2,0},{3,1},{4,6},{5,7},{6,4},{7,5},{8,10},{9,11},{10,... | collective-permute-start | bytes 786440 | tf_op jit(solution)/shard_map/ppermute | solution.py:65
  239.1 24.9 %collective-permute-start.23 = (bf16[2,128,512]{2,1,0:T(8,128)(2,1)S(1)}, bf16[2,128,512]{2,1,0:T(8,128)(2,1)S(1)}, u32[]{:S(2)}, u32[]{:S(2)}) collective-permute-start(bf16[2,128,512]{2,1,0:T(8,128)(2,1)S(1)} %get-tuple-element.60), channel_id=1, source_target_pairs={{0,3},{1,2},{2,1},{3,0},{4,7},{5,6},{6,5},{7,4},{8,11},{9,10},{10,... | collective-permute-start | bytes 786440 | tf_op jit(solution)/shard_map/ppermute | solution.py:65
  242.3 22.0 %collective-permute-start.31 = (bf16[1,1,1,2,2,64,512]{6,5,4,3,2,1,0:T(8,128)(2,1)S(1)}, bf16[1,1,1,2,2,64,512]{6,5,4,3,2,1,0:T(8,128)(2,1)S(1)}, u32[]{:S(2)}, u32[]{:S(2)}) collective-permute-start(bf16[1,1,1,2,2,64,512]{6,5,4,3,2,1,0:T(8,128)(2,1)S(1)} %get-tuple-element.52), channel_id=1, source_target_pairs={{0,16},{4,20},{8,24},{12,28},{16,0},{20,4},{24,8},{28,12},{1,17},{... | collective-permute-start | bytes 786440 | tf_op jit(solution)/shard_map/ppermute | solution.py:65
  243.9 20.4 %collective-permute-start.32 = (bf16[1,1,1,2,2,64,512]{6,5,4,3,2,1,0:T(8,128)(2,1)S(1)}, bf16[1,1,1,2,2,64,512]{6,5,4,3,2,1,0:T(8,128)(2,1)S(1)}, u32[]{:S(2)}, u32[]{:S(2)}) collective-permute-start(bf16[1,1,1,2,2,64,512]{6,5,4,3,2,1,0:T(8,128)(2,1)S(1)} %get-tuple-element.54), channel_id=1, source_target_pairs={{0,8},{4,12},{8,0},{12,4},{16,24},{20,28},{24,16},{28,20},{1,9},{5... | collective-permute-start | bytes 786440 | tf_op jit(solution)/shard_map/ppermute | solution.py:65
  261.6 8.2 %collective-permute-start.33 = (bf16[1,1,1,2,2,64,512]{6,5,4,3,2,1,0:T(8,128)(2,1)S(1)}, bf16[1,1,1,2,2,64,512]{6,5,4,3,2,1,0:T(8,128)(2,1)S(1)}, u32[]{:S(2)}, u32[]{:S(2)}) collective-permute-start(bf16[1,1,1,2,2,64,512]{6,5,4,3,2,1,0:T(8,128)(2,1)S(1)} %get-tuple-element.53), channel_id=1, source_target_pairs={{0,24},{4,28},{8,16},{12,20},{16,8},{20,12},{24,0},{28,4},{1,25},{... | collective-permute-start | bytes 786440 | tf_op jit(solution)/shard_map/ppermute | solution.py:65
  283.5 12.4 %collective-permute-start.25 = (bf16[1,1,1,2,2,16,3200]{6,5,4,3,2,1,0:T(8,128)(2,1)S(1)}, bf16[1,1,1,2,2,16,3200]{6,5,4,3,2,1,0:T(8,128)(2,1)S(1)}, u32[]{:S(2)}, u32[]{:S(2)}) collective-permute-start(bf16[1,1,1,2,2,16,3200]{6,5,4,3,2,1,0:T(8,128)(2,1)S(1)} %get-tuple-element.47), channel_id=1, source_target_pairs={{0,16},{4,20},{8,24},{12,28},{16,0},{20,4},{24,8},{28,12},{1,17},{... | collective-permute-start | bytes 1228808 | tf_op jit(solution)/shard_map/ppermute | solution.py:65
  285.1 11.0 %collective-permute-start.26 = (bf16[1,1,1,2,2,16,3200]{6,5,4,3,2,1,0:T(8,128)(2,1)S(1)}, bf16[1,1,1,2,2,16,3200]{6,5,4,3,2,1,0:T(8,128)(2,1)S(1)}, u32[]{:S(2)}, u32[]{:S(2)}) collective-permute-start(bf16[1,1,1,2,2,16,3200]{6,5,4,3,2,1,0:T(8,128)(2,1)S(1)} %get-tuple-element.49), channel_id=1, source_target_pairs={{0,8},{4,12},{8,0},{12,4},{16,24},{20,28},{24,16},{28,20},{1,9},{5... | collective-permute-start | bytes 1228808 | tf_op jit(solution)/shard_map/ppermute | solution.py:65
  286.5 13.8 %collective-permute-start.27 = (bf16[1,1,1,2,2,16,3200]{6,5,4,3,2,1,0:T(8,128)(2,1)S(1)}, bf16[1,1,1,2,2,16,3200]{6,5,4,3,2,1,0:T(8,128)(2,1)S(1)}, u32[]{:S(2)}, u32[]{:S(2)}) collective-permute-start(bf16[1,1,1,2,2,16,3200]{6,5,4,3,2,1,0:T(8,128)(2,1)S(1)} %get-tuple-element.48), channel_id=1, source_target_pairs={{0,24},{4,28},{8,16},{12,20},{16,8},{20,12},{24,0},{28,4},{1,25},{... | collective-permute-start | bytes 1228808 | tf_op jit(solution)/shard_map/ppermute | solution.py:65
  307.2 6.7 %collective-permute-start.29 = (bf16[1,1,1,1,1,16,3200]{6,5,4,3,2,1,0:T(8,128)(2,1)S(1)}, bf16[1,1,1,1,1,16,3200]{6,5,4,3,2,1,0:T(8,128)(2,1)S(1)}, u32[]{:S(2)}, u32[]{:S(2)}) collective-permute-start(bf16[1,1,1,1,1,16,3200]{6,5,4,3,2,1,0:T(8,128)(2,1)S(1)} %constant_dynamic-slice_fusion.10), channel_id=1, source_target_pairs={{0,2},{1,3},{2,0},{3,1},{4,6},{5,7},{6,4},{7,5},{8,10},{9,11},{10,... | collective-permute-start | bytes 307208 | tf_op jit(solution)/shard_map/ppermute | solution.py:65
  (49 other events, 639.7 us)

commit v2 on v1

--- a/solution.py
+++ b/solution.py
@@ -1,6 +1,11 @@
+import functools
+import math
+
 import jax
 import jax.numpy as jnp
 from jax import lax
+from jax.experimental import pallas as pl
+from jax.experimental.pallas import tpu as pltpu
 from jax.sharding import PartitionSpec as P
 
 D = 512
@@ -46,10 +51,6 @@
     first_mean = jnp.mean(grad_hat, -1, keepdims=True)
     cross_mean = jnp.mean(grad_hat * normed, -1, keepdims=True)
     return (grad_hat - first_mean - normed * cross_mean) * inverse
-
-
-def gelu_exact(values):
-    return jax.nn.gelu(values, approximate=False)
 
 
 def adamw(master, first, second, gradient, rate, decay):
@@ -145,6 +146,244 @@
     for bit in range(zbits):
         held = halve(held, "pos", pos_size, z, (bit,), 0)
     return held.reshape(rows, cols)
+
+
+CHUNK = 512
+TILE = 256
+
+tail_slope = 0.39 / math.sqrt(2.0)
+tail_series = (
+    0.23532609033994684,
+    0.09138275083966492,
+    0.6495739793206253,
+    -0.6354188599562557,
+    0.8866760936996321,
+    -0.22754005589281026,
+)
+exp_scale = -0.5 / math.log(2.0)
+density = 1.0 / math.sqrt(2.0 * math.pi)
+
+
+def gelu_and_slope(v):
+    size = jnp.abs(v)
+    t = 1.0 / (1.0 + tail_slope * size)
+    bell = jnp.exp2(exp_scale * (v * v))
+    series = 0.5 * tail_series[-1]
+    for c in reversed(tail_series[:-1]):
+        series = series * t + 0.5 * c
+    tail = series * t * bell
+    phi = jnp.where(v > 0, 1.0 - tail, tail)
+    return v * phi, phi + (density * v) * bell
+
+
+def dot(a, b, ca=1, cb=0):
+    return lax.dot_general(a, b, (((ca,), (cb,)), ((), ())), preferred_element_type=wide)
+
+
+def project_kernel(
+    x_ref, w_ref, gain_in, bias_in, bias_hidden, gain_gate, bias_gate,
+    scaled_ref, left_ref, slope_ref, normed_ref, inverse_ref, gate_ref, half_ref,
+):
+    normed, _ = norm_parts(x_ref[...].astype(wide))
+    scaled = (normed * gain_in[...] + bias_in[...]).astype(low_type)
+    scaled_ref[...] = scaled
+
+    def part(step, base, out):
+        at = pl.multiple_of(step * CHUNK, CHUNK)
+        cols = pl.ds(pl.multiple_of(base + at, CHUNK), CHUNK)
+        value, slope = gelu_and_slope(dot(scaled, w_ref[:, cols]) + bias_hidden[:, cols])
+        slope_ref[:, cols] = slope.astype(low_type)
+        out[:, pl.ds(at, CHUNK)] = value.astype(out.dtype)
+
+    def body(step, carry):
+        part(step, 0, left_ref)
+        part(step, GATE, half_ref)
+        return carry
+
+    lax.fori_loop(0, GATE // CHUNK, body, 0)
+    normed_gate, inverse = norm_parts(half_ref[...])
+    inverse_ref[...] = inverse
+    normed_ref[...] = normed_gate.astype(low_type)
+    gate_ref[...] = (normed_gate * gain_gate[...] + bias_gate[...]).astype(low_type)
+
+
+def mix_kernel(
+    x_ref, own_ref, key_ref, keep_ref, ws_ref, wo_ref, bias_s, bias_o, left_ref, gate_ref,
+    mixed_ref, spatial_ref, gated_ref,
+):
+    same = own_ref[0] == key_ref[0]
+    mixing = jnp.where(same, ws_ref[...].astype(wide), 0.0).astype(low_type)
+    branch = jnp.zeros(x_ref.shape[1:], wide)
+    for c in range(GATE // CHUNK):
+        cols = slice(c * CHUNK, (c + 1) * CHUNK)
+        spatial = dot(mixing, gate_ref[0, :, cols]) + bias_s[...]
+        gated = (left_ref[0, :, cols].astype(wide) * spatial).astype(low_type)
+        spatial_ref[0, :, cols] = spatial.astype(low_type)
+        gated_ref[0, :, cols] = gated
+        branch = branch + dot(gated, wo_ref[cols, :])
+    mixed = x_ref[0].astype(wide) + keep_ref[0] * (branch + bias_o[...])
+    mixed_ref[0] = mixed.astype(low_type)
+
+
+def back_kernel(
+    cot_ref, own_ref, key_ref, own_line, key_line, keep_ref, ws_ref, wst_ref, wo_ref, gain_gate,
+    left_ref, gate_ref, normed_ref, inverse_ref, spatial_ref, gated_ref, slope_ref,
+    pre_ref, dwo_ref, dws_ref, dbo_ref, dbs_ref, dgain_ref, dbias_ref, dbh_ref,
+    dwo_acc, dws_acc, gate_acc,
+):
+    row = pl.program_id(0)
+
+    @pl.when(row == 0)
+    def _():
+        for ref in (dwo_acc, dws_acc, dbo_ref, dbs_ref, dgain_ref, dbias_ref, dbh_ref):
+            ref[...] = jnp.zeros_like(ref)
+
+    same = own_ref[0] == key_line[0]
+    mixing_back = jnp.where(
+        own_line[0] == key_ref[0], wst_ref[...].astype(wide), 0.0
+    ).astype(low_type)
+    grad_branch = cot_ref[0].astype(wide) * keep_ref[0]
+    dbo_ref[...] += jnp.sum(grad_branch, 0, keepdims=True)
+    branch_low = grad_branch.astype(low_type)
+    length = branch_low.shape[0]
+    products = jnp.zeros((length, length), wide)
+    first = jnp.zeros((length, 1), wide)
+    cross = jnp.zeros((length, 1), wide)
+    for c in range(GATE // CHUNK):
+        cols = slice(c * CHUNK, (c + 1) * CHUNK)
+        grad_gated = dot(branch_low, wo_ref[cols, :], 1, 1)
+        dwo_acc[cols, :] += dot(gated_ref[0, :, cols], branch_low, 0, 0)
+        grad_spatial = grad_gated * left_ref[0, :, cols].astype(wide)
+        spatial_low = grad_spatial.astype(low_type)
+        dbs_ref[...] += jnp.sum(grad_spatial, 1, keepdims=True)
+        pre = (grad_gated * spatial_ref[0, :, cols].astype(wide)) * slope_ref[0, :, cols].astype(wide)
+        pre_ref[0, :, cols] = pre.astype(low_type)
+        dbh_ref[:, cols] += jnp.sum(pre, 0, keepdims=True)
+        products = products + dot(spatial_low, gate_ref[0, :, cols], 1, 1)
+        grad_gate = dot(mixing_back, spatial_low)
+        normed = normed_ref[0, :, cols].astype(wide)
+        dgain_ref[:, cols] += jnp.sum(grad_gate * normed, 0, keepdims=True)
+        dbias_ref[:, cols] += jnp.sum(grad_gate, 0, keepdims=True)
+        grad_hat = grad_gate * gain_gate[:, cols]
+        gate_acc[:, cols] = grad_hat
+        first = first + jnp.sum(grad_hat, 1, keepdims=True)
+        cross = cross + jnp.sum(grad_hat * normed, 1, keepdims=True)
+    dws_acc[...] += jnp.where(same, products, 0.0)
+    first = first * (1.0 / GATE)
+    cross = cross * (1.0 / GATE)
+    inverse = inverse_ref[0]
+    for c in range(GATE // CHUNK):
+        cols = slice(c * CHUNK, (c + 1) * CHUNK)
+        rest = slice(GATE + c * CHUNK, GATE + (c + 1) * CHUNK)
+        normed = normed_ref[0, :, cols].astype(wide)
+        grad_right = (gate_acc[:, cols] - first - normed * cross) * inverse
+        pre = grad_right * slope_ref[0, :, rest].astype(wide)
+        pre_ref[0, :, rest] = pre.astype(low_type)
+        dbh_ref[:, rest] += jnp.sum(pre, 0, keepdims=True)
+
+    @pl.when(row == pl.num_programs(0) - 1)
+    def _():
+        dwo_ref[...] = dwo_acc[...].astype(low_type)
+        dws_ref[...] = dws_acc[...].astype(low_type)
+
+
+def whole(*shape):
+    return pl.BlockSpec(shape, lambda r: (0,) * len(shape))
+
+
+def per_row(*shape):
+    return pl.BlockSpec((1,) + shape, lambda r: (r,) + (0,) * len(shape))
+
+
+def shaped(dtype, *shape):
+    return jax.ShapeDtypeStruct(shape, dtype)
+
+
+def project(x, weight_in, gain_in, bias_in, bias_hidden, gain_gate, bias_gate):
+    total = x.shape[0]
+    tile = min(TILE, total)
+    block = lambda n: pl.BlockSpec((tile, n), lambda i: (i, 0))
+    return pl.pallas_call(
+        project_kernel,
+        grid=(total // tile,),
+        in_specs=[block(D), whole(D, HID), whole(1, D), whole(1, D), whole(1, HID), whole(1, GATE), whole(1, GATE)],
+        out_specs=[block(D), block(GATE), block(HID), block(GATE), block(1), block(GATE)],
+        out_shape=[
+            shaped(low_type, total, D),
+            shaped(low_type, total, GATE),
+            shaped(low_type, total, HID),
+            shaped(low_type, total, GATE),
+            shaped(wide, total, 1),
+            shaped(low_type, total, GATE),
+        ],
+        scratch_shapes=[pltpu.VMEM((tile, GATE), wide)],
+        cost_estimate=pl.CostEstimate(
+            flops=2 * total * D * HID + 40 * total * HID, transcendentals=2 * total * HID, bytes_accessed=20 << 20
+        ),
+        name="project",
+    )(x, weight_in, gain_in, bias_in, bias_hidden, gain_gate, bias_gate)
+
+
+def mix(x, own, key, keep, ws, wo, bias_s, bias_o, left, gate):
+    rows, length, _ = x.shape
+    return pl.pallas_call(
+        mix_kernel,
+        grid=(rows,),
+        in_specs=[
+            per_row(length, D), per_row(length, 1), per_row(1, length), per_row(length, 1),
+            whole(length, length), whole(GATE, D), whole(length, 1), whole(1, D),
+            per_row(length, GATE), per_row(length, GATE),
+        ],
+        out_specs=[per_row(length, D), per_row(length, GATE), per_row(length, GATE)],
+        out_shape=[
+            shaped(low_type, rows, length, D),
+            shaped(low_type, rows, length, GATE),
+            shaped(low_type, rows, length, GATE),
+        ],
+        cost_estimate=pl.CostEstimate(
+            flops=4 * rows * length * GATE * D, transcendentals=0, bytes_accessed=16 << 20
+        ),
+        name="mix",
+    )(x, own, key, keep, ws, wo, bias_s, bias_o, left, gate)
+
+
+def back(cot, own, key, keep, ws, wst, wo, gain_gate, left, gate, normed, inverse, spatial, gated, slope):
+    rows, length, _ = cot.shape
+    own_line = own.reshape(rows, 1, length)
+    key_col = key.reshape(rows, length, 1)
+    return pl.pallas_call(
+        back_kernel,
+        grid=(rows,),
+        in_specs=[
+            per_row(length, D), per_row(length, 1), per_row(length, 1), per_row(1, length), per_row(1, length),
+            per_row(length, 1), whole(length, length), whole(length, length), whole(GATE, D), whole(1, GATE),
+            per_row(length, GATE), per_row(length, GATE), per_row(length, GATE), per_row(length, 1),
+            per_row(length, GATE), per_row(length, GATE), per_row(length, HID),
+        ],
+        out_specs=[
+            per_row(length, HID), whole(GATE, D), whole(length, length), whole(1, D), whole(length, 1),
+            whole(1, GATE), whole(1, GATE), whole(1, HID),
+        ],
+        out_shape=[
+            shaped(low_type, rows, length, HID),
+            shaped(low_type, GATE, D),
+            shaped(low_type, length, length),
+            shaped(wide, 1, D),
+            shaped(wide, length, 1),
+            shaped(wide, 1, GATE),
+            shaped(wide, 1, GATE),
+            shaped(wide, 1, HID),
+        ],
+        scratch_shapes=[
+            pltpu.VMEM((GATE, D), wide),
+            pltpu.VMEM((length, length), wide),
+            pltpu.VMEM((length, GATE), wide),
+        ],
+        cost_estimate=pl.CostEstimate(
+            flops=8 * rows * length * GATE * D, transcendentals=0, bytes_accessed=30 << 20
+        ),
+        name="back",
+    )(cot, own, key_col, own_line, key, keep, ws, wst, wo, gain_gate, left, gate, normed, inverse, spatial, gated, slope)
 
 
 def local_fn(sizes):
@@ -230,45 +469,44 @@
         own_rows = lambda value: lax.dynamic_slice_in_dim(value, z * mine, mine, 0)
         segments = relative(own_rows(segment_ids), 1)
         padding = relative(own_rows(pad_mask), 1)
-        keeping = padding.astype(wide) * (1.0 - own_rows(skip_flags).astype(wide))[:, None]
-        keep_flat = keeping.reshape(-1, 1)
-        same_rows = (segments[:, :, None] == segments[:, None, :]) & (padding[:, None, :] == 1)
+        keep = padding.astype(wide) * (1.0 - own_rows(skip_flags).astype(wide))[:, None]
+        keep = keep[:, :, None]
+        own = segments[:, :, None]
+        key = jnp.where(padding == 1, segments, -1)[:, None, :]
         mixing_rows = relative(relative(weight_spatial, 0), 1)
-        bias_rows = relative(bias_spatial, 0)
-        mixing = jnp.where(same_rows, mixing_rows[None], jnp.zeros((), low_type))
-
-        inputs = inputs_low.astype(wide).reshape(-1, D)
-        normed_in, inverse_in = norm_parts(inputs)
-        scaled_in = (normed_in * gain_in + bias_in).astype(low_type)
-        hidden_pre = jnp.dot(scaled_in, weight_in, preferred_element_type=wide) + bias_hidden
-        hidden, gelu_back = jax.vjp(gelu_exact, hidden_pre)
-        left_half = hidden[:, :GATE]
-        normed_gate, inverse_gate = norm_parts(hidden[:, GATE:])
-        gate_low = (normed_gate * gain_gate + bias_gate).astype(low_type).reshape(mine, SEQ, GATE)
-        spatial = (
-            jnp.einsum("rij,rjc->ric", mixing, gate_low, preferred_element_type=wide)
-            + bias_rows[None, :, None]
-        ).reshape(-1, GATE)
-        gated = (left_half * spatial).astype(low_type)
-        branch = jnp.dot(gated, weight_out, preferred_element_type=wide) + bias_out
-        mixed_rows = (inputs + branch * keep_flat).astype(low_type).reshape(mine, SEQ, D)
+        bias_rows = relative(bias_spatial, 0)[:, None]
+
+        scaled_in, left_half, slope, normed_gate, inverse_gate, gate_low = project(
+            inputs_low.reshape(-1, D),
+            weight_in,
+            gain_in[None],
+            bias_in[None],
+            bias_hidden[None],
+            gain_gate[None],
+            bias_gate[None],
+        )
+        by_row = lambda value: value.reshape(mine, SEQ, -1)
+        left_half, slope, normed_gate, inverse_gate, gate_low = map(
+            by_row, (left_half, slope, normed_gate, inverse_gate, gate_low)
+        )
+        mixed_rows, spatial, gated = mix(
+            inputs_low, own, key, keep, mixing_rows, weight_out, bias_rows, bias_out[None], left_half, gate_low
+        )
         mixed = to_places(mixed_rows)
-
-        grad_branch = back_low.astype(wide).reshape(-1, D) * keep_flat
-        grad_bias_out = jnp.sum(grad_branch, 0)
-        branch_low = grad_branch.astype(low_type)
-        grad_weight_out = jnp.einsum("tg,td->gd", gated, branch_low, preferred_element_type=wide)
-        grad_gated = jnp.einsum("td,gd->tg", branch_low, weight_out, preferred_element_type=wide)
-        grad_spatial = grad_gated * left_half
-        grad_left = grad_gated * spatial
-        grad_bias_spatial = jnp.sum(grad_spatial.reshape(mine, SEQ, GATE), (0, 2))
-        spatial_low = grad_spatial.astype(low_type).reshape(mine, SEQ, GATE)
-        grad_gate = jnp.einsum("rij,ric->rjc", mixing, spatial_low, preferred_element_type=wide)
-        products = jnp.einsum("ric,rjc->rij", spatial_low, gate_low, preferred_element_type=wide)
-        grad_weight_spatial = jnp.sum(jnp.where(same_rows, products, 0.0), 0)
-        grad_gate = grad_gate.reshape(-1, GATE)
-        grad_gain_gate = jnp.sum(grad_gate * normed_gate, 0)
-        grad_bias_gate = jnp.sum(grad_gate, 0)
+        (
+            pre_low,
+            grad_weight_out,
+            grad_weight_spatial,
+            grad_bias_out,
+            grad_bias_spatial,
+            grad_gain_gate,
+            grad_bias_gate,
+            grad_bias_hidden,
+        ) = back(
+            back_low, own, key, keep, mixing_rows, mixing_rows.T, weight_out, gain_gate[None],
+            left_half, gate_low, normed_gate, inverse_gate, spatial, gated, slope,
+        )
+        pre_low = pre_low.reshape(-1, HID)
 
         grad_rest = jnp.concatenate(
             [
@@ -281,11 +519,7 @@
         )
         rest_sum = reduce_blocks(grad_rest.reshape(-1, D), sizes, place)
 
-        grad_right = norm_back(grad_gate * gain_gate, normed_gate, inverse_gate)
-        grad_hidden = jnp.concatenate([grad_left, grad_right], 1)
-        grad_pre = gelu_back(grad_hidden)[0]
-        grad_bias_hidden = jnp.sum(grad_pre, 0)
-        pre_low = grad_pre.astype(low_type)
+        normed_in, inverse_in = norm_parts(inputs_low.astype(wide).reshape(-1, D))
         grad_weight_in = jnp.einsum("td,th->dh", scaled_in, pre_low, preferred_element_type=wide)
         grad_scaled = jnp.einsum("th,dh->td", pre_low, weight_in, preferred_element_type=wide)
         grad_gain_in = jnp.sum(grad_scaled * normed_in, 0)
@@ -298,11 +532,11 @@
             [
                 grad_gain_in,
                 grad_bias_in,
-                grad_bias_hidden,
-                grad_gain_gate,
-                grad_bias_gate,
-                relative(grad_bias_spatial, 0),
-                grad_bias_out,
+                grad_bias_hidden[0],
+                grad_gain_gate[0],
+                grad_bias_gate[0],
+                relative(grad_bias_spatial[:, 0], 0),
+                grad_bias_out[0],
             ]
         )
         vector_part = grad_vector.astype(low_type).reshape(in_rows * devices, -1)

time: 321 us -> 256 us (0.80); the launches traced: 316 us -> 255 us
  matrix products: 73.2 us -> 14.5 us
  Pallas kernels: 0 us -> 49.3 us
  other arithmetic: 67.3 us -> 26.1 us
  waiting for transfers between devices: 98.8 us -> 81.2 us
  local copies, waits for them, and re-layouts: 20.8 us -> 27.2 us
    dot_general x7 -> x0, matrix products: 62.9 us -> none  [the longest x1 33.2 us: local(): jnp.dot(scaled_in, weight_in, preferred_element_type=wide) + bias_hidden]
    pallas_call x0 -> x3, Pallas kernels: none -> 49.3 us  [the longest x1 21.5 us: project(): pl.pallas_call(project_kernel, grid=(total // tile,), in_specs=[block(D),...]
    mul x2 -> x0, other arithmetic: 20.7 us -> none  [the longest x1 11.9 us: local(): grad_left = grad_gated * spatial]
    reduce_sum x4 -> x0, other arithmetic: 19.5 us -> none  [the longest x1 14.1 us: local(): grad_bias_hidden = jnp.sum(grad_pre, 0)]
    ppermute x36, waiting for transfers between devices: 98.8 us -> 81.2 us  [swap(): return lax.ppermute(value, axis, [(i, i ^ mask) for i in range(size)])]
    broadcast_in_dim x0 -> x8, local copies, waits for them, and re-layouts: none -> 5.96 us  [the longest x1 1.03 us: local(): own = segments[:, :, None]]
    unnamed x107 -> x115, local copies, waits for them, and re-layouts: 11.3 us -> 7.29 us
    select_n x8, other arithmetic: 1.97 us -> 5.34 us  [exchange(): jnp.where(mine == 0, jnp.concatenate([a, c], axis), jnp.concatenate([c, a...]
  transfers between devices with their start and end apart: 36 -> 36, of which waited for: 14 -> 17; matrix products, arithmetic and copies ran while one was open for 10% -> 18% of each run, Pallas kernels for 0% -> 8%
where the time goes in v2:
time: 256 us; the launch traced here: 255 us
  waiting for transfers between devices  81.2 us (32%)
  starting transfers between devices  55.1 us (22%)
  Pallas kernels  49.3 us (19%)
  local copies, waits for them, and re-layouts  27.2 us (11%)
  other arithmetic  26.1 us (10%)
  matrix products  14.5 us (6%)
    ppermute x36, waiting for transfers between devices, swap(): return lax.ppermute(value, axis, [(i, i ^ mask) for i in range(size)])  81.2 us
    ppermute x36, starting transfers between devices, swap(): return lax.ppermute(value, axis, [(i, i ^ mask) for i in range(size)])  55.1 us
    pallas_call x1, Pallas kernels, project(): pl.pallas_call(project_kernel, grid=(total // tile,), in_specs=[block(D),...  21.5 us
    pallas_call x1, Pallas kernels, back(): pl.pallas_call(back_kernel, grid=(rows,), in_specs=[per_row(length, D), p...  19.3 us
    pallas_call x1, Pallas kernels, mix(): pl.pallas_call(mix_kernel, grid=(rows,), in_specs=[per_row(length, D), pe...  8.5 us
    dot_general x1, matrix products, local(): jnp.einsum('th,dh->td', pre_low, weight_in, preferred_element_type=wide)  7.74 us
    unnamed x115, local copies, waits for them, and re-layouts  7.29 us
    dot_general x1, matrix products, local(): jnp.einsum('td,th->dh', scaled_in, pre_low, preferred_element_type=wide)  6.81 us
  transfers between devices with their start and end apart: 36, of which 17 were waited for; matrix products, arithmetic and copies ran while one was open for 18% of the time, Pallas kernels for 8%

profile of v2, /device:TPU:0, one launch (start us, length us, event | category | flops | bytes accessed | tf_op | source)
XLA Modules:
  0.0 255.3 jit_solution(11078700732277703203)
XLA Ops:
  2.5 4.1 %collective-permute-start.3 = (bf16[1,1,1,1,1,64,512]{6,5,4,3,2,1,0:T(8,128)(2,1)S(1)}, bf16[1,1,1,1,1,64,512]{6,5,4,3,2,1,0:T(8,128)(2,1)}, u32[]{:S(2)}, u32[]{:S(2)}) collective-permute-start(bf16[1,1,1,1,1,64,512]{6,5,4,3,2,1,0:T(8,128)(2,1)S(1)} %bitcast.130), channel_id=1, source_target_pairs={{0,2},{1,3},{2,0},{3,1},{4,6},{5,7},{6,4},{7,5},{8,10},{9,11},{10,... | collective-permute-start | bytes 196616 | tf_op jit(solution)/shard_map/ppermute | solution.py:66
  22.2 2.6 %collective-permute-done.4 = bf16[1,1,1,2,1,64,512]{6,5,3,4,2,1,0:T(8,128)(2,1)S(1)} collective-permute-done((bf16[1,1,1,2,1,64,512]{6,5,3,4,2,1,0:T(8,128)(2,1)S(1)}, bf16[1,1,1,2,1,64,512]{6,5,3,4,2,1,0:T(8,128)(2,1)S(1)}, u32[]{:S(2)}, u32[]{:S(2)}) %collective-permute-start.4) | collective-permute-done | bytes 131104 | tf_op jit(solution)/shard_map/ppermute | solution.py:66
  24.8 2.7 %collective-permute-start.7 = (bf16[1,1,1,2,2,64,512]{6,5,4,3,2,1,0:T(8,128)(2,1)S(1)}, bf16[1,1,1,2,2,64,512]{6,5,4,3,2,1,0:T(8,128)(2,1)S(1)}, u32[]{:S(2)}, u32[]{:S(2)}) collective-permute-start(bf16[1,1,1,2,2,64,512]{6,5,4,3,2,1,0:T(8,128)(2,1)S(1)} %copy_select_fusion.1), channel_id=1, source_target_pairs={{0,24},{4,28},{8,16},{12,20},{16,8},{20,12},{24,0},{28,4},{1,25},{... | collective-permute-start | bytes 786440 | tf_op jit(solution)/shard_map/ppermute | solution.py:66
  28.6 2.7 %collective-permute-start.13 = (bf16[1,1,1,2,2,16,3200]{6,5,4,3,2,1,0:T(8,128)(2,1)S(1)}, bf16[1,1,1,2,2,16,3200]{6,5,4,3,2,1,0:T(8,128)(2,1)S(1)}, u32[]{:S(2)}, u32[]{:S(2)}) collective-permute-start(bf16[1,1,1,2,2,16,3200]{6,5,4,3,2,1,0:T(8,128)(2,1)S(1)} %copy_select_fusion), channel_id=1, source_target_pairs={{0,24},{4,28},{8,16},{12,20},{16,8},{20,12},{24,0},{28,4},{1,25},{... | collective-permute-start | bytes 1228808 | tf_op jit(solution)/shard_map/ppermute | solution.py:66
  31.9 3.1 %collective-permute-done.7 = bf16[1,1,1,2,2,64,512]{6,5,4,3,2,1,0:T(8,128)(2,1)S(1)} collective-permute-done((bf16[1,1,1,2,2,64,512]{6,5,4,3,2,1,0:T(8,128)(2,1)S(1)}, bf16[1,1,1,2,2,64,512]{6,5,4,3,2,1,0:T(8,128)(2,1)S(1)}, u32[]{:S(2)}, u32[]{:S(2)}) %collective-permute-start.7) | collective-permute-done | bytes 262176 | tf_op jit(solution)/shard_map/ppermute | solution.py:66
  35.0 4.6 %collective-permute-start.2 = (bf16[2,128,512]{2,1,0:T(8,128)(2,1)S(1)}, bf16[2,128,512]{2,1,0:T(8,128)(2,1)S(1)}, u32[]{:S(2)}, u32[]{:S(2)}) collective-permute-start(bf16[2,128,512]{2,1,0:T(8,128)(2,1)S(1)} %copy-done.14), channel_id=1, source_target_pairs={{0,3},{1,2},{2,1},{3,0},{4,7},{5,6},{6,5},{7,4},{8,11},{9,10},{10,... | collective-permute-start | bytes 786440 | tf_op jit(solution)/shard_map/ppermute | solution.py:66
  39.6 7.9 %collective-permute-done.6 = bf16[1,1,1,2,2,64,512]{6,5,4,3,2,1,0:T(8,128)(2,1)S(1)} collective-permute-done((bf16[1,1,1,2,2,64,512]{6,5,4,3,2,1,0:T(8,128)(2,1)S(1)}, bf16[1,1,1,2,2,64,512]{6,5,4,3,2,1,0:T(8,128)(2,1)S(1)}, u32[]{:S(2)}, u32[]{:S(2)}) %collective-permute-start.6) | collective-permute-done | bytes 262176 | tf_op jit(solution)/shard_map/ppermute | solution.py:66
  47.5 2.7 %collective-permute-start.1 = (bf16[2,128,512]{2,1,0:T(8,128)(2,1)S(1)}, bf16[2,128,512]{2,1,0:T(8,128)(2,1)S(1)}, u32[]{:S(2)}, u32[]{:S(2)}) collective-permute-start(bf16[2,128,512]{2,1,0:T(8,128)(2,1)S(1)} %copy-done.13), channel_id=1, source_target_pairs={{0,2},{1,3},{2,0},{3,1},{4,6},{5,7},{6,4},{7,5},{8,10},{9,11},{10,... | collective-permute-start | bytes 786440 | tf_op jit(solution)/shard_map/ppermute | solution.py:66
  50.3 2.3 collective-permute-start
  56.5 8.6 %collective-permute-done.11 = bf16[1,1,1,2,2,16,3200]{6,5,4,3,2,1,0:T(8,128)(2,1)S(1)} collective-permute-done((bf16[1,1,1,2,2,16,3200]{6,5,4,3,2,1,0:T(8,128)(2,1)S(1)}, bf16[1,1,1,2,2,16,3200]{6,5,4,3,2,1,0:T(8,128)(2,1)S(1)}, u32[]{:S(2)}, u32[]{:S(2)}) %collective-permute-start.11) | collective-permute-done | bytes 409632 | tf_op jit(solution)/shard_map/ppermute | solution.py:66
  66.0 2.5 collective-permute-start.19
  72.4 9.0 %collective-permute-done.19 = bf16[2,128,512]{2,1,0:T(8,128)(2,1)S(1)} collective-permute-done((bf16[2,128,512]{2,1,0:T(8,128)(2,1)S(1)}, bf16[2,128,512]{2,1,0:T(8,128)(2,1)S(1)}, u32[]{:S(2)}, u32[]{:S(2)}) %collective-permute-start.19) | collective-permute-done | bytes 262176 | tf_op jit(solution)/shard_map/ppermute | solution.py:66
  87.5 3.5 %maximum_select_fusion = bf16[2,2,2,2,2,16,3200]{6,5,4,3,2,1,0:T(8,128)(2,1)S(1)} fusion(bf16[2,2,1,2,2,16,3200]{6,5,4,3,2,1,0:T(8,128)(2,1)} %collective-permute-done.14, bf16[2,2,1,2,2,16,3200]{6,5,4,3,2,1,0:T(8,128)(2,1)} %copy-done.2, pred[]{:T(512)S(6)} %eq.48), kind=kLoop, calls=%fused_computation.4 | loop fusion | flops 4915200 | bytes 6553601 | tf_op jit(solution)/shard_map/jit(_where)/select_n | solution.py:101
  91.1 2.2 slice.112.w_ref
  99.0 21.5 %project.1 = (bf16[1024,512]{1,0:T(8,128)(2,1)}, bf16[1024,1536]{1,0:T(8,128)(2,1)}, bf16[1024,3072]{1,0:T(8,128)(2,1)}, bf16[1024,1536]{1,0:T(8,128)(2,1)}, f32...) custom-call(bf16[1024,512]{1,0:T(8,128)(2,1)} %bitcast.104, bf16[512,3072]{1,0:T(8,128)(2,1)} %slice.112.w_ref, ...), custom_call_target="tpu_custom_call" | custom-call | flops 3347054592 | bytes 20971520 | tf_op jit(solution)/shard_map/project/pallas_call | solution.py:306
  120.5 8.5 %mix.1 = (bf16[2,512,512]{2,1,0:T(8,128)(2,1)}, bf16[2,512,1536]{2,1,0:T(8,128)(2,1)}, bf16[2,512,1536]{2,1,0:T(8,128)(2,1)}) custom-call(bf16[2,512,512]{2,1,0:T(8,128)(2,1)} %copy-done, s32[2,512,1]{2,1,0:T(8,128)} %copy.95.own_ref, s32[2,1,512]{2,1,0:T(1,128)} %compare_select_fusion.key_ref.key_line, f32[2,512,1]{2,1,0:T(8,128)} %broadcast_multiply_fusion.keep_ref, ...), custom_call_target="tpu_custom_call" | custom-call | flops 3221225472 | bytes 16777216 | tf_op jit(solution)/shard_map/mix/pallas_call | solution.py:329
  129.0 2.1 fusion.41
  133.0 19.3 %back.1 = (bf16[2,512,3072]{2,1,0:T(8,128)(2,1)}, bf16[1536,512]{1,0:T(8,128)(2,1)}, bf16[512,512]{1,0:T(8,128)(2,1)}, f32[1,512]{1,0:T(1,128)}, f32[512,1]{1,0:...) custom-call(bf16[2,512,512]{2,1,0:T(8,128)(2,1)} %pad_maximum_fusion.3.cot_ref, ...), custom_call_target="tpu_custom_call" | custom-call | flops 6442450944 | bytes 31457280 | tf_op jit(solution)/shard_map/back/pallas_call | solution.py:354
  152.4 7.7 %multiply_reduce_fusion = (bf16[512]{0:T(512)(128)(2,1)}, f32[1024]{0:T(1024)S(1)}, f32[1024]{0:T(1024)S(1)}, bf16[512]{0:T(512)(128)(2,1)}, f32[1024,512]{1,0:T(8,128)S(1)}) fusion(f32[1024]{0:T(1024)} %bitcast.157, f32[1024]{0:T(1024)} %bitcast.159, bf16[2,512,512]{2,1,0:T(8,128)(2,1)} %copy-done, f32[512]{0:T(512)} %slice.98, ...), kind=kOutput, calls=%fused_computation.16 | convolution fusion | flops 3226465280 | bytes 12603392 | tf_op jit(solution)/shard_map/th,dh->td/dot_general | solution.py:524
  163.4 2.5 collective-permute-start.21
  168.4 6.8 %convolution_convert_fusion = bf16[512,3072]{1,0:T(8,128)(2,1)S(1)} fusion(bf16[1024,512]{1,0:T(8,128)(2,1)S(1)} %copy-done.47, bf16[1024,3072]{1,0:T(8,128)(2,1)} %bitcast.163), kind=kOutput, calls=%fused_computation.2 | convolution fusion | flops 3222798336 | bytes 10485760 | tf_op jit(solution)/shard_map/td,th->dh/dot_general | solution.py:523
  178.0 4.2 %collective-permute-start.16 = (bf16[2,128,512]{2,1,0:T(8,128)(2,1)S(1)}, bf16[2,128,512]{2,1,0:T(8,128)(2,1)S(1)}, u32[]{:S(2)}, u32[]{:S(2)}) collective-permute-start(bf16[2,128,512]{2,1,0:T(8,128)(2,1)S(1)} %copy-done.16), channel_id=1, source_target_pairs={{0,2},{1,3},{2,0},{3,1},{4,6},{5,7},{6,4},{7,5},{8,10},{9,11},{10,... | collective-permute-start | bytes 786440 | tf_op jit(solution)/shard_map/ppermute | solution.py:66
  182.2 9.2 %collective-permute-done.22 = bf16[2,128,512]{2,1,0:T(8,128)(2,1)S(1)} collective-permute-done((bf16[2,128,512]{2,1,0:T(8,128)(2,1)S(1)}, bf16[2,128,512]{2,1,0:T(8,128)(2,1)S(1)}, u32[]{:S(2)}, u32[]{:S(2)}) %collective-permute-start.22) | collective-permute-done | bytes 262176 | tf_op jit(solution)/shard_map/ppermute | solution.py:66
  192.2 2.1 collective-permute-start.33
  199.2 2.1 collective-permute-done.15
  202.4 5.5 %collective-permute-done.32 = bf16[1,1,1,2,2,64,512]{6,5,4,3,2,1,0:T(8,128)(2,1)S(1)} collective-permute-done((bf16[1,1,1,2,2,64,512]{6,5,4,3,2,1,0:T(8,128)(2,1)S(1)}, bf16[1,1,1,2,2,64,512]{6,5,4,3,2,1,0:T(8,128)(2,1)S(1)}, u32[]{:S(2)}, u32[]{:S(2)}) %collective-permute-start.32) | collective-permute-done | bytes 262176 | tf_op jit(solution)/shard_map/ppermute | solution.py:66
  210.1 3.2 %collective-permute-done.34 = bf16[1,1,1,2,1,64,512]{6,5,4,3,2,1,0:T(8,128)(2,1)S(1)} collective-permute-done((bf16[1,1,1,2,1,64,512]{6,5,4,3,2,1,0:T(8,128)(2,1)S(1)}, bf16[1,1,1,2,1,64,512]{6,5,4,3,2,1,0:T(8,128)(2,1)S(1)}, u32[]{:S(2)}, u32[]{:S(2)}) %collective-permute-start.34) | collective-permute-done | bytes 131104 | tf_op jit(solution)/shard_map/ppermute | solution.py:66
  213.4 3.3 %collective-permute-start.35 = (bf16[1,1,1,1,1,64,512]{6,5,4,3,2,1,0:T(8,128)(2,1)S(1)}, bf16[1,1,1,1,1,64,512]{6,5,4,3,2,1,0:T(8,128)(2,1)S(1)}, u32[]{:S(2)}, u32[]{:S(2)}) collective-permute-start(bf16[1,1,1,1,1,64,512]{6,5,4,3,2,1,0:T(8,128)(2,1)S(1)} %constant_dynamic-slice_fusion), channel_id=1, source_target_pairs={{0,2},{1,3},{2,0},{3,1},{4,6},{5,7},{6,4},{7,5},{8,10},{9,11},{10,... | collective-permute-start | bytes 196616 | tf_op jit(solution)/shard_map/ppermute | solution.py:66
  224.0 9.0 %collective-permute-done.27 = bf16[1,1,1,2,2,16,3200]{6,5,4,3,2,1,0:T(8,128)(2,1)S(1)} collective-permute-done((bf16[1,1,1,2,2,16,3200]{6,5,4,3,2,1,0:T(8,128)(2,1)S(1)}, bf16[1,1,1,2,2,16,3200]{6,5,4,3,2,1,0:T(8,128)(2,1)S(1)}, u32[]{:S(2)}, u32[]{:S(2)}) %collective-permute-start.27) | collective-permute-done | bytes 409632 | tf_op jit(solution)/shard_map/ppermute | solution.py:66
  233.0 7.1 %collective-permute-done.26 = bf16[1,1,1,2,2,16,3200]{6,5,4,3,2,1,0:T(8,128)(2,1)S(1)} collective-permute-done((bf16[1,1,1,2,2,16,3200]{6,5,4,3,2,1,0:T(8,128)(2,1)S(1)}, bf16[1,1,1,2,2,16,3200]{6,5,4,3,2,1,0:T(8,128)(2,1)S(1)}, u32[]{:S(2)}, u32[]{:S(2)}) %collective-permute-start.26) | collective-permute-done | bytes 409632 | tf_op jit(solution)/shard_map/ppermute | solution.py:66
  241.1 5.7 %collective-permute-done.28 = bf16[1,1,1,2,1,16,3200]{6,5,4,3,2,1,0:T(8,128)(2,1)S(1)} collective-permute-done((bf16[1,1,1,2,1,16,3200]{6,5,4,3,2,1,0:T(8,128)(2,1)S(1)}, bf16[1,1,1,2,1,16,3200]{6,5,4,3,2,1,0:T(8,128)(2,1)S(1)}, u32[]{:S(2)}, u32[]{:S(2)}) %collective-permute-start.28) | collective-permute-done | bytes 204832 | tf_op jit(solution)/shard_map/ppermute | solution.py:66
  249.5 4.1 %collective-permute-done.29 = bf16[1,1,1,1,1,16,3200]{6,5,4,3,2,1,0:T(8,128)(2,1)S(1)} collective-permute-done((bf16[1,1,1,1,1,16,3200]{6,5,4,3,2,1,0:T(8,128)(2,1)S(1)}, bf16[1,1,1,1,1,16,3200]{6,5,4,3,2,1,0:T(8,128)(2,1)S(1)}, u32[]{:S(2)}, u32[]{:S(2)}) %collective-permute-start.29) | collective-permute-done | bytes 102432 | tf_op jit(solution)/shard_map/ppermute | solution.py:66
  (282 shorter events, 71.0 us)
Async XLA Ops:
  2.5 15.5 %collective-permute-start.3 = (bf16[1,1,1,1,1,64,512]{6,5,4,3,2,1,0:T(8,128)(2,1)S(1)}, bf16[1,1,1,1,1,64,512]{6,5,4,3,2,1,0:T(8,128)(2,1)}, u32[]{:S(2)}, u32[]{:S(2)}) collective-permute-start(bf16[1,1,1,1,1,64,512]{6,5,4,3,2,1,0:T(8,128)(2,1)S(1)} %bitcast.130), channel_id=1, source_target_pairs={{0,2},{1,3},{2,0},{3,1},{4,6},{5,7},{6,4},{7,5},{8,10},{9,11},{10,... | collective-permute-start | bytes 196616 | tf_op jit(solution)/shard_map/ppermute | solution.py:66
  8.5 13.3 %collective-permute-start.9 = (bf16[1,1,1,1,1,16,3200]{6,5,4,3,2,1,0:T(8,128)(2,1)S(1)}, bf16[1,1,1,1,1,16,3200]{6,5,4,3,2,1,0:T(8,128)(2,1)S(1)}, u32[]{:S(2)}, u32[]{:S(2)}) collective-permute-start(bf16[1,1,1,1,1,16,3200]{6,5,4,3,2,1,0:T(8,128)(2,1)S(1)} %get-tuple-element.132), channel_id=1, source_target_pairs={{0,2},{1,3},{2,0},{3,1},{4,6},{5,7},{6,4},{7,5},{8,10},{9,11},{10,... | collective-permute-start | bytes 307208 | tf_op jit(solution)/shard_map/ppermute | solution.py:66
  21.8 6.6 %collective-permute-start.10 = (bf16[1,1,1,2,1,16,3200]{6,5,3,4,2,1,0:T(8,128)(2,1)S(1)}, bf16[1,1,1,2,1,16,3200]{6,5,3,4,2,1,0:T(8,128)(2,1)S(1)}, u32[]{:S(2)}, u32[]{:S(2)}) collective-permute-start(bf16[1,1,1,2,1,16,3200]{6,5,3,4,2,1,0:T(8,128)(2,1)S(1)} %fusion.12), channel_id=1, source_target_pairs={{0,1},{1,0},{2,3},{3,2},{4,5},{5,4},{6,7},{7,6},{8,9},{9,8},{10,11... | collective-permute-start | bytes 614408 | tf_op jit(solution)/shard_map/ppermute | solution.py:66
  24.8 10.1 %collective-permute-start.7 = (bf16[1,1,1,2,2,64,512]{6,5,4,3,2,1,0:T(8,128)(2,1)S(1)}, bf16[1,1,1,2,2,64,512]{6,5,4,3,2,1,0:T(8,128)(2,1)S(1)}, u32[]{:S(2)}, u32[]{:S(2)}) collective-permute-start(bf16[1,1,1,2,2,64,512]{6,5,4,3,2,1,0:T(8,128)(2,1)S(1)} %copy_select_fusion.1), channel_id=1, source_target_pairs={{0,24},{4,28},{8,16},{12,20},{16,8},{20,12},{24,0},{28,4},{1,25},{... | collective-permute-start | bytes 786440 | tf_op jit(solution)/shard_map/ppermute | solution.py:66
  27.6 19.9 %collective-permute-start.6 = (bf16[1,1,1,2,2,64,512]{6,5,4,3,2,1,0:T(8,128)(2,1)S(1)}, bf16[1,1,1,2,2,64,512]{6,5,4,3,2,1,0:T(8,128)(2,1)S(1)}, u32[]{:S(2)}, u32[]{:S(2)}) collective-permute-start(bf16[1,1,1,2,2,64,512]{6,5,4,3,2,1,0:T(8,128)(2,1)S(1)} %copy_select_fusion.1), channel_id=1, source_target_pairs={{0,16},{4,20},{8,24},{12,28},{16,0},{20,4},{24,8},{28,12},{1,17},{... | collective-permute-start | bytes 786440 | tf_op jit(solution)/shard_map/ppermute | solution.py:66
  28.1 22.2 %collective-permute-start.5 = (bf16[1,1,1,2,2,64,512]{6,5,4,3,2,1,0:T(8,128)(2,1)S(1)}, bf16[1,1,1,2,2,64,512]{6,5,4,3,2,1,0:T(8,128)(2,1)S(1)}, u32[]{:S(2)}, u32[]{:S(2)}) collective-permute-start(bf16[1,1,1,2,2,64,512]{6,5,4,3,2,1,0:T(8,128)(2,1)S(1)} %copy_select_fusion.1), channel_id=1, source_target_pairs={{0,8},{4,12},{8,0},{12,4},{16,24},{20,28},{24,16},{28,20},{1,9},{5... | collective-permute-start | bytes 786440 | tf_op jit(solution)/shard_map/ppermute | solution.py:66
  28.6 24.3 %collective-permute-start.13 = (bf16[1,1,1,2,2,16,3200]{6,5,4,3,2,1,0:T(8,128)(2,1)S(1)}, bf16[1,1,1,2,2,16,3200]{6,5,4,3,2,1,0:T(8,128)(2,1)S(1)}, u32[]{:S(2)}, u32[]{:S(2)}) collective-permute-start(bf16[1,1,1,2,2,16,3200]{6,5,4,3,2,1,0:T(8,128)(2,1)S(1)} %copy_select_fusion), channel_id=1, source_target_pairs={{0,24},{4,28},{8,16},{12,20},{16,8},{20,12},{24,0},{28,4},{1,25},{... | collective-permute-start | bytes 1228808 | tf_op jit(solution)/shard_map/ppermute | solution.py:66
  31.3 23.5 %collective-permute-start.12 = (bf16[1,1,1,2,2,16,3200]{6,5,4,3,2,1,0:T(8,128)(2,1)S(1)}, bf16[1,1,1,2,2,16,3200]{6,5,4,3,2,1,0:T(8,128)(2,1)S(1)}, u32[]{:S(2)}, u32[]{:S(2)}) collective-permute-start(bf16[1,1,1,2,2,16,3200]{6,5,4,3,2,1,0:T(8,128)(2,1)S(1)} %copy_select_fusion), channel_id=1, source_target_pairs={{0,16},{4,20},{8,24},{12,28},{16,0},{20,4},{24,8},{28,12},{1,17},{... | collective-permute-start | bytes 1228808 | tf_op jit(solution)/shard_map/ppermute | solution.py:66
  35.0 30.6 %collective-permute-start.2 = (bf16[2,128,512]{2,1,0:T(8,128)(2,1)S(1)}, bf16[2,128,512]{2,1,0:T(8,128)(2,1)S(1)}, u32[]{:S(2)}, u32[]{:S(2)}) collective-permute-start(bf16[2,128,512]{2,1,0:T(8,128)(2,1)S(1)} %copy-done.14), channel_id=1, source_target_pairs={{0,3},{1,2},{2,1},{3,0},{4,7},{5,6},{6,5},{7,4},{8,11},{9,10},{10,... | collective-permute-start | bytes 786440 | tf_op jit(solution)/shard_map/ppermute | solution.py:66
  47.5 21.1 %collective-permute-start.1 = (bf16[2,128,512]{2,1,0:T(8,128)(2,1)S(1)}, bf16[2,128,512]{2,1,0:T(8,128)(2,1)S(1)}, u32[]{:S(2)}, u32[]{:S(2)}) collective-permute-start(bf16[2,128,512]{2,1,0:T(8,128)(2,1)S(1)} %copy-done.13), channel_id=1, source_target_pairs={{0,2},{1,3},{2,0},{3,1},{4,6},{5,7},{6,4},{7,5},{8,10},{9,11},{10,... | collective-permute-start | bytes 786440 | tf_op jit(solution)/shard_map/ppermute | solution.py:66
  50.3 19.2 %collective-permute-start = (bf16[2,128,512]{2,1,0:T(8,128)(2,1)S(1)}, bf16[2,128,512]{2,1,0:T(8,128)(2,1)S(1)}, u32[]{:S(2)}, u32[]{:S(2)}) collective-permute-start(bf16[2,128,512]{2,1,0:T(8,128)(2,1)S(1)} %copy-done.12), channel_id=1, source_target_pairs={{0,1},{1,0},{2,3},{3,2},{4,5},{5,4},{6,7},{7,6},{8,9},{9,8},{10,11... | collective-permute-start | bytes 786440 | tf_op jit(solution)/shard_map/ppermute | solution.py:66
  52.9 19.5 %collective-permute-start.20 = (bf16[2,128,512]{2,1,0:T(8,128)(2,1)}, bf16[2,128,512]{2,1,0:T(8,128)(2,1)S(1)}, u32[]{:S(2)}, u32[]{:S(2)}) collective-permute-start(bf16[2,128,512]{2,1,0:T(8,128)(2,1)} %get-tuple-element.86), channel_id=1, source_target_pairs={{0,3},{1,2},{2,1},{3,0},{4,7},{5,6},{6,5},{7,4},{8,11},{9,10},{10,... | collective-permute-start | bytes 786440 | tf_op jit(solution)/shard_map/ppermute | solution.py:66
  54.9 10.2 %collective-permute-start.11 = (bf16[1,1,1,2,2,16,3200]{6,5,4,3,2,1,0:T(8,128)(2,1)S(1)}, bf16[1,1,1,2,2,16,3200]{6,5,4,3,2,1,0:T(8,128)(2,1)S(1)}, u32[]{:S(2)}, u32[]{:S(2)}) collective-permute-start(bf16[1,1,1,2,2,16,3200]{6,5,4,3,2,1,0:T(8,128)(2,1)S(1)} %copy_select_fusion), channel_id=1, source_target_pairs={{0,8},{4,12},{8,0},{12,4},{16,24},{20,28},{24,16},{28,20},{1,9},{5... | collective-permute-start | bytes 1228808 | tf_op jit(solution)/shard_map/ppermute | solution.py:66
  65.1 18.2 %collective-permute-start.8 = (bf16[2,2,1,2,2,64,512]{6,5,4,3,2,1,0:T(8,128)(2,1)S(1)}, bf16[2,2,1,2,2,64,512]{6,5,4,3,2,1,0:T(8,128)(2,1)S(1)}, u32[]{:S(2)}, u32[]{:S(2)}) collective-permute-start(bf16[2,2,1,2,2,64,512]{6,5,4,3,2,1,0:T(8,128)(2,1)S(1)} %maximum_select_fusion.3), channel_id=1, source_target_pairs={{0,4},{4,0},{8,12},{12,8},{16,20},{20,16},{24,28},{28,24},{1,5},{5... | collective-permute-start | bytes 3145736 | tf_op jit(solution)/shard_map/ppermute | solution.py:66
  66.0 15.3 %collective-permute-start.19 = (bf16[2,128,512]{2,1,0:T(8,128)(2,1)S(1)}, bf16[2,128,512]{2,1,0:T(8,128)(2,1)S(1)}, u32[]{:S(2)}, u32[]{:S(2)}) collective-permute-start(bf16[2,128,512]{2,1,0:T(8,128)(2,1)S(1)} %copy-done.11), channel_id=1, source_target_pairs={{0,2},{1,3},{2,0},{3,1},{4,6},{5,7},{6,4},{7,5},{8,10},{9,11},{10,... | collective-permute-start | bytes 786440 | tf_op jit(solution)/shard_map/ppermute | solution.py:66
  68.5 13.7 %collective-permute-start.18 = (bf16[2,128,512]{2,1,0:T(8,128)(2,1)S(1)}, bf16[2,128,512]{2,1,0:T(8,128)(2,1)S(1)}, u32[]{:S(2)}, u32[]{:S(2)}) collective-permute-start(bf16[2,128,512]{2,1,0:T(8,128)(2,1)S(1)} %copy-done.10), channel_id=1, source_target_pairs={{0,1},{1,0},{2,3},{3,2},{4,5},{5,4},{6,7},{7,6},{8,9},{9,8},{10,11... | collective-permute-start | bytes 786440 | tf_op jit(solution)/shard_map/ppermute | solution.py:66
  69.4 18.0 %collective-permute-start.14 = (bf16[2,2,1,2,2,16,3200]{6,5,4,3,2,1,0:T(8,128)(2,1)S(1)}, bf16[2,2,1,2,2,16,3200]{6,5,4,3,2,1,0:T(8,128)(2,1)}, u32[]{:S(2)}, u32[]{:S(2)}) collective-permute-start(bf16[2,2,1,2,2,16,3200]{6,5,4,3,2,1,0:T(8,128)(2,1)S(1)} %maximum_select_fusion.2), channel_id=1, source_target_pairs={{0,4},{4,0},{8,12},{12,8},{16,20},{20,16},{24,28},{28,24},{1,5},{5... | collective-permute-start | bytes 4915208 | tf_op jit(solution)/shard_map/ppermute | solution.py:66
  131.1 63.2 %collective-permute-start.17 = (bf16[2,128,512]{2,1,0:T(8,128)(2,1)}, bf16[2,128,512]{2,1,0:T(8,128)(2,1)}, u32[]{:S(2)}, u32[]{:S(2)}) collective-permute-start(bf16[2,128,512]{2,1,0:T(8,128)(2,1)} %get-tuple-element.93), channel_id=1, source_target_pairs={{0,3},{1,2},{2,1},{3,0},{4,7},{5,6},{6,5},{7,4},{8,11},{9,10},{10,... | collective-permute-start | bytes 786440 | tf_op jit(solution)/shard_map/ppermute | solution.py:66
  161.4 15.7 %collective-permute-start.23 = (bf16[2,128,512]{2,1,0:T(8,128)(2,1)S(1)}, bf16[2,128,512]{2,1,0:T(8,128)(2,1)S(1)}, u32[]{:S(2)}, u32[]{:S(2)}) collective-permute-start(bf16[2,128,512]{2,1,0:T(8,128)(2,1)S(1)} %get-tuple-element.81), channel_id=1, source_target_pairs={{0,3},{1,2},{2,1},{3,0},{4,7},{5,6},{6,5},{7,4},{8,11},{9,10},{10,... | collective-permute-start | bytes 786440 | tf_op jit(solution)/shard_map/ppermute | solution.py:66
  163.4 28.0 %collective-permute-start.22 = (bf16[2,128,512]{2,1,0:T(8,128)(2,1)S(1)}, bf16[2,128,512]{2,1,0:T(8,128)(2,1)S(1)}, u32[]{:S(2)}, u32[]{:S(2)}) collective-permute-start(bf16[2,128,512]{2,1,0:T(8,128)(2,1)S(1)} %get-tuple-element.82), channel_id=1, source_target_pairs={{0,2},{1,3},{2,0},{3,1},{4,6},{5,7},{6,4},{7,5},{8,10},{9,11},{10,... | collective-permute-start | bytes 786440 | tf_op jit(solution)/shard_map/ppermute | solution.py:66
  163.4 28.1 %collective-permute-start.21 = (bf16[2,128,512]{2,1,0:T(8,128)(2,1)S(1)}, bf16[2,128,512]{2,1,0:T(8,128)(2,1)S(1)}, u32[]{:S(2)}, u32[]{:S(2)}) collective-permute-start(bf16[2,128,512]{2,1,0:T(8,128)(2,1)S(1)} %get-tuple-element.83), channel_id=1, source_target_pairs={{0,1},{1,0},{2,3},{3,2},{4,5},{5,4},{6,7},{7,6},{8,9},{9,8},{10,11... | collective-permute-start | bytes 786440 | tf_op jit(solution)/shard_map/ppermute | solution.py:66
  176.7 15.1 %collective-permute-start.30 = (bf16[2,2,1,2,2,64,512]{6,5,4,3,2,1,0:T(8,128)(2,1)S(1)}, bf16[2,2,1,2,2,64,512]{6,5,4,3,2,1,0:T(8,128)(2,1)S(1)}, u32[]{:S(2)}, u32[]{:S(2)}) collective-permute-start(bf16[2,2,1,2,2,64,512]{6,5,4,3,2,1,0:T(8,128)(2,1)S(1)} %fusion.4), channel_id=1, source_target_pairs={{0,4},{4,0},{8,12},{12,8},{16,20},{20,16},{24,28},{28,24},{1,5},{5... | collective-permute-start | bytes 3145736 | tf_op jit(solution)/shard_map/ppermute | solution.py:66
  178.0 17.8 %collective-permute-start.16 = (bf16[2,128,512]{2,1,0:T(8,128)(2,1)S(1)}, bf16[2,128,512]{2,1,0:T(8,128)(2,1)S(1)}, u32[]{:S(2)}, u32[]{:S(2)}) collective-permute-start(bf16[2,128,512]{2,1,0:T(8,128)(2,1)S(1)} %copy-done.16), channel_id=1, source_target_pairs={{0,2},{1,3},{2,0},{3,1},{4,6},{5,7},{6,4},{7,5},{8,10},{9,11},{10,... | collective-permute-start | bytes 786440 | tf_op jit(solution)/shard_map/ppermute | solution.py:66
  191.4 9.9 %collective-permute-start.15 = (bf16[2,128,512]{2,1,0:T(8,128)(2,1)S(1)}, bf16[2,128,512]{2,1,0:T(8,128)(2,1)S(1)}, u32[]{:S(2)}, u32[]{:S(2)}) collective-permute-start(bf16[2,128,512]{2,1,0:T(8,128)(2,1)S(1)} %copy-done.15), channel_id=1, source_target_pairs={{0,1},{1,0},{2,3},{3,2},{4,5},{5,4},{6,7},{7,6},{8,9},{9,8},{10,11... | collective-permute-start | bytes 786440 | tf_op jit(solution)/shard_map/ppermute | solution.py:66
  191.5 27.6 %collective-permute-start.24 = (bf16[2,2,1,2,2,16,3200]{6,5,4,3,2,1,0:T(8,128)(2,1)S(1)}, bf16[2,2,1,2,2,16,3200]{6,5,4,3,2,1,0:T(8,128)(2,1)S(1)}, u32[]{:S(2)}, u32[]{:S(2)}) collective-permute-start(bf16[2,2,1,2,2,16,3200]{6,5,4,3,2,1,0:T(8,128)(2,1)S(1)} %constant_dynamic-slice_fusion.18), channel_id=1, source_target_pairs={{0,4},{4,0},{8,12},{12,8},{16,20},{20,16},{24,28},{28,24},{1,5},{5... | collective-permute-start | bytes 4915208 | tf_op jit(solution)/shard_map/ppermute | solution.py:66
  192.2 10.2 %collective-permute-start.33 = (bf16[1,1,1,2,2,64,512]{6,5,4,3,2,1,0:T(8,128)(2,1)S(1)}, bf16[1,1,1,2,2,64,512]{6,5,4,3,2,1,0:T(8,128)(2,1)S(1)}, u32[]{:S(2)}, u32[]{:S(2)}) collective-permute-start(bf16[1,1,1,2,2,64,512]{6,5,4,3,2,1,0:T(8,128)(2,1)S(1)} %get-tuple-element.74), channel_id=1, source_target_pairs={{0,24},{4,28},{8,16},{12,20},{16,8},{20,12},{24,0},{28,4},{1,25},{... | collective-permute-start | bytes 786440 | tf_op jit(solution)/shard_map/ppermute | solution.py:66
  194.3 13.6 %collective-permute-start.32 = (bf16[1,1,1,2,2,64,512]{6,5,4,3,2,1,0:T(8,128)(2,1)S(1)}, bf16[1,1,1,2,2,64,512]{6,5,4,3,2,1,0:T(8,128)(2,1)S(1)}, u32[]{:S(2)}, u32[]{:S(2)}) collective-permute-start(bf16[1,1,1,2,2,64,512]{6,5,4,3,2,1,0:T(8,128)(2,1)S(1)} %get-tuple-element.75), channel_id=1, source_target_pairs={{0,8},{4,12},{8,0},{12,4},{16,24},{20,28},{24,16},{28,20},{1,9},{5... | collective-permute-start | bytes 786440 | tf_op jit(solution)/shard_map/ppermute | solution.py:66
  195.8 12.1 %collective-permute-start.31 = (bf16[1,1,1,2,2,64,512]{6,5,4,3,2,1,0:T(8,128)(2,1)S(1)}, bf16[1,1,1,2,2,64,512]{6,5,4,3,2,1,0:T(8,128)(2,1)S(1)}, u32[]{:S(2)}, u32[]{:S(2)}) collective-permute-start(bf16[1,1,1,2,2,64,512]{6,5,4,3,2,1,0:T(8,128)(2,1)S(1)} %get-tuple-element.73), channel_id=1, source_target_pairs={{0,16},{4,20},{8,24},{12,28},{16,0},{20,4},{24,8},{28,12},{1,17},{... | collective-permute-start | bytes 786440 | tf_op jit(solution)/shard_map/ppermute | solution.py:66
  219.7 13.3 %collective-permute-start.27 = (bf16[1,1,1,2,2,16,3200]{6,5,4,3,2,1,0:T(8,128)(2,1)S(1)}, bf16[1,1,1,2,2,16,3200]{6,5,4,3,2,1,0:T(8,128)(2,1)S(1)}, u32[]{:S(2)}, u32[]{:S(2)}) collective-permute-start(bf16[1,1,1,2,2,16,3200]{6,5,4,3,2,1,0:T(8,128)(2,1)S(1)} %get-tuple-element.71), channel_id=1, source_target_pairs={{0,24},{4,28},{8,16},{12,20},{16,8},{20,12},{24,0},{28,4},{1,25},{... | collective-permute-start | bytes 1228808 | tf_op jit(solution)/shard_map/ppermute | solution.py:66
  221.8 18.4 %collective-permute-start.26 = (bf16[1,1,1,2,2,16,3200]{6,5,4,3,2,1,0:T(8,128)(2,1)S(1)}, bf16[1,1,1,2,2,16,3200]{6,5,4,3,2,1,0:T(8,128)(2,1)S(1)}, u32[]{:S(2)}, u32[]{:S(2)}) collective-permute-start(bf16[1,1,1,2,2,16,3200]{6,5,4,3,2,1,0:T(8,128)(2,1)S(1)} %get-tuple-element.72), channel_id=1, source_target_pairs={{0,8},{4,12},{8,0},{12,4},{16,24},{20,28},{24,16},{28,20},{1,9},{5... | collective-permute-start | bytes 1228808 | tf_op jit(solution)/shard_map/ppermute | solution.py:66
  223.0 17.2 %collective-permute-start.25 = (bf16[1,1,1,2,2,16,3200]{6,5,4,3,2,1,0:T(8,128)(2,1)S(1)}, bf16[1,1,1,2,2,16,3200]{6,5,4,3,2,1,0:T(8,128)(2,1)S(1)}, u32[]{:S(2)}, u32[]{:S(2)}) collective-permute-start(bf16[1,1,1,2,2,16,3200]{6,5,4,3,2,1,0:T(8,128)(2,1)S(1)} %get-tuple-element.70), channel_id=1, source_target_pairs={{0,16},{4,20},{8,24},{12,28},{16,0},{20,4},{24,8},{28,12},{1,17},{... | collective-permute-start | bytes 1228808 | tf_op jit(solution)/shard_map/ppermute | solution.py:66
  246.9 6.7 %collective-permute-start.29 = (bf16[1,1,1,1,1,16,3200]{6,5,4,3,2,1,0:T(8,128)(2,1)S(1)}, bf16[1,1,1,1,1,16,3200]{6,5,4,3,2,1,0:T(8,128)(2,1)S(1)}, u32[]{:S(2)}, u32[]{:S(2)}) collective-permute-start(bf16[1,1,1,1,1,16,3200]{6,5,4,3,2,1,0:T(8,128)(2,1)S(1)} %constant_dynamic-slice_fusion.13), channel_id=1, source_target_pairs={{0,2},{1,3},{2,0},{3,1},{4,6},{5,7},{6,4},{7,5},{8,10},{9,11},{10,... | collective-permute-start | bytes 307208 | tf_op jit(solution)/shard_map/ppermute | solution.py:66
  (52 other events, 481.5 us)

commit v3 on v1

v3 whole, which is shorter than its diff:
```python
import functools
import math

import jax
import jax.numpy as jnp
from jax import lax
from jax.experimental import pallas as pl
from jax.experimental.pallas import tpu as pltpu
from jax.sharding import PartitionSpec as P


D = 512
HID = 3072
SEQ = 512
GATE = 1536
LANE = 128

norm_eps = 1e-05
beta_one = 0.9
beta_two = 0.999
adam_eps = 1e-08
step_count = 10.0
decay_matrix = 0.1
rate_in = 0.12
rate_spatial = 0.2
rate_out = 0.07
rate_vector = 1.0

low_type = jnp.bfloat16
wide = jnp.float32


def norm_parts(values):
    average = jnp.mean(values, -1, keepdims=True)
    centred = values - average
    spread = jnp.mean(centred * centred, -1, keepdims=True)
    inverse = lax.rsqrt(spread + norm_eps)
    return (centred * inverse, inverse)


def norm_back(grad_hat, normed, inverse):
    first_mean = jnp.mean(grad_hat, -1, keepdims=True)
    cross_mean = jnp.mean(grad_hat * normed, -1, keepdims=True)
    return (grad_hat - first_mean - normed * cross_mean) * inverse


def adamw(master, first, second, gradient, rate, decay):
    first_new = beta_one * first + (1.0 - beta_one) * gradient
    second_new = beta_two * second + (1.0 - beta_two) * gradient * gradient
    first_hat = first_new / (1.0 - beta_one**step_count)
    second_hat = second_new / (1.0 - beta_two**step_count)
    master_new = master - rate * (first_hat / (jnp.sqrt(second_hat) + adam_eps) + decay * master)
    return (master_new, first_new, second_new)


def swap(value, axis, size, mask):
    return lax.ppermute(value, axis, [(i, i ^ mask) for i in range(size)])


def bit_count(size):
    bits = size.bit_length() - 1
    assert size == 1 << bits
    return bits


def batch_rounds(bits):
    if bits == 3:
        return [(1, 2), (0,)]
    return [(b,) for b in range(1, bits)] + [(0,)]


def gather_blocks(block, sizes, place):
    batch_size, pos_size = sizes
    b, z = place
    rows, cols = block.shape
    bits = bit_count(batch_size)
    zbits = bit_count(pos_size)
    total = bits + zbits
    held = block.reshape((1,) * total + (rows, cols))

    def exchange(held, axis_name, size, index, group, shift):
        pieces = [held]
        for g in range(1, 1 << len(group)):
            mask = sum((1 << group[i]) for i in range(len(group)) if (g >> i) & 1)
            pieces.append(swap(held, axis_name, size, mask))
        for bit in group:
            axis = total - 1 - (bit + shift)
            mine = (index >> bit) & 1
            merged = []
            for a, c in zip(pieces[0::2], pieces[1::2]):
                merged.append(
                    jnp.where(
                        mine == 0,
                        jnp.concatenate([a, c], axis),
                        jnp.concatenate([c, a], axis),
                    )
                )
            pieces = merged
        return pieces[0]

    for bit in reversed(range(zbits)):
        held = exchange(held, "pos", pos_size, z, (bit,), 0)
    for group in batch_rounds(bits):
        held = exchange(held, "batch", batch_size, b, group, zbits)
    return held.reshape(batch_size * pos_size * rows, cols)


def reduce_blocks(grad, sizes, place, late=None):
    batch_size, pos_size = sizes
    b, z = place
    bits = bit_count(batch_size)
    zbits = bit_count(pos_size)
    total = bits + zbits
    rows = grad.shape[0] // (batch_size * pos_size)
    held = grad.reshape((2,) * total + (rows, -1))
    if late is not None:
        late = late.reshape((2,) * total + (rows, -1))

    def halve(held, axis_name, size, index, group, shift):
        parts = {0: held}
        for i, bit in enumerate(group):
            axis = total - 1 - (bit + shift)
            mine = (index >> bit) & 1
            spread = {}
            for g, part in parts.items():
                spread[g] = lax.dynamic_slice_in_dim(part, mine, 1, axis)
                spread[g | (1 << i)] = lax.dynamic_slice_in_dim(part, 1 - mine, 1, axis)
            parts = spread
        summed = parts[0].astype(wide)
        for g, part in parts.items():
            if g:
                mask = sum((1 << group[i]) for i in range(len(group)) if (g >> i) & 1)
                summed = summed + swap(part, axis_name, size, mask).astype(wide)
        return summed.astype(grad.dtype)

    for group in reversed(batch_rounds(bits)):
        held = halve(held, "batch", batch_size, b, group, zbits)
        if late is not None:
            late = halve(late, "batch", batch_size, b, group, zbits)
            held = jnp.concatenate([held, late], total + 1)
            late = None
    for bit in range(zbits):
        held = halve(held, "pos", pos_size, z, (bit,), 0)
    return held.reshape(rows, -1)


CHUNK = 512

lengths = (D, D, HID, GATE, GATE, SEQ, D)
ends = [sum(lengths[: i + 1]) for i in range(len(lengths))]
GAIN_IN, BIAS_IN, BIAS_HIDDEN, GAIN_GATE, BIAS_GATE, BIAS_SPATIAL, BIAS_OUT = (
    slice(end - n, end) for end, n in zip(ends, lengths)
)
VEC = ends[-1]


def shifted(outer, inner):
    return slice(outer.start + inner.start, outer.start + inner.stop)


tail_slope = 0.39 / math.sqrt(2.0)
tail_series = (
    0.23532609033994684,
    0.09138275083966492,
    0.6495739793206253,
    -0.6354188599562557,
    0.8866760936996321,
    -0.22754005589281026,
)
exp_scale = -0.5 / math.log(2.0)
density = 1.0 / math.sqrt(2.0 * math.pi)


def gelu_and_slope(v):
    size = jnp.abs(v)
    t = 1.0 / (1.0 + tail_slope * size)
    bell = jnp.exp2(exp_scale * (v * v))
    series = 0.5 * tail_series[-1]
    for c in reversed(tail_series[:-1]):
        series = series * t + 0.5 * c
    tail = series * t * bell
    phi = jnp.where(v > 0, 1.0 - tail, tail)
    return v * phi, phi + (density * v) * bell


def dot(a, b, ca=1, cb=0):
    return lax.dot_general(a, b, (((ca,), (cb,)), ((), ())), preferred_element_type=wide)


def column_blocks(k):
    return slice(k * CHUNK, (k + 1) * CHUNK)


def block_at(z, k, size, base=0):
    return pl.ds(pl.multiple_of(base + (z ^ k) * size, LANE), size)


def project_kernel(pos_size, *refs):
    pieces = refs[:pos_size]
    (w_ref, vec, x_ref, scaled_ref, left_ref, slope_ref, normed_ref, inverse_ref, gate_ref, half_ref) = refs[
        pos_size:
    ]
    mine, _, length, _ = x_ref.shape
    total = mine * length
    for k in range(pos_size):

        @pl.when(pl.program_id(0) == k)
        def _():
            x_ref[:, 0] = pieces[k][...]

    normed, _ = norm_parts(x_ref[:, 0].reshape(total, D).astype(wide))
    scaled = (normed * vec[:, GAIN_IN] + vec[:, BIAS_IN]).astype(low_type)
    scaled_ref[:, 0] = scaled.reshape(mine, length, D)

    def part(step, base):
        at = pl.multiple_of(step * CHUNK, CHUNK)
        cols = pl.ds(pl.multiple_of(base + at, CHUNK), CHUNK)
        bias = vec[:, pl.ds(pl.multiple_of(BIAS_HIDDEN.start + base + at, CHUNK), CHUNK)]
        value, slope = gelu_and_slope(dot(scaled, w_ref[:, cols]) + bias)
        slope_ref[:, 0, :, cols] = slope.astype(low_type).reshape(mine, length, CHUNK)
        return pl.ds(at, CHUNK), value

    def body(step, carry):
        cols, value = part(step, 0)
        left_ref[:, 0, :, cols] = value.astype(low_type).reshape(mine, length, CHUNK)
        cols, value = part(step, GATE)
        half_ref[:, cols] = value
        return carry

    lax.fori_loop(0, GATE // CHUNK, body, 0)
    normed_gate, inverse = norm_parts(half_ref[...])
    inverse_ref[:, 0] = inverse.reshape(mine, length, 1)
    normed_ref[:, 0] = normed_gate.astype(low_type).reshape(mine, length, GATE)
    gate = (normed_gate * vec[:, GAIN_GATE] + vec[:, BIAS_GATE]).astype(low_type)
    gate_ref[:, 0] = gate.reshape(mine, length, GATE)


def mix_kernel(pos_size, *refs):
    (x_ref, seg_ref, pad_ref, skip_ref, ws_ref, wo_ref, vec, left_ref, gate_ref) = refs[:9]
    mixed_refs = refs[9 : 9 + pos_size]
    spatial_ref, gated_ref, mixing_ref, col_ref, line_ref = refs[9 + pos_size :]
    z = lax.axis_index("pos")
    row = z * pl.num_programs(0) + pl.program_id(0)
    length = x_ref.shape[1]
    part = length // pos_size
    places = range(pos_size)

    def line(ref):
        rows = jnp.concatenate([ref[:, block_at(z, k, part)] for k in places], 1)
        at = lax.broadcasted_iota(jnp.int32, rows.shape, 0)
        return jnp.sum(jnp.where(at == row, rows.astype(wide), 0.0), 0, keepdims=True)

    segment = line(seg_ref)
    padding = line(pad_ref)
    keep = padding * (1.0 - skip_ref[row].astype(wide))
    key = jnp.where(padding == 1.0, segment, -1.0)
    bias = jnp.concatenate([vec[:, block_at(z, k, part, BIAS_SPATIAL.start)] for k in places], 1)
    lines = jnp.concatenate([segment, keep, bias, key, jnp.zeros((4, length), wide)], 0)
    col = lines.T
    line_ref[0] = lines
    col_ref[0] = col
    weights = jnp.concatenate(
        [
            jnp.concatenate([ws_ref[block_at(z, i, part), block_at(z, j, part)] for j in places], 1)
            for i in places
        ],
        0,
    )
    masked = jnp.where(col[:, 0:1] == key, weights.astype(wide), 0.0)
    mixing = masked.astype(low_type)
    mixing_ref[0] = masked.T.astype(low_type)
    branch = jnp.zeros(x_ref.shape[1:], wide)
    for c in range(GATE // CHUNK):
        cols = column_blocks(c)
        spatial = dot(mixing, gate_ref[0, :, cols]) + col[:, 2:3]
        gated = (left_ref[0, :, cols].astype(wide) * spatial).astype(low_type)
        spatial_ref[0, :, cols] = spatial.astype(low_type)
        gated_ref[0, :, cols] = gated
        branch = branch + dot(gated, wo_ref[cols, :])
    mixed = (x_ref[0].astype(wide) + col[:, 1:2] * (branch + vec[:, BIAS_OUT])).astype(low_type)
    for k in places:
        mixed_refs[k][0] = mixed[k * part : (k + 1) * part]


def back_kernel(pos_size, *refs):
    cot_refs = refs[:pos_size]
    (
        col_ref, line_ref, mixing_ref, wo_ref, vec, left_ref, gate_ref, normed_ref, inverse_ref,
        spatial_ref, gated_ref, slope_ref, pre_ref, dwo_ref, dws_ref, dvec, dwo_acc, dws_acc, gate_acc,
    ) = refs[pos_size:]
    row = pl.program_id(0)
    z = lax.axis_index("pos")

    @pl.when(row == 0)
    def _():
        for ref in (dwo_acc, dws_acc, dvec):
            ref[...] = jnp.zeros_like(ref)

    col = col_ref[0]
    same = col[:, 0:1] == line_ref[0][3:4]
    mixing_back = mixing_ref[0]
    cot = jnp.concatenate([ref[0] for ref in cot_refs], 0)
    grad_branch = cot.astype(wide) * col[:, 1:2]
    dvec[:, BIAS_OUT] += jnp.sum(grad_branch, 0, keepdims=True)
    branch_low = grad_branch.astype(low_type)
    length = branch_low.shape[0]
    part = length // pos_size
    products = jnp.zeros((length, length), wide)
    first = jnp.zeros((length, 1), wide)
    cross = jnp.zeros((length, 1), wide)
    spatial_bias = jnp.zeros((8, length), wide)
    ones = jnp.ones((8, CHUNK), low_type)
    for c in range(GATE // CHUNK):
        cols = column_blocks(c)
        grad_gated = dot(branch_low, wo_ref[cols, :], 1, 1)
        dwo_acc[cols, :] += dot(gated_ref[0, :, cols], branch_low, 0, 0)
        spatial_low = (grad_gated * left_ref[0, :, cols].astype(wide)).astype(low_type)
        spatial_bias = spatial_bias + dot(ones, spatial_low, 1, 1)
        pre = (grad_gated * spatial_ref[0, :, cols].astype(wide)) * slope_ref[0, :, cols].astype(wide)
        pre_ref[0, :, cols] = pre.astype(low_type)
        dvec[:, shifted(BIAS_HIDDEN, cols)] += jnp.sum(pre, 0, keepdims=True)
        products = products + dot(spatial_low, gate_ref[0, :, cols], 1, 1)
        grad_gate = dot(mixing_back, spatial_low)
        normed = normed_ref[0, :, cols].astype(wide)
        dvec[:, shifted(GAIN_GATE, cols)] += jnp.sum(grad_gate * normed, 0, keepdims=True)
        dvec[:, shifted(BIAS_GATE, cols)] += jnp.sum(grad_gate, 0, keepdims=True)
        grad_hat = grad_gate * vec[:, shifted(GAIN_GATE, cols)]
        gate_acc[:, cols] = grad_hat
        first = first + jnp.sum(grad_hat, 1, keepdims=True)
        cross = cross + jnp.sum(grad_hat * normed, 1, keepdims=True)
    for k in range(pos_size):
        dvec[:, block_at(z, k, part, BIAS_SPATIAL.start)] += spatial_bias[0:1, k * part : (k + 1) * part]
    dws_acc[...] += jnp.where(same, products, 0.0)
    first = first * (1.0 / GATE)
    cross = cross * (1.0 / GATE)
    inverse = inverse_ref[0]
    for c in range(GATE // CHUNK):
        cols = column_blocks(c)
        rest = shifted(slice(GATE, HID), cols)
        normed = normed_ref[0, :, cols].astype(wide)
        grad_right = (gate_acc[:, cols] - first - normed * cross) * inverse
        pre = grad_right * slope_ref[0, :, rest].astype(wide)
        pre_ref[0, :, rest] = pre.astype(low_type)
        dvec[:, shifted(BIAS_HIDDEN, rest)] += jnp.sum(pre, 0, keepdims=True)

    @pl.when(row == pl.num_programs(0) - 1)
    def _():
        dwo_ref[...] = dwo_acc[...].astype(low_type)
        for i in range(pos_size):
            for j in range(pos_size):
                dws_ref[block_at(z, i, part), block_at(z, j, part)] = dws_acc[
                    i * part : (i + 1) * part, j * part : (j + 1) * part
                ].astype(low_type)


def input_kernel(pos_size, pre_ref, w_ref, x_ref, vec, dvec_in, *refs):
    pieces, dvec = refs[:pos_size], refs[pos_size]
    step = pl.program_id(0)
    mine, _, length, _ = x_ref.shape
    total = mine * length

    @pl.when(step == 0)
    def _():
        dvec[...] = dvec_in[...]

    normed, inverse = norm_parts(x_ref[:, 0].reshape(total, D).astype(wide))
    grad_scaled = dot(pre_ref[:, 0].reshape(total, HID), w_ref[...], 1, 1)
    dvec[:, GAIN_IN] += jnp.sum(grad_scaled * normed, 0, keepdims=True)
    dvec[:, BIAS_IN] += jnp.sum(grad_scaled, 0, keepdims=True)
    grad = norm_back(grad_scaled * vec[:, GAIN_IN], normed, inverse).astype(low_type)
    for k in range(pos_size):

        @pl.when(step == k)
        def _():
            pieces[k][...] = grad.reshape(mine, length, D)


def whole(*shape):
    return pl.BlockSpec(shape, lambda r: (0,) * len(shape))


def per_row(*shape):
    return pl.BlockSpec((1,) + shape, lambda r: (r,) + (0,) * len(shape))


def shaped(dtype, *shape):
    return jax.ShapeDtypeStruct(shape, dtype)


def cost(flops, size, rare=0):
    return pl.CostEstimate(flops=flops, transcendentals=rare, bytes_accessed=size)


def project(pieces, w, vec):
    pos_size = len(pieces)
    mine, length, _ = pieces[0].shape
    block = lambda n: pl.BlockSpec((mine, 1, length, n), lambda i: (0, i, 0, 0))
    out = lambda dtype, n: shaped(dtype, mine, pos_size, length, n)
    total = mine * pos_size * length
    return pl.pallas_call(
        functools.partial(project_kernel, pos_size),
        grid=(pos_size,),
        in_specs=[whole(mine, length, D)] * pos_size + [whole(D, HID), whole(1, VEC)],
        out_specs=[block(D), block(D), block(GATE), block(HID), block(GATE), block(1), block(GATE)],
        out_shape=[
            out(low_type, D), out(low_type, D), out(low_type, GATE), out(low_type, HID),
            out(low_type, GATE), out(wide, 1), out(low_type, GATE),
        ],
        scratch_shapes=[pltpu.VMEM((mine * length, GATE), wide)],
        cost_estimate=cost(2 * total * D * HID + 40 * total * HID, 20 << 20, 2 * total * HID),
        name="project",
    )(*pieces, w, vec)


def mix(pos_size, x, seg, pad, skip, ws, wo, vec, left, gate):
    mine, length, _ = x.shape
    part = length // pos_size
    return pl.pallas_call(
        functools.partial(mix_kernel, pos_size),
        grid=(mine,),
        in_specs=[
            per_row(length, D), whole(*seg.shape), whole(*pad.shape), pl.BlockSpec(memory_space=pltpu.SMEM),
            whole(length, length), whole(GATE, D), whole(1, VEC), per_row(length, GATE), per_row(length, GATE),
        ],
        out_specs=[per_row(part, D)] * pos_size
        + [
            per_row(length, GATE), per_row(length, GATE), per_row(length, length), per_row(length, 8),
            per_row(8, length),
        ],
        out_shape=[shaped(low_type, mine, part, D)] * pos_size
        + [
            shaped(low_type, mine, length, GATE),
            shaped(low_type, mine, length, GATE),
            shaped(low_type, mine, length, length),
            shaped(wide, mine, length, 8),
            shaped(wide, mine, 8, length),
        ],
        cost_estimate=cost(4 * mine * length * GATE * D, 16 << 20),
        name="mix",
    )(x, seg, pad, skip, ws, wo, vec, left, gate)


def back(pieces, col, line, mixing, wo, vec, left, gate, normed, inverse, spatial, gated, slope):
    pos_size = len(pieces)
    mine, part, _ = pieces[0].shape
    length = part * pos_size
    return pl.pallas_call(
        functools.partial(back_kernel, pos_size),
        grid=(mine,),
        in_specs=[per_row(part, D)] * pos_size
        + [
            per_row(length, 8), per_row(8, length), per_row(length, length), whole(GATE, D), whole(1, VEC),
            per_row(length, GATE), per_row(length, GATE), per_row(length, GATE), per_row(length, 1),
            per_row(length, GATE), per_row(length, GATE), per_row(length, HID),
        ],
        out_specs=[per_row(length, HID), whole(GATE, D), whole(length, length), whole(1, VEC)],
        out_shape=[
            shaped(low_type, mine, length, HID),
            shaped(low_type, GATE, D),
            shaped(low_type, length, length),
            shaped(wide, 1, VEC),
        ],
        scratch_shapes=[
            pltpu.VMEM((GATE, D), wide),
            pltpu.VMEM((length, length), wide),
            pltpu.VMEM((length, GATE), wide),
        ],
        cost_estimate=cost(8 * mine * length * GATE * D, 30 << 20),
        name="back",
    )(*pieces, col, line, mixing, wo, vec, left, gate, normed, inverse, spatial, gated, slope)


def input_back(pre, w, x, vec, dvec):
    mine, pos_size, length, _ = x.shape
    block = lambda n: pl.BlockSpec((mine, 1, length, n), lambda i: (0, i, 0, 0))
    return pl.pallas_call(
        functools.partial(input_kernel, pos_size),
        grid=(pos_size,),
        in_specs=[block(HID), whole(D, HID), block(D), whole(1, VEC), whole(1, VEC)],
        out_specs=[whole(mine, length, D)] * pos_size + [whole(1, VEC)],
        out_shape=[shaped(low_type, mine, length, D)] * pos_size + [shaped(wide, 1, VEC)],
        cost_estimate=cost(2 * mine * pos_size * length * D * HID, 12 << 20),
        name="input_back",
    )(pre, w, x, vec, dvec)


def local_fn(sizes):
    batch_size, pos_size = sizes

    def local(
        tokens,
        cotangent,
        segment_ids,
        pad_mask,
        skip_flags,
        in_master,
        spatial_master,
        out_master,
        vector_master,
        in_first,
        spatial_first,
        out_first,
        vector_first,
        in_second,
        spatial_second,
        out_second,
        vector_second,
    ):
        b = lax.axis_index("batch")
        z = lax.axis_index("pos")
        place = (b, z)
        devices = batch_size * pos_size
        rows = tokens.shape[0]
        length = tokens.shape[1]
        mine = rows // pos_size

        def exchange(parts):
            return [part if k == 0 else swap(part, "pos", pos_size, k) for k, part in enumerate(parts)]

        def split_rows(value):
            return [lax.dynamic_slice_in_dim(value, (z ^ k) * mine, mine, 0) for k in range(pos_size)]

        def join_rows(parts):
            for bit in range(bit_count(pos_size)):
                lower = ((z >> bit) & 1) == 0
                parts = [
                    jnp.where(
                        lower, jnp.concatenate([u, v], 0), jnp.concatenate([v, u], 0)
                    )
                    for u, v in zip(parts[0::2], parts[1::2])
                ]
            return parts[0]

        in_rows = D // devices if D % devices == 0 else 1
        in_block = in_master.astype(low_type).reshape(in_rows, -1)
        vector_block = vector_master.astype(low_type).reshape(in_rows, -1)
        vector_cols = vector_block.shape[1]
        vector_block = jnp.pad(vector_block, ((0, 0), (0, LANE - vector_cols)))
        in_block = jnp.concatenate([in_block, vector_block], 1)
        spatial_block = spatial_master.astype(low_type).reshape(-1, D)
        out_block = out_master.astype(low_type).reshape(-1, D)
        rest_block = jnp.concatenate([spatial_block, out_block], 0)
        spatial_rows = spatial_block.shape[0]
        in_width = in_master.shape[0] // in_rows

        in_all = gather_blocks(in_block, sizes, place)
        token_parts = exchange(split_rows(tokens))
        rest_all = gather_blocks(rest_block, sizes, place).reshape(devices, -1, D)
        back_parts = exchange(split_rows(cotangent))

        vec = in_all[:, in_width : in_width + vector_cols].reshape(1, -1).astype(wide)
        weight_spatial = rest_all[:, :spatial_rows].reshape(SEQ, SEQ)
        weight_out = rest_all[:, spatial_rows:].reshape(GATE, D)
        saved = project(token_parts, in_all, vec)
        inputs = saved[0]
        by_row = lambda value: value.reshape(mine, SEQ, -1)
        inputs_low, scaled_in, left_half, slope, normed_gate, inverse_gate, gate_low = map(by_row, saved)
        outs = mix(
            pos_size, inputs_low, segment_ids, pad_mask, skip_flags, weight_spatial, weight_out, vec,
            left_half, gate_low,
        )
        mixed_parts = exchange(outs[:pos_size])
        mixed = join_rows(mixed_parts)
        spatial, gated, mixing, col, line = outs[pos_size:]
        pre_low, grad_weight_out, grad_weight_spatial, grad_vector = back(
            back_parts, col, line, mixing, weight_out, vec, left_half, gate_low, normed_gate,
            inverse_gate, spatial, gated, slope,
        )
        scaled_in = scaled_in.reshape(-1, D)
        pre_low = pre_low.reshape(-1, HID)

        grad_rest = jnp.concatenate(
            [
                grad_weight_spatial.reshape(devices, spatial_rows, D),
                grad_weight_out.reshape(devices, -1, D),
            ],
            1,
        )
        rest_sum = reduce_blocks(grad_rest.reshape(-1, D), sizes, place)

        grad_weight_in = jnp.einsum("td,th->dh", scaled_in, pre_low, preferred_element_type=wide)
        grad_weight_in = grad_weight_in.astype(low_type)
        grad_weight_in, pre_low = lax.optimization_barrier((grad_weight_in, pre_low))
        outs = input_back(
            pre_low.reshape(mine, pos_size, length, HID), in_all, inputs, vec, grad_vector
        )
        grad_parts = exchange(outs[:pos_size])
        input_grad = cotangent.astype(wide) + join_rows(grad_parts).astype(wide)
        grad_vector = outs[pos_size]

        vector_part = grad_vector.astype(low_type).reshape(in_rows * devices, -1)
        vector_part = jnp.pad(vector_part, ((0, 0), (0, LANE - vector_cols)))
        in_part = grad_weight_in.reshape(in_rows * devices, -1)
        in_sum = reduce_blocks(in_part, sizes, place, vector_part)

        shards = (
            in_sum[:, :in_width].reshape(-1).astype(wide),
            rest_sum[:spatial_rows].reshape(-1).astype(wide),
            rest_sum[spatial_rows:].reshape(-1).astype(wide),
            in_sum[:, in_width : in_width + vector_cols].reshape(-1).astype(wide),
        )
        in_new = adamw(in_master, in_first, in_second, shards[0], rate_in, decay_matrix)
        spatial_new = adamw(
            spatial_master, spatial_first, spatial_second, shards[1], rate_spatial, decay_matrix
        )
        out_new = adamw(out_master, out_first, out_second, shards[2], rate_out, decay_matrix)
        vector_new = adamw(vector_master, vector_first, vector_second, shards[3], rate_vector, 0.0)
        return (
            mixed,
            input_grad,
            in_new[0],
            in_new[1],
            in_new[2],
            spatial_new[0],
            spatial_new[1],
            spatial_new[2],
            out_new[0],
            out_new[1],
            out_new[2],
            vector_new[0],
            vector_new[1],
            vector_new[2],
        )

    return local


def solution(mesh):
    sizes = (mesh.shape["batch"], mesh.shape["pos"])
    flat = P(("batch", "pos"))
    acts = P("batch", "pos", None)
    placed = (acts, acts, P("batch", None), P("batch", None), P("batch")) + (flat,) * 12
    return jax.shard_map(
        local_fn(sizes),
        mesh=mesh,
        in_specs=placed,
        out_specs=(acts, acts) + (flat,) * 12,
        check_vma=False,
    )
```

time: 321 us -> 255 us (0.79); the launches traced: 316 us -> 254 us
  matrix products: 73.2 us -> 7.65 us
  Pallas kernels: 0 us -> 60.5 us
  other arithmetic: 67.3 us -> 22.7 us
  local copies, waits for them, and re-layouts: 20.8 us -> 10.8 us
    dot_general x8 -> x0, matrix products: 68 us -> none  [the longest x1 33.2 us: local(): jnp.dot(scaled_in, weight_in, preferred_element_type=wide) + bias_hidden]
    pallas_call x0 -> x4, Pallas kernels: none -> 60.5 us  [the longest x1 22.6 us: project(): pl.pallas_call(functools.partial(project_kernel, pos_size), grid=(pos_siz...]
    reduce_sum x7 -> x0, other arithmetic: 21.7 us -> none  [the longest x1 14.1 us: local(): grad_bias_hidden = jnp.sum(grad_pre, 0)]
    mul x3 -> x0, other arithmetic: 20.7 us -> none  [the longest x1 11.9 us: local(): grad_left = grad_gated * spatial]
    unnamed x107 -> x58, local copies, waits for them, and re-layouts: 11.3 us -> 2.72 us
    select_n x8, other arithmetic: 1.97 us -> 6.59 us  [exchange(): jnp.where(mine == 0, jnp.concatenate([a, c], axis), jnp.concatenate([c, a...]
    concatenate x10 -> x2, other arithmetic: 5.3 us -> 1.16 us  [the longest x1 1.05 us: local(): jnp.concatenate([grad_weight_spatial.reshape(devices, spatial_rows, D), g...]
    select_n x0 -> x5, other arithmetic: none -> 3.53 us  [join_rows(): jnp.where(lower, jnp.concatenate([u, v], 0), jnp.concatenate([v, u], 0))]
  transfers between devices with their start and end apart: 36 -> 37, of which waited for: 14 -> 21; matrix products, arithmetic and copies ran while one was open for 10% -> 13% of each run, Pallas kernels for 0% -> 24%
where the time goes in v3:
time: 255 us; the launch traced here: 254 us
  waiting for transfers between devices  97.2 us (38%)
  Pallas kernels  60.5 us (24%)
  starting transfers between devices  54.2 us (21%)
  other arithmetic  22.7 us (9%)
  local copies, waits for them, and re-layouts  10.8 us (4%)
  matrix products  7.65 us (3%)
    ppermute x37, waiting for transfers between devices, swap(): return lax.ppermute(value, axis, [(i, i ^ mask) for i in range(size)])  97.2 us
    ppermute x37, starting transfers between devices, swap(): return lax.ppermute(value, axis, [(i, i ^ mask) for i in range(size)])  54.2 us
    pallas_call x1, Pallas kernels, project(): pl.pallas_call(functools.partial(project_kernel, pos_size), grid=(pos_siz...  22.6 us
    pallas_call x1, Pallas kernels, back(): pl.pallas_call(functools.partial(back_kernel, pos_size), grid=(mine,), in...  19.4 us
    pallas_call x1, Pallas kernels, mix(): pl.pallas_call(functools.partial(mix_kernel, pos_size), grid=(mine,), in_...  9.53 us
    pallas_call x1, Pallas kernels, input_back(): pl.pallas_call(functools.partial(input_kernel, pos_size), grid=(pos_size,...  8.93 us
    dot_general x1, matrix products, local(): jnp.einsum('td,th->dh', scaled_in, pre_low, preferred_element_type=wide)  7.65 us
    select_n x8, other arithmetic, exchange(): jnp.where(mine == 0, jnp.concatenate([a, c], axis), jnp.concatenate([c, a...  6.59 us
  transfers between devices with their start and end apart: 37, of which 21 were waited for; matrix products, arithmetic and copies ran while one was open for 13% of the time, Pallas kernels for 24%

profile of v3, /device:TPU:0, one launch (start us, length us, event | category | flops | bytes accessed | tf_op | source)
XLA Modules:
  0.0 254.4 jit_solution(2029124326179889404)
XLA Ops:
  2.4 4.1 %collective-permute-start.9 = (bf16[1,1,1,1,1,64,512]{6,5,4,3,2,1,0:T(8,128)(2,1)S(1)}, bf16[1,1,1,1,1,64,512]{6,5,4,3,2,1,0:T(8,128)(2,1)S(1)}, u32[]{:S(2)}, u32[]{:S(2)}) collective-permute-start(bf16[1,1,1,1,1,64,512]{6,5,4,3,2,1,0:T(8,128)(2,1)S(1)} %bitcast.101), channel_id=1, source_target_pairs={{0,2},{1,3},{2,0},{3,1},{4,6},{5,7},{6,4},{7,5},{8,10},{9,11},{10,... | collective-permute-start | bytes 196616 | tf_op jit(solution)/shard_map/ppermute | solution.py:57
  10.2 3.3 %collective-permute-start.10 = (bf16[1,1,1,2,1,64,512]{6,5,3,4,2,1,0:T(8,128)(2,1)S(1)}, bf16[1,1,1,2,1,64,512]{6,5,3,4,2,1,0:T(8,128)(2,1)S(1)}, u32[]{:S(2)}, u32[]{:S(2)}) collective-permute-start(bf16[1,1,1,2,1,64,512]{6,5,3,4,2,1,0:T(8,128)(2,1)S(1)} %fusion.15), channel_id=1, source_target_pairs={{0,1},{1,0},{2,3},{3,2},{4,5},{5,4},{6,7},{7,6},{8,9},{9,8},{10,11... | collective-permute-start | bytes 393224 | tf_op jit(solution)/shard_map/ppermute | solution.py:57
  13.5 2.4 collective-permute-done.3
  16.1 2.6 %collective-permute-done.10 = bf16[1,1,1,2,1,64,512]{6,5,3,4,2,1,0:T(8,128)(2,1)S(1)} collective-permute-done((bf16[1,1,1,2,1,64,512]{6,5,3,4,2,1,0:T(8,128)(2,1)S(1)}, bf16[1,1,1,2,1,64,512]{6,5,3,4,2,1,0:T(8,128)(2,1)S(1)}, u32[]{:S(2)}, u32[]{:S(2)}) %collective-permute-start.10) | collective-permute-done | bytes 131104 | tf_op jit(solution)/shard_map/ppermute | solution.py:57
  18.7 2.4 collective-permute-start.13
  22.5 2.4 collective-permute-start.7
  25.5 17.2 %collective-permute-done.7 = bf16[1,1,1,2,2,16,3200]{6,5,4,3,2,1,0:T(8,128)(2,1)S(1)} collective-permute-done((bf16[1,1,1,2,2,16,3200]{6,5,4,3,2,1,0:T(8,128)(2,1)S(1)}, bf16[1,1,1,2,2,16,3200]{6,5,4,3,2,1,0:T(8,128)(2,1)S(1)}, u32[]{:S(2)}, u32[]{:S(2)}) %collective-permute-start.7) | collective-permute-done | bytes 409632 | tf_op jit(solution)/shard_map/ppermute | solution.py:57
  42.6 5.8 %collective-permute-done.6 = bf16[1,1,1,2,2,16,3200]{6,5,4,3,2,1,0:T(8,128)(2,1)S(1)} collective-permute-done((bf16[1,1,1,2,2,16,3200]{6,5,4,3,2,1,0:T(8,128)(2,1)S(1)}, bf16[1,1,1,2,2,16,3200]{6,5,4,3,2,1,0:T(8,128)(2,1)S(1)}, u32[]{:S(2)}, u32[]{:S(2)}) %collective-permute-start.6) | collective-permute-done | bytes 409632 | tf_op jit(solution)/shard_map/ppermute | solution.py:57
  52.9 2.1 constant_dynamic-slice_fusion.13
  56.9 2.5 collective-permute-start.2
  60.4 2.5 maximum_select_fusion.1
  67.0 2.5 maximum_select_fusion
  72.0 2.5 collective-permute-start.20
  74.4 2.3 collective-permute-done.1.refs_2_
  76.7 22.6 %project.1 = (bf16[2,4,128,512]{3,2,1,0:T(8,128)(2,1)}, bf16[2,4,128,512]{3,2,1,0:T(8,128)(2,1)}, bf16[2,4,128,1536]{3,2,1,0:T(8,128)(2,1)}, bf16[2,4,128,3072]{...) custom-call(bf16[2,128,512]{2,1,0:T(8,128)(2,1)} %get-tuple-element., ...), custom_call_target="tpu_custom_call" | custom-call | flops 3347054592 | bytes 20971520 | tf_op jit(solution)/shard_map/project/pallas_call | solution.py:400
  99.3 9.5 %mix.1 = (bf16[2,128,512]{2,1,0:T(8,128)(2,1)}, bf16[2,128,512]{2,1,0:T(8,128)(2,1)}, bf16[2,128,512]{2,1,0:T(8,128)(2,1)}, bf16[2,128,512]{2,1,0:T(8,128)(2,1)}...) custom-call(bf16[2,512,512]{2,1,0:T(8,128)(2,1)} %bitcast.111, ...), custom_call_target="tpu_custom_call" | custom-call | flops 3221225472 | bytes 16777216 | tf_op jit(solution)/shard_map/mix/pallas_call | solution.py:418
  111.4 19.4 %back.1 = (bf16[2,512,3072]{2,1,0:T(8,128)(2,1)}, bf16[1536,512]{1,0:T(8,128)(2,1)}, bf16[512,512]{1,0:T(8,128)(2,1)}, f32[1,8192]{1,0:T(1,128)}) custom-call(bf16[2,128,512]{2,1,0:T(8,128)(2,1)} %get-tuple-element.88.refs_0_, bf16[2,128,512]{2,1,0:T(8,128)(2,1)} %copy-done.7, bf16[2,128,512]{2,1,0:T(8,128)(2,1)} %copy-done.8, ...), custom_call_target="tpu_custom_call" | custom-call | flops 6442450944 | bytes 31457280 | tf_op jit(solution)/shard_map/back/pallas_call | solution.py:447
  130.8 7.7 %convolution_convert_fusion = bf16[512,3072]{1,0:T(8,128)(2,1)} fusion(bf16[1024,512]{1,0:T(8,128)(2,1)S(1)} %bitcast.112, bf16[1024,3072]{1,0:T(8,128)(2,1)} %bitcast.109), kind=kOutput, calls=%fused_computation | convolution fusion | flops 3222798336 | bytes 10485760 | tf_op jit(solution)/shard_map/td,th->dh/dot_general | solution.py:581
  138.5 8.9 %input_back.1 = (bf16[2,128,512]{2,1,0:T(8,128)(2,1)}, bf16[2,128,512]{2,1,0:T(8,128)(2,1)}, bf16[2,128,512]{2,1,0:T(8,128)(2,1)}, bf16[2,128,512]{2,1,0:T(8,128)(2,1)}, f32[1,8192]{1,0:T(1,128)}) custom-call(bf16[2,4,128,3072]{3,2,1,0:T(8,128)(2,1)} %bitcast.110, bf16[512,3200]{1,0:T(8,128)(2,1)} %bitcast.79, ...), custom_call_target="tpu_custom_call" | custom-call | flops 3221225472 | bytes 12582912 | tf_op jit(solution)/shard_map/input_back/pallas_call | solution.py:476
  147.4 2.3 collective-permute-start.23
  149.7 15.7 %collective-permute-start.22 = (bf16[2,128,512]{2,1,0:T(8,128)(2,1)}, bf16[2,128,512]{2,1,0:T(8,128)(2,1)}, u32[]{:S(2)}, u32[]{:S(2)}) collective-permute-start(bf16[2,128,512]{2,1,0:T(8,128)(2,1)} %get-tuple-element.62), channel_id=1, source_target_pairs={{0,2},{1,3},{2,0},{3,1},{4,6},{5,7},{6,4},{7,5},{8,10},{9,11},{10,... | collective-permute-start | bytes 786440 | tf_op jit(solution)/shard_map/ppermute | solution.py:57
  169.7 11.2 %collective-permute-done.22 = bf16[2,128,512]{2,1,0:T(8,128)(2,1)} collective-permute-done((bf16[2,128,512]{2,1,0:T(8,128)(2,1)}, bf16[2,128,512]{2,1,0:T(8,128)(2,1)}, u32[]{:S(2)}, u32[]{:S(2)}) %collective-permute-start.22) | collective-permute-done | bytes 262176 | tf_op jit(solution)/shard_map/ppermute | solution.py:57
  185.2 2.5 collective-permute-start.34
  190.5 4.9 %collective-permute-done.34 = bf16[1,1,1,2,2,64,512]{6,5,4,3,2,1,0:T(8,128)(2,1)S(1)} collective-permute-done((bf16[1,1,1,2,2,64,512]{6,5,4,3,2,1,0:T(8,128)(2,1)S(1)}, bf16[1,1,1,2,2,64,512]{6,5,4,3,2,1,0:T(8,128)(2,1)S(1)}, u32[]{:S(2)}, u32[]{:S(2)}) %collective-permute-start.34) | collective-permute-done | bytes 262176 | tf_op jit(solution)/shard_map/ppermute | solution.py:57
  195.7 3.7 %collective-permute-done.33 = bf16[1,1,1,2,2,64,512]{6,5,4,3,2,1,0:T(8,128)(2,1)S(1)} collective-permute-done((bf16[1,1,1,2,2,64,512]{6,5,4,3,2,1,0:T(8,128)(2,1)S(1)}, bf16[1,1,1,2,2,64,512]{6,5,4,3,2,1,0:T(8,128)(2,1)S(1)}, u32[]{:S(2)}, u32[]{:S(2)}) %collective-permute-start.33) | collective-permute-done | bytes 262176 | tf_op jit(solution)/shard_map/ppermute | solution.py:57
  201.7 4.9 %collective-permute-done.16 = bf16[2,128,512]{2,1,0:T(8,128)(2,1)S(1)} collective-permute-done((bf16[2,128,512]{2,1,0:T(8,128)(2,1)S(1)}, bf16[2,128,512]{2,1,0:T(8,128)(2,1)S(1)}, u32[]{:S(2)}, u32[]{:S(2)}) %collective-permute-start.16) | collective-permute-done | bytes 262176 | tf_op jit(solution)/shard_map/ppermute | solution.py:57
  207.7 4.1 %collective-permute-done.15 = bf16[2,128,512]{2,1,0:T(8,128)(2,1)S(1)} collective-permute-done((bf16[2,128,512]{2,1,0:T(8,128)(2,1)S(1)}, bf16[2,128,512]{2,1,0:T(8,128)(2,1)S(1)}, u32[]{:S(2)}, u32[]{:S(2)}) %collective-permute-start.15) | collective-permute-done | bytes 262176 | tf_op jit(solution)/shard_map/ppermute | solution.py:57
  214.5 4.0 %collective-permute-done.36 = bf16[1,1,1,1,1,64,512]{6,5,4,3,2,1,0:T(8,128)(2,1)S(1)} collective-permute-done((bf16[1,1,1,1,1,64,512]{6,5,4,3,2,1,0:T(8,128)(2,1)S(1)}, bf16[1,1,1,1,1,64,512]{6,5,4,3,2,1,0:T(8,128)(2,1)S(1)}, u32[]{:S(2)}, u32[]{:S(2)}) %collective-permute-start.36) | collective-permute-done | bytes 65568 | tf_op jit(solution)/shard_map/ppermute | solution.py:57
  223.7 9.0 %collective-permute-done.28 = bf16[1,1,1,2,2,16,3200]{6,5,4,3,2,1,0:T(8,128)(2,1)S(1)} collective-permute-done((bf16[1,1,1,2,2,16,3200]{6,5,4,3,2,1,0:T(8,128)(2,1)S(1)}, bf16[1,1,1,2,2,16,3200]{6,5,4,3,2,1,0:T(8,128)(2,1)S(1)}, u32[]{:S(2)}, u32[]{:S(2)}) %collective-permute-start.28) | collective-permute-done | bytes 409632 | tf_op jit(solution)/shard_map/ppermute | solution.py:57
  232.7 4.8 %collective-permute-done.27 = bf16[1,1,1,2,2,16,3200]{6,5,4,3,2,1,0:T(8,128)(2,1)S(1)} collective-permute-done((bf16[1,1,1,2,2,16,3200]{6,5,4,3,2,1,0:T(8,128)(2,1)S(1)}, bf16[1,1,1,2,2,16,3200]{6,5,4,3,2,1,0:T(8,128)(2,1)S(1)}, u32[]{:S(2)}, u32[]{:S(2)}) %collective-permute-start.27) | collective-permute-done | bytes 409632 | tf_op jit(solution)/shard_map/ppermute | solution.py:57
  238.5 7.0 %collective-permute-done.29 = bf16[1,1,1,2,1,16,3200]{6,5,4,3,2,1,0:T(8,128)(2,1)S(1)} collective-permute-done((bf16[1,1,1,2,1,16,3200]{6,5,4,3,2,1,0:T(8,128)(2,1)S(1)}, bf16[1,1,1,2,1,16,3200]{6,5,4,3,2,1,0:T(8,128)(2,1)S(1)}, u32[]{:S(2)}, u32[]{:S(2)}) %collective-permute-start.29) | collective-permute-done | bytes 204832 | tf_op jit(solution)/shard_map/ppermute | solution.py:57
  247.0 5.7 %collective-permute-done.30 = bf16[1,1,1,1,1,16,3200]{6,5,4,3,2,1,0:T(8,128)(2,1)S(1)} collective-permute-done((bf16[1,1,1,1,1,16,3200]{6,5,4,3,2,1,0:T(8,128)(2,1)S(1)}, bf16[1,1,1,1,1,16,3200]{6,5,4,3,2,1,0:T(8,128)(2,1)S(1)}, u32[]{:S(2)}, u32[]{:S(2)}) %collective-permute-start.30) | collective-permute-done | bytes 102432 | tf_op jit(solution)/shard_map/ppermute | solution.py:57
  (175 shorter events, 50.8 us)
Async XLA Ops:
  2.4 7.8 %collective-permute-start.9 = (bf16[1,1,1,1,1,64,512]{6,5,4,3,2,1,0:T(8,128)(2,1)S(1)}, bf16[1,1,1,1,1,64,512]{6,5,4,3,2,1,0:T(8,128)(2,1)S(1)}, u32[]{:S(2)}, u32[]{:S(2)}) collective-permute-start(bf16[1,1,1,1,1,64,512]{6,5,4,3,2,1,0:T(8,128)(2,1)S(1)} %bitcast.101), channel_id=1, source_target_pairs={{0,2},{1,3},{2,0},{3,1},{4,6},{5,7},{6,4},{7,5},{8,10},{9,11},{10,... | collective-permute-start | bytes 196616 | tf_op jit(solution)/shard_map/ppermute | solution.py:57
  8.3 7.6 %collective-permute-start.3 = (bf16[1,1,1,1,1,16,3200]{6,5,4,3,2,1,0:T(8,128)(2,1)S(1)}, bf16[1,1,1,1,1,16,3200]{6,5,4,3,2,1,0:T(8,128)(2,1)S(1)}, u32[]{:S(2)}, u32[]{:S(2)}) collective-permute-start(bf16[1,1,1,1,1,16,3200]{6,5,4,3,2,1,0:T(8,128)(2,1)S(1)} %get-tuple-element.102), channel_id=1, source_target_pairs={{0,2},{1,3},{2,0},{3,1},{4,6},{5,7},{6,4},{7,5},{8,10},{9,11},{10,... | collective-permute-start | bytes 307208 | tf_op jit(solution)/shard_map/ppermute | solution.py:57
  10.2 8.5 %collective-permute-start.10 = (bf16[1,1,1,2,1,64,512]{6,5,3,4,2,1,0:T(8,128)(2,1)S(1)}, bf16[1,1,1,2,1,64,512]{6,5,3,4,2,1,0:T(8,128)(2,1)S(1)}, u32[]{:S(2)}, u32[]{:S(2)}) collective-permute-start(bf16[1,1,1,2,1,64,512]{6,5,3,4,2,1,0:T(8,128)(2,1)S(1)} %fusion.15), channel_id=1, source_target_pairs={{0,1},{1,0},{2,3},{3,2},{4,5},{5,4},{6,7},{7,6},{8,9},{9,8},{10,11... | collective-permute-start | bytes 393224 | tf_op jit(solution)/shard_map/ppermute | solution.py:57
  18.7 32.3 %collective-permute-start.13 = (bf16[1,1,1,2,2,64,512]{6,5,4,3,2,1,0:T(8,128)(2,1)S(1)}, bf16[1,1,1,2,2,64,512]{6,5,4,3,2,1,0:T(8,128)(2,1)S(1)}, u32[]{:S(2)}, u32[]{:S(2)}) collective-permute-start(bf16[1,1,1,2,2,64,512]{6,5,4,3,2,1,0:T(8,128)(2,1)S(1)} %copy_select_fusion.1), channel_id=1, source_target_pairs={{0,24},{4,28},{8,16},{12,20},{16,8},{20,12},{24,0},{28,4},{1,25},{... | collective-permute-start | bytes 786440 | tf_op jit(solution)/shard_map/ppermute | solution.py:57
  21.2 29.9 %collective-permute-start.12 = (bf16[1,1,1,2,2,64,512]{6,5,4,3,2,1,0:T(8,128)(2,1)S(1)}, bf16[1,1,1,2,2,64,512]{6,5,4,3,2,1,0:T(8,128)(2,1)S(1)}, u32[]{:S(2)}, u32[]{:S(2)}) collective-permute-start(bf16[1,1,1,2,2,64,512]{6,5,4,3,2,1,0:T(8,128)(2,1)S(1)} %copy_select_fusion.1), channel_id=1, source_target_pairs={{0,16},{4,20},{8,24},{12,28},{16,0},{20,4},{24,8},{28,12},{1,17},{... | collective-permute-start | bytes 786440 | tf_op jit(solution)/shard_map/ppermute | solution.py:57
  21.7 29.5 %collective-permute-start.11 = (bf16[1,1,1,2,2,64,512]{6,5,4,3,2,1,0:T(8,128)(2,1)S(1)}, bf16[1,1,1,2,2,64,512]{6,5,4,3,2,1,0:T(8,128)(2,1)S(1)}, u32[]{:S(2)}, u32[]{:S(2)}) collective-permute-start(bf16[1,1,1,2,2,64,512]{6,5,4,3,2,1,0:T(8,128)(2,1)S(1)} %copy_select_fusion.1), channel_id=1, source_target_pairs={{0,8},{4,12},{8,0},{12,4},{16,24},{20,28},{24,16},{28,20},{1,9},{5... | collective-permute-start | bytes 786440 | tf_op jit(solution)/shard_map/ppermute | solution.py:57
  22.5 20.1 %collective-permute-start.7 = (bf16[1,1,1,2,2,16,3200]{6,5,4,3,2,1,0:T(8,128)(2,1)S(1)}, bf16[1,1,1,2,2,16,3200]{6,5,4,3,2,1,0:T(8,128)(2,1)S(1)}, u32[]{:S(2)}, u32[]{:S(2)}) collective-permute-start(bf16[1,1,1,2,2,16,3200]{6,5,4,3,2,1,0:T(8,128)(2,1)S(1)} %copy_select_fusion), channel_id=1, source_target_pairs={{0,24},{4,28},{8,16},{12,20},{16,8},{20,12},{24,0},{28,4},{1,25},{... | collective-permute-start | bytes 1228808 | tf_op jit(solution)/shard_map/ppermute | solution.py:57
  24.9 23.5 %collective-permute-start.6 = (bf16[1,1,1,2,2,16,3200]{6,5,4,3,2,1,0:T(8,128)(2,1)S(1)}, bf16[1,1,1,2,2,16,3200]{6,5,4,3,2,1,0:T(8,128)(2,1)S(1)}, u32[]{:S(2)}, u32[]{:S(2)}) collective-permute-start(bf16[1,1,1,2,2,16,3200]{6,5,4,3,2,1,0:T(8,128)(2,1)S(1)} %copy_select_fusion), channel_id=1, source_target_pairs={{0,16},{4,20},{8,24},{12,28},{16,0},{20,4},{24,8},{28,12},{1,17},{... | collective-permute-start | bytes 1228808 | tf_op jit(solution)/shard_map/ppermute | solution.py:57
  42.6 8.0 %collective-permute-start.5 = (bf16[1,1,1,2,2,16,3200]{6,5,4,3,2,1,0:T(8,128)(2,1)S(1)}, bf16[1,1,1,2,2,16,3200]{6,5,4,3,2,1,0:T(8,128)(2,1)S(1)}, u32[]{:S(2)}, u32[]{:S(2)}) collective-permute-start(bf16[1,1,1,2,2,16,3200]{6,5,4,3,2,1,0:T(8,128)(2,1)S(1)} %copy_select_fusion), channel_id=1, source_target_pairs={{0,8},{4,12},{8,0},{12,4},{16,24},{20,28},{24,16},{28,20},{1,9},{5... | collective-permute-start | bytes 1228808 | tf_op jit(solution)/shard_map/ppermute | solution.py:57
  51.0 14.0 %collective-permute-start.8 = (bf16[2,2,1,2,2,16,3200]{6,5,4,3,2,1,0:T(8,128)(2,1)S(1)}, bf16[2,2,1,2,2,16,3200]{6,5,4,3,2,1,0:T(8,128)(2,1)}, u32[]{:S(2)}, u32[]{:S(2)}) collective-permute-start(bf16[2,2,1,2,2,16,3200]{6,5,4,3,2,1,0:T(8,128)(2,1)S(1)} %maximum_select_fusion.2), channel_id=1, source_target_pairs={{0,4},{4,0},{8,12},{12,8},{16,20},{20,16},{24,28},{28,24},{1,5},{5... | collective-permute-start | bytes 4915208 | tf_op jit(solution)/shard_map/ppermute | solution.py:57
  52.4 7.9 %collective-permute-start.14 = (bf16[2,2,1,2,2,64,512]{6,5,4,3,2,1,0:T(8,128)(2,1)}, bf16[2,2,1,2,2,64,512]{6,5,4,3,2,1,0:T(8,128)(2,1)}, u32[]{:S(2)}, u32[]{:S(2)}) collective-permute-start(bf16[2,2,1,2,2,64,512]{6,5,4,3,2,1,0:T(8,128)(2,1)} %maximum_select_fusion.3), channel_id=1, source_target_pairs={{0,4},{4,0},{8,12},{12,8},{16,20},{20,16},{24,28},{28,24},{1,5},{5... | collective-permute-start | bytes 3145736 | tf_op jit(solution)/shard_map/ppermute | solution.py:57
  55.0 17.0 %collective-permute-start = (bf16[2,128,512]{2,1,0:T(8,128)(2,1)}, bf16[2,128,512]{2,1,0:T(8,128)(2,1)}, u32[]{:S(2)}, u32[]{:S(2)}) collective-permute-start(bf16[2,128,512]{2,1,0:T(8,128)(2,1)} %get-tuple-element.91), channel_id=1, source_target_pairs={{0,1},{1,0},{2,3},{3,2},{4,5},{5,4},{6,7},{7,6},{8,9},{9,8},{10,11... | collective-permute-start | bytes 786440 | tf_op jit(solution)/shard_map/ppermute | solution.py:57
  55.0 21.7 %collective-permute-start.1 = (bf16[2,128,512]{2,1,0:T(8,128)(2,1)}, bf16[2,128,512]{2,1,0:T(8,128)(2,1)}, u32[]{:S(2)}, u32[]{:S(2)}) collective-permute-start(bf16[2,128,512]{2,1,0:T(8,128)(2,1)} %get-tuple-element.93), channel_id=1, source_target_pairs={{0,2},{1,3},{2,0},{3,1},{4,6},{5,7},{6,4},{7,5},{8,10},{9,11},{10,... | collective-permute-start | bytes 786440 | tf_op jit(solution)/shard_map/ppermute | solution.py:57
  56.9 19.8 %collective-permute-start.2 = (bf16[2,128,512]{2,1,0:T(8,128)(2,1)S(1)}, bf16[2,128,512]{2,1,0:T(8,128)(2,1)}, u32[]{:S(2)}, u32[]{:S(2)}) collective-permute-start(bf16[2,128,512]{2,1,0:T(8,128)(2,1)S(1)} %get-tuple-element.90), channel_id=1, source_target_pairs={{0,3},{1,2},{2,1},{3,0},{4,7},{5,6},{6,5},{7,4},{8,11},{9,10},{10,... | collective-permute-start | bytes 786440 | tf_op jit(solution)/shard_map/ppermute | solution.py:57
  60.4 50.1 %collective-permute-start.18 = (bf16[2,128,512]{2,1,0:T(8,128)(2,1)}, bf16[2,128,512]{2,1,0:T(8,128)(2,1)S(1)}, u32[]{:S(2)}, u32[]{:S(2)}) collective-permute-start(bf16[2,128,512]{2,1,0:T(8,128)(2,1)} %get-tuple-element.87), channel_id=1, source_target_pairs={{0,1},{1,0},{2,3},{3,2},{4,5},{5,4},{6,7},{7,6},{8,9},{9,8},{10,11... | collective-permute-start | bytes 786440 | tf_op jit(solution)/shard_map/ppermute | solution.py:57
  65.0 45.5 %collective-permute-start.19 = (bf16[2,128,512]{2,1,0:T(8,128)(2,1)}, bf16[2,128,512]{2,1,0:T(8,128)(2,1)S(1)}, u32[]{:S(2)}, u32[]{:S(2)}) collective-permute-start(bf16[2,128,512]{2,1,0:T(8,128)(2,1)} %get-tuple-element.89), channel_id=1, source_target_pairs={{0,2},{1,3},{2,0},{3,1},{4,6},{5,7},{6,4},{7,5},{8,10},{9,11},{10,... | collective-permute-start | bytes 786440 | tf_op jit(solution)/shard_map/ppermute | solution.py:57
  72.0 38.6 %collective-permute-start.20 = (bf16[2,128,512]{2,1,0:T(8,128)(2,1)}, bf16[2,128,512]{2,1,0:T(8,128)(2,1)S(1)}, u32[]{:S(2)}, u32[]{:S(2)}) collective-permute-start(bf16[2,128,512]{2,1,0:T(8,128)(2,1)} %get-tuple-element.86), channel_id=1, source_target_pairs={{0,3},{1,2},{2,1},{3,0},{4,7},{5,6},{6,5},{7,4},{8,11},{9,10},{10,... | collective-permute-start | bytes 786440 | tf_op jit(solution)/shard_map/ppermute | solution.py:57
  108.9 92.8 %collective-permute-start.17 = (bf16[2,128,512]{2,1,0:T(8,128)(2,1)}, bf16[2,128,512]{2,1,0:T(8,128)(2,1)}, u32[]{:S(2)}, u32[]{:S(2)}) collective-permute-start(bf16[2,128,512]{2,1,0:T(8,128)(2,1)} %get-tuple-element.47), channel_id=1, source_target_pairs={{0,3},{1,2},{2,1},{3,0},{4,7},{5,6},{6,5},{7,4},{8,11},{9,10},{10,... | collective-permute-start | bytes 786440 | tf_op jit(solution)/shard_map/ppermute | solution.py:57
  147.4 22.1 %collective-permute-start.23 = (bf16[2,128,512]{2,1,0:T(8,128)(2,1)}, bf16[2,128,512]{2,1,0:T(8,128)(2,1)S(1)}, u32[]{:S(2)}, u32[]{:S(2)}) collective-permute-start(bf16[2,128,512]{2,1,0:T(8,128)(2,1)} %get-tuple-element.63), channel_id=1, source_target_pairs={{0,3},{1,2},{2,1},{3,0},{4,7},{5,6},{6,5},{7,4},{8,11},{9,10},{10,... | collective-permute-start | bytes 786440 | tf_op jit(solution)/shard_map/ppermute | solution.py:57
  149.7 31.1 %collective-permute-start.22 = (bf16[2,128,512]{2,1,0:T(8,128)(2,1)}, bf16[2,128,512]{2,1,0:T(8,128)(2,1)}, u32[]{:S(2)}, u32[]{:S(2)}) collective-permute-start(bf16[2,128,512]{2,1,0:T(8,128)(2,1)} %get-tuple-element.62), channel_id=1, source_target_pairs={{0,2},{1,3},{2,0},{3,1},{4,6},{5,7},{6,4},{7,5},{8,10},{9,11},{10,... | collective-permute-start | bytes 786440 | tf_op jit(solution)/shard_map/ppermute | solution.py:57
  166.5 17.1 %collective-permute-start.31 = (bf16[2,2,1,2,2,64,512]{6,5,4,3,2,1,0:T(8,128)(2,1)}, bf16[2,2,1,2,2,64,512]{6,5,4,3,2,1,0:T(8,128)(2,1)}, u32[]{:S(2)}, u32[]{:S(2)}) collective-permute-start(bf16[2,2,1,2,2,64,512]{6,5,4,3,2,1,0:T(8,128)(2,1)} %fusion), channel_id=1, source_target_pairs={{0,4},{4,0},{8,12},{12,8},{16,20},{20,16},{24,28},{28,24},{1,5},{5... | collective-permute-start | bytes 3145736 | tf_op jit(solution)/shard_map/ppermute | solution.py:57
  169.5 14.0 %collective-permute-start.21 = (bf16[2,128,512]{2,1,0:T(8,128)(2,1)S(1)}, bf16[2,128,512]{2,1,0:T(8,128)(2,1)S(1)}, u32[]{:S(2)}, u32[]{:S(2)}) collective-permute-start(bf16[2,128,512]{2,1,0:T(8,128)(2,1)S(1)} %copy-done.25), channel_id=1, source_target_pairs={{0,1},{1,0},{2,3},{3,2},{4,5},{5,4},{6,7},{7,6},{8,9},{9,8},{10,11... | collective-permute-start | bytes 786440 | tf_op jit(solution)/shard_map/ppermute | solution.py:57
  169.5 49.1 %collective-permute-start.24 = (bf16[2,2,1,2,2,16,3072]{6,5,4,3,2,1,0:T(8,128)(2,1)S(1)}, bf16[2,2,1,2,2,16,3072]{6,5,4,3,2,1,0:T(8,128)(2,1)S(1)}, u32[]{:S(2)}, u32[]{:S(2)}) collective-permute-start(bf16[2,2,1,2,2,16,3072]{6,5,4,3,2,1,0:T(8,128)(2,1)S(1)} %constant_dynamic-slice_fusion.8), channel_id=1, source_target_pairs={{0,4},{4,0},{8,12},{12,8},{16,20},{20,16},{24,28},{28,24},{1,5},{5... | collective-permute-start | bytes 4718600 | tf_op jit(solution)/shard_map/ppermute | solution.py:57
  185.2 10.2 %collective-permute-start.34 = (bf16[1,1,1,2,2,64,512]{6,5,4,3,2,1,0:T(8,128)(2,1)S(1)}, bf16[1,1,1,2,2,64,512]{6,5,4,3,2,1,0:T(8,128)(2,1)S(1)}, u32[]{:S(2)}, u32[]{:S(2)}) collective-permute-start(bf16[1,1,1,2,2,64,512]{6,5,4,3,2,1,0:T(8,128)(2,1)S(1)} %get-tuple-element.84), channel_id=1, source_target_pairs={{0,24},{4,28},{8,16},{12,20},{16,8},{20,12},{24,0},{28,4},{1,25},{... | collective-permute-start | bytes 786440 | tf_op jit(solution)/shard_map/ppermute | solution.py:57
  187.7 11.7 %collective-permute-start.33 = (bf16[1,1,1,2,2,64,512]{6,5,4,3,2,1,0:T(8,128)(2,1)S(1)}, bf16[1,1,1,2,2,64,512]{6,5,4,3,2,1,0:T(8,128)(2,1)S(1)}, u32[]{:S(2)}, u32[]{:S(2)}) collective-permute-start(bf16[1,1,1,2,2,64,512]{6,5,4,3,2,1,0:T(8,128)(2,1)S(1)} %get-tuple-element.85), channel_id=1, source_target_pairs={{0,8},{4,12},{8,0},{12,4},{16,24},{20,28},{24,16},{28,20},{1,9},{5... | collective-permute-start | bytes 786440 | tf_op jit(solution)/shard_map/ppermute | solution.py:57
  188.3 11.2 %collective-permute-start.32 = (bf16[1,1,1,2,2,64,512]{6,5,4,3,2,1,0:T(8,128)(2,1)S(1)}, bf16[1,1,1,2,2,64,512]{6,5,4,3,2,1,0:T(8,128)(2,1)S(1)}, u32[]{:S(2)}, u32[]{:S(2)}) collective-permute-start(bf16[1,1,1,2,2,64,512]{6,5,4,3,2,1,0:T(8,128)(2,1)S(1)} %get-tuple-element.83), channel_id=1, source_target_pairs={{0,16},{4,20},{8,24},{12,28},{16,0},{20,4},{24,8},{28,12},{1,17},{... | collective-permute-start | bytes 786440 | tf_op jit(solution)/shard_map/ppermute | solution.py:57
  195.4 11.2 %collective-permute-start.16 = (bf16[2,128,512]{2,1,0:T(8,128)(2,1)S(1)}, bf16[2,128,512]{2,1,0:T(8,128)(2,1)S(1)}, u32[]{:S(2)}, u32[]{:S(2)}) collective-permute-start(bf16[2,128,512]{2,1,0:T(8,128)(2,1)S(1)} %copy-done.24), channel_id=1, source_target_pairs={{0,2},{1,3},{2,0},{3,1},{4,6},{5,7},{6,4},{7,5},{8,10},{9,11},{10,... | collective-permute-start | bytes 786440 | tf_op jit(solution)/shard_map/ppermute | solution.py:57
  199.4 12.4 %collective-permute-start.15 = (bf16[2,128,512]{2,1,0:T(8,128)(2,1)S(1)}, bf16[2,128,512]{2,1,0:T(8,128)(2,1)S(1)}, u32[]{:S(2)}, u32[]{:S(2)}) collective-permute-start(bf16[2,128,512]{2,1,0:T(8,128)(2,1)S(1)} %copy-done.23), channel_id=1, source_target_pairs={{0,1},{1,0},{2,3},{3,2},{4,5},{5,4},{6,7},{7,6},{8,9},{9,8},{10,11... | collective-permute-start | bytes 786440 | tf_op jit(solution)/shard_map/ppermute | solution.py:57
  199.6 13.6 %collective-permute-start.35 = (bf16[1,1,1,2,1,64,512]{6,5,4,3,2,1,0:T(8,128)(2,1)S(1)}, bf16[1,1,1,2,1,64,512]{6,5,4,3,2,1,0:T(8,128)(2,1)S(1)}, u32[]{:S(2)}, u32[]{:S(2)}) collective-permute-start(bf16[1,1,1,2,1,64,512]{6,5,4,3,2,1,0:T(8,128)(2,1)S(1)} %constant_dynamic-slice_fusion.1), channel_id=1, source_target_pairs={{0,1},{1,0},{2,3},{3,2},{4,5},{5,4},{6,7},{7,6},{8,9},{9,8},{10,11... | collective-permute-start | bytes 393224 | tf_op jit(solution)/shard_map/ppermute | solution.py:57
  219.4 13.3 %collective-permute-start.28 = (bf16[1,1,1,2,2,16,3200]{6,5,4,3,2,1,0:T(8,128)(2,1)S(1)}, bf16[1,1,1,2,2,16,3200]{6,5,4,3,2,1,0:T(8,128)(2,1)S(1)}, u32[]{:S(2)}, u32[]{:S(2)}) collective-permute-start(bf16[1,1,1,2,2,16,3200]{6,5,4,3,2,1,0:T(8,128)(2,1)S(1)} %get-tuple-element.82), channel_id=1, source_target_pairs={{0,24},{4,28},{8,16},{12,20},{16,8},{20,12},{24,0},{28,4},{1,25},{... | collective-permute-start | bytes 1228808 | tf_op jit(solution)/shard_map/ppermute | solution.py:57
  220.8 16.8 %collective-permute-start.27 = (bf16[1,1,1,2,2,16,3200]{6,5,4,3,2,1,0:T(8,128)(2,1)S(1)}, bf16[1,1,1,2,2,16,3200]{6,5,4,3,2,1,0:T(8,128)(2,1)S(1)}, u32[]{:S(2)}, u32[]{:S(2)}) collective-permute-start(bf16[1,1,1,2,2,16,3200]{6,5,4,3,2,1,0:T(8,128)(2,1)S(1)} %get-tuple-element.81), channel_id=1, source_target_pairs={{0,8},{4,12},{8,0},{12,4},{16,24},{20,28},{24,16},{28,20},{1,9},{5... | collective-permute-start | bytes 1228808 | tf_op jit(solution)/shard_map/ppermute | solution.py:57
  221.7 16.4 %collective-permute-start.26 = (bf16[1,1,1,2,2,16,3200]{6,5,4,3,2,1,0:T(8,128)(2,1)S(1)}, bf16[1,1,1,2,2,16,3200]{6,5,4,3,2,1,0:T(8,128)(2,1)S(1)}, u32[]{:S(2)}, u32[]{:S(2)}) collective-permute-start(bf16[1,1,1,2,2,16,3200]{6,5,4,3,2,1,0:T(8,128)(2,1)S(1)} %get-tuple-element.80), channel_id=1, source_target_pairs={{0,16},{4,20},{8,24},{12,28},{16,0},{20,4},{24,8},{28,12},{1,17},{... | collective-permute-start | bytes 1228808 | tf_op jit(solution)/shard_map/ppermute | solution.py:57
  (32 other events, 367.1 us)
